TPU v7x, 512 devices: a whole 4x8x8 slice. The times are simulated.
512 devices in a mesh: lat: 16 (over z_hi, x), lev: 32 (over y, z_lo, core).
Axes of the slice: x: 4, y: 8, z: 8 (z_hi: 4, z_lo: 2; z = z_hi * 2 + z_lo), core: 2. Of those that a mesh axis runs over, the one named last changes fastest.
Arguments:
- state: float32 [6, 48, 128, 1152], P(None, 'lat', 'lev'), may hold values from -6 to 6
- courant: float32 [2, 48, 128, 1152], P(None, 'lat', 'lev'), may hold values from -0.4 to 0.4
- offsets: int32 [2, 48, 128, 1152], P(None, 'lat', 'lev'), may hold values from -1 to 2
- log_thickness: float32 [48, 128, 1152], P('lat', 'lev'), may hold values from 0.05 to 0.5
- surface: float32 [48, 1152], P('lat'), may hold values from -6 to 6
- remap_level: int32 [48, 128, 1152], P('lat', None, 'lev'), may hold values from 0 to 127, as said below
- remap_weight: float32 [48, 128, 1152], P('lat', None, 'lev'), may hold values from 0 to 1
Outputs:
- remapped: float32 [6, 48, 128, 1152], P(None, 'lat', 'lev')
- geopotential: float32 [48, 128, 1152], P('lat', 'lev')
Inputs may be any that keep to these rules, and one draw needn't show every extreme that they name: `remap_level`: the source level of target level k lies within 2 of k.
All inputs are finite; a program needn't handle non-finite values.
Results may differ from a plain program's by a relative error of at most 0.00007.
Values sent between devices are 32-bit elements; how exact they have to be, the bound alone decides.
No kernel may reach another device: no remote copies, remote signals or barrier semaphores. Data moves between devices by JAX's collectives and lax.ppermute only.
A program may use at most 64 MiB of HBM per device.

v0:
```python
import jax
import jax.numpy as jnp
from jax import lax
from jax.sharding import PartitionSpec as P

SUBSTEPS = 2


def extended_2(block, sides, width):
    for axis, dim in sides:
        count = lax.axis_size(axis)
        forward = [(i, i + 1) for i in range(count - 1)]
        backward = [(target, source) for source, target in forward]
        low = lax.ppermute(
            lax.slice_in_dim(block, block.shape[dim] - width, None, axis=dim), axis, forward
        )
        high = lax.ppermute(lax.slice_in_dim(block, 0, width, axis=dim), axis, backward)
        block = jnp.concatenate([low, block, high], axis=dim)
    return block


def from_behind(x, axis, by):
    count = lax.axis_size(axis)
    pairs = [(i, i + by) for i in range(count) if 0 <= i + by < count]
    return lax.ppermute(x, axis, pairs)


def from_everyone(x, axis):
    count = lax.axis_size(axis)
    return lax.all_to_all(jnp.broadcast_to(x[None], (count, *x.shape)), axis, 0, 0, tiled=True)


def joined_by_halves(pieces, combine):
    while len(jax.tree.leaves(pieces)[0]) > 1:
        pieces = jax.vmap(combine)(*(pieces[side::2] for side in (0, 1)))
    return pieces[0]


def entering(x, axis, combine, identity):
    count, position = (lax.axis_size(axis), lax.axis_index(axis))
    passed = jnp.arange(count) > position

    def kept(part, zero, own):
        part = jnp.where(
            passed.reshape(-1, *(1 for _ in own.shape)), part, jnp.asarray(zero, own.dtype)
        )
        return part[::-1]

    pieces = from_everyone(x, axis)
    return joined_by_halves(kept(pieces, identity, x), combine)


def local_parabola(extended, delta, weight):
    margin = 4
    count = extended.shape[-2] - 2 * margin
    edges = (
        7.0 * (extended[..., 1:-2, :] + extended[..., 2:-1, :])
        - (extended[..., :-3, :] + extended[..., 3:, :])
    ) / 12.0
    centre = jnp.zeros(extended.shape[:-2] + (count, extended.shape[-1]), jnp.float32)
    left = centre
    right = centre
    for offset in range(-2, 3):
        chosen = delta == offset
        start = margin + offset
        centre = jnp.where(chosen, extended[..., start : start + count, :], centre)
        left = jnp.where(chosen, edges[..., start - 2 : start - 2 + count, :], left)
        right = jnp.where(chosen, edges[..., start - 1 : start - 1 + count, :], right)
    slope = right - left
    curve = 6.0 * centre - 3.0 * (left + right)
    return left + weight * (slope + curve * (1.0 - weight))


def add_terms(earlier, later):
    return earlier + later


def per_device(state, courant, offsets, log_thickness, surface, remap_level, remap_weight):
    count, rows, levels, width = state.shape
    north_masks = [offsets[0] == offset for offset in range(-1, 3)]
    east_masks = [offsets[1] == offset for offset in range(-1, 3)]
    field = state
    for substep in range(SUBSTEPS):
        padded = extended_2(field, (("lat", 1),), 2)
        picked = jnp.zeros_like(field)
        for number, offset in enumerate(range(-1, 3)):
            picked = jnp.where(
                north_masks[number][None], padded[:, offset + 2 : offset + 2 + rows], picked
            )
        north = courant[0][None] * picked
        below = from_behind(north[:, rows - 1 :], "lat", 1)
        south = jnp.concatenate([below, north[:, : rows - 1]], axis=1)
        moved = jnp.zeros_like(field)
        for number, offset in enumerate(range(-1, 3)):
            moved = jnp.where(east_masks[number][None], jnp.roll(field, -offset, axis=3), moved)
        east = courant[1][None] * moved
        west = jnp.roll(east, 1, axis=3)
        field = field - (north - south) - (east - west)
    heating = field[0] * log_thickness
    lower_local = jnp.cumsum(heating[:, ::-1], axis=1)[:, ::-1] - heating
    column_sum = jnp.sum(heating, axis=1)
    deeper = entering(column_sum, "lev", add_terms, jnp.zeros_like(column_sum))
    geopotential = surface[:, None, :] + deeper[:, None, :] + lower_local + 0.5 * heating
    total_levels = remap_level.shape[1]
    delta_col = (remap_level - jnp.arange(total_levels, dtype=jnp.int32)[None, :, None]).astype(
        jnp.float32
    )
    inputs = lax.all_to_all(
        jnp.stack([delta_col, remap_weight]), "lev", split_axis=2, concat_axis=3, tiled=True
    )
    margin = 4
    before = []
    before.insert(0, from_behind(field, "lev", 1))
    after_list = [from_behind(field, "lev", -1)]
    joined = jnp.concatenate(before + [field] + after_list, axis=2)
    first = lax.axis_index("lev") * levels
    whole = levels * lax.axis_size("lev")
    position = first - margin + jnp.arange(levels + 2 * margin, dtype=jnp.int32)
    where_from = jnp.clip(position, 0, whole - 1) - (first - margin)
    extended = jnp.take(joined, where_from, axis=2)
    remapped = local_parabola(extended, inputs[0][None], inputs[1][None])
    return (remapped, geopotential)


def solution(mesh):
    in_specs = (
        P(None, "lat", "lev", None),
        P(None, "lat", "lev", None),
        P(None, "lat", "lev", None),
        P("lat", "lev", None),
        P("lat", None),
        P("lat", None, "lev"),
        P("lat", None, "lev"),
    )
    out_specs = (P(None, "lat", "lev", None), P("lat", "lev", None))
    return jax.shard_map(
        per_device, mesh=mesh, in_specs=in_specs, out_specs=out_specs, check_vma=False
    )
```

profile of v0, /device:TPU:320, one launch (start us, length us, event | category | flops | bytes accessed | tf_op | source)
XLA Modules:
  0.0 116.3 jit_solution(181216330594921575)
XLA Ops:
  0.6 1.1 copy.181
  1.7 0.8 fusion.46
  2.6 3.7 %collective-permute-start = (f32[6,2,4,1152]{3,0,1,2:T(8,128)}, f32[6,2,4,1152]{3,0,1,2:T(8,128)S(1)}, u32[]{:S(2)}, u32[]{:S(2)}) collective-permute-start(f32[6,2,4,1152]{3,0,1,2:T(8,128)} %get-tuple-element.26), channel_id=1, source_target_pairs={{32,0},{64,32},{96,64},{128,96},{160,128},{192,160},{224,192},{256... | collective-permute-start | bytes 663560 | tf_op jit(solution)/shard_map/ppermute | solution.py:17
  6.3 2.1 %collective-permute-start.1 = (f32[6,2,4,1152]{3,0,1,2:T(8,128)}, f32[6,2,4,1152]{3,0,1,2:T(8,128)S(1)}, u32[]{:S(2)}, u32[]{:S(2)}) collective-permute-start(f32[6,2,4,1152]{3,0,1,2:T(8,128)} %get-tuple-element.27), channel_id=1, source_target_pairs={{0,32},{32,64},{64,96},{96,128},{128,160},{160,192},{192,224},{224... | collective-permute-start | bytes 663560 | tf_op jit(solution)/shard_map/ppermute | solution.py:14
  8.7 0.3 copy.167
  8.9 1.2 %reshape.103 = f32[32,1,864]{2,1,0:T(1,128)} reshape(f32[128,3,2,36]{3,2,1,0:T(2,128)S(1)} %bitcast.60) | data formatting | bytes 221184
  10.2 8.7 %all-to-all-start = ((f32[32,1,864]{2,1,0:T(1,128)}), f32[32,1,864]{2,1,0:T(1,128)S(1)}, u32[]{:S(2)}, u32[]{:S(2)}) async-start(f32[32,1,864]{2,1,0:T(1,128)} %reshape.103), calls=%async_computation | async-start | bytes 229376 | tf_op jit(solution)/shard_map/all_to_all | solution.py:108
  19.4 0.4 copy-done.11
  20.1 0.6 copy.172
  20.8 0.6 copy.175
  21.4 0.6 copy.176
  22.0 0.6 copy.177
  22.7 0.4 fusion.30
  23.2 0.6 compare_and_fusion
  23.8 4.0 %all-to-all-done = f32[32,1,864]{2,1,0:T(1,128)S(1)} async-done(((f32[32,1,864]{2,1,0:T(1,128)}), f32[32,1,864]{2,1,0:T(1,128)S(1)}, u32[]{:S(2)}, u32[]{:S(2)}) %all-to-all-start) | async-done | bytes 110624 | tf_op jit(solution)/shard_map/all_to_all | solution.py:108
  27.8 0.5 broadcast.175
  28.3 0.9 reduce
  29.2 0.6 reshape.104
  30.2 1.0 fusion.27
  31.2 3.4 %collective-permute-start.2 = (f32[6,1,4,1152]{3,0,1,2:T(8,128)S(1)}, f32[6,1,4,1152]{3,0,1,2:T(8,128)S(1)}, u32[]{:S(2)}, u32[]{:S(2)}) collective-permute-start(f32[6,1,4,1152]{3,0,1,2:T(8,128)S(1)} %slice.291), channel_id=1, source_target_pairs={{0,32},{32,64},{64,96},{96,128},{128,160},{160,192},{192,224},{224... | collective-permute-start | bytes 331784 | tf_op jit(solution)/shard_map/ppermute | solution.py:25
  34.7 8.7 %collective-permute-done.2 = f32[6,1,4,1152]{3,0,1,2:T(8,128)S(1)} collective-permute-done((f32[6,1,4,1152]{3,0,1,2:T(8,128)S(1)}, f32[6,1,4,1152]{3,0,1,2:T(8,128)S(1)}, u32[]{:S(2)}, u32[]{:S(2)}) %collective-permute-start.2) | collective-permute-done | bytes 110624 | tf_op jit(solution)/shard_map/ppermute | solution.py:25
  43.4 0.2 fusion.29
  44.1 3.0 %collective-permute-start.3 = (f32[6,2,4,1152]{3,0,1,2:T(8,128)S(1)}, f32[6,2,4,1152]{3,0,1,2:T(8,128)S(1)}, u32[]{:S(2)}, u32[]{:S(2)}) collective-permute-start(f32[6,2,4,1152]{3,0,1,2:T(8,128)S(1)} %get-tuple-element.21), channel_id=1, source_target_pairs={{32,0},{64,32},{96,64},{128,96},{160,128},{192,160},{224,192},{256... | collective-permute-start | bytes 663560 | tf_op jit(solution)/shard_map/ppermute | solution.py:17
  47.1 3.0 %collective-permute-start.4 = (f32[6,2,4,1152]{3,0,1,2:T(8,128)S(1)}, f32[6,2,4,1152]{3,0,1,2:T(8,128)S(1)}, u32[]{:S(2)}, u32[]{:S(2)}) collective-permute-start(f32[6,2,4,1152]{3,0,1,2:T(8,128)S(1)} %get-tuple-element.20), channel_id=1, source_target_pairs={{0,32},{32,64},{64,96},{96,128},{128,160},{160,192},{192,224},{224... | collective-permute-start | bytes 663560 | tf_op jit(solution)/shard_map/ppermute | solution.py:14
  50.2 3.8 %collective-permute-done.3 = f32[6,2,4,1152]{3,0,1,2:T(8,128)S(1)} collective-permute-done((f32[6,2,4,1152]{3,0,1,2:T(8,128)S(1)}, f32[6,2,4,1152]{3,0,1,2:T(8,128)S(1)}, u32[]{:S(2)}, u32[]{:S(2)}) %collective-permute-start.3) | collective-permute-done | bytes 221216 | tf_op jit(solution)/shard_map/ppermute | solution.py:17
  54.0 7.7 %collective-permute-done.4 = f32[6,2,4,1152]{3,0,1,2:T(8,128)S(1)} collective-permute-done((f32[6,2,4,1152]{3,0,1,2:T(8,128)S(1)}, f32[6,2,4,1152]{3,0,1,2:T(8,128)S(1)}, u32[]{:S(2)}, u32[]{:S(2)}) %collective-permute-start.4) | collective-permute-done | bytes 221216 | tf_op jit(solution)/shard_map/ppermute | solution.py:14
  61.7 0.3 fusion.5
  62.0 1.9 %collective-permute-start.5 = (f32[6,1,4,1152]{3,0,1,2:T(8,128)S(1)}, f32[6,1,4,1152]{3,0,1,2:T(8,128)S(1)}, u32[]{:S(2)}, u32[]{:S(2)}) collective-permute-start(f32[6,1,4,1152]{3,0,1,2:T(8,128)S(1)} %slice.305), channel_id=1, source_target_pairs={{0,32},{32,64},{64,96},{96,128},{128,160},{160,192},{192,224},{224... | collective-permute-start | bytes 331784 | tf_op jit(solution)/shard_map/ppermute | solution.py:25
  64.0 0.4 fusion.34
  64.5 8.8 %collective-permute-done.5 = f32[6,1,4,1152]{3,0,1,2:T(8,128)S(1)} collective-permute-done((f32[6,1,4,1152]{3,0,1,2:T(8,128)S(1)}, f32[6,1,4,1152]{3,0,1,2:T(8,128)S(1)}, u32[]{:S(2)}, u32[]{:S(2)}) %collective-permute-start.5) | collective-permute-done | bytes 110624 | tf_op jit(solution)/shard_map/ppermute | solution.py:25
  73.3 0.2 fusion.33
  73.5 1.9 %collective-permute-start.6 = (f32[6,3,4,1152]{3,0,1,2:T(8,128)S(1)}, f32[6,3,4,1152]{3,0,1,2:T(8,128)S(1)}, u32[]{:S(2)}, u32[]{:S(2)}) collective-permute-start(f32[6,3,4,1152]{3,0,1,2:T(8,128)S(1)} %fusion.33), channel_id=1, source_target_pairs={{0,1},{1,2},{2,3},{3,4},{4,5},{5,6},{6,7},{7,8},{8,9},{9,10},{10,1... | collective-permute-start | bytes 995336 | tf_op jit(solution)/shard_map/ppermute | solution.py:25
  75.4 6.6 %collective-permute-start.7 = (f32[6,3,4,1152]{3,0,1,2:T(8,128)S(1)}, f32[6,3,4,1152]{3,0,1,2:T(8,128)S(1)}, u32[]{:S(2)}, u32[]{:S(2)}) collective-permute-start(f32[6,3,4,1152]{3,0,1,2:T(8,128)S(1)} %fusion.33), channel_id=1, source_target_pairs={{1,0},{2,1},{3,2},{4,3},{5,4},{6,5},{7,6},{8,7},{9,8},{10,9},{11,1... | collective-permute-start | bytes 995336 | tf_op jit(solution)/shard_map/ppermute | solution.py:25
  82.7 0.6 copy.196
  83.5 0.6 copy.197
  84.3 0.6 copy.198
  85.1 0.9 broadcast_in_dim.209
  86.0 9.6 %all-to-all-start.1 = ((f32[32,3,1152]{2,1,0:T(4,128)}), f32[32,3,1152]{2,1,0:T(4,128)S(1)}, u32[]{:S(2)}, u32[]{:S(2)}) async-start(f32[32,3,1152]{2,1,0:T(4,128)} %broadcast_in_dim.209), calls=%async_computation.1 | async-start | bytes 1179648 | tf_op jit(solution)/shard_map/all_to_all | solution.py:30
  95.6 0.3 rev.7
  96.1 0.3 rev.8
  96.6 0.6 gather_fusion
  97.3 0.8 select_bitcast_fusion
  98.3 0.5 copy-done.13
  98.8 0.6 fusion.15
  99.4 0.8 copy.202
  100.2 14.5 %all-to-all-done.1 = f32[32,3,1152]{2,1,0:T(4,128)S(1)} async-done(((f32[32,3,1152]{2,1,0:T(4,128)}), f32[32,3,1152]{2,1,0:T(4,128)S(1)}, u32[]{:S(2)}, u32[]{:S(2)}) %all-to-all-start.1) | async-done | bytes 442400 | tf_op jit(solution)/shard_map/all_to_all | solution.py:30
  115.2 0.4 copy-done.19
  115.6 0.6 multiply_add_fusion
  (99 shorter events, 4.2 us)
Async XLA Ops:
  0.6 7.8 %copy-start.17 = (s32[3,128,36]{1,2,0:T(8,128)S(1)}, s32[3,128,36]{1,2,0:T(8,128)}, u32[]{:S(2)}) copy-start(s32[3,128,36]{1,2,0:T(8,128)} %param.12) | copy-start | bytes 165892
  0.6 7.8 %copy-start.16 = (f32[3,128,36]{1,2,0:T(8,128)S(1)}, f32[3,128,36]{1,2,0:T(8,128)}, u32[]{:S(2)}) copy-start(f32[3,128,36]{1,2,0:T(8,128)} %param.13) | copy-start | bytes 165892
  2.6 27.5 %collective-permute-start = (f32[6,2,4,1152]{3,0,1,2:T(8,128)}, f32[6,2,4,1152]{3,0,1,2:T(8,128)S(1)}, u32[]{:S(2)}, u32[]{:S(2)}) collective-permute-start(f32[6,2,4,1152]{3,0,1,2:T(8,128)} %get-tuple-element.26), channel_id=1, source_target_pairs={{32,0},{64,32},{96,64},{128,96},{160,128},{192,160},{224,192},{256... | collective-permute-start | bytes 663560 | tf_op jit(solution)/shard_map/ppermute | solution.py:17
  6.3 23.8 %collective-permute-start.1 = (f32[6,2,4,1152]{3,0,1,2:T(8,128)}, f32[6,2,4,1152]{3,0,1,2:T(8,128)S(1)}, u32[]{:S(2)}, u32[]{:S(2)}) collective-permute-start(f32[6,2,4,1152]{3,0,1,2:T(8,128)} %get-tuple-element.27), channel_id=1, source_target_pairs={{0,32},{32,64},{64,96},{96,128},{128,160},{160,192},{192,224},{224... | collective-permute-start | bytes 663560 | tf_op jit(solution)/shard_map/ppermute | solution.py:14
  10.2 17.6 %all-to-all-start = ((f32[32,1,864]{2,1,0:T(1,128)}), f32[32,1,864]{2,1,0:T(1,128)S(1)}, u32[]{:S(2)}, u32[]{:S(2)}) async-start(f32[32,1,864]{2,1,0:T(1,128)} %reshape.103), calls=%async_computation | async-start | bytes 229376 | tf_op jit(solution)/shard_map/all_to_all | solution.py:108
  18.9 0.9 copy-start.11
  18.9 1.2 %copy-start.12 = (f32[2,3,4,1152]{3,2,1,0:T(4,128)S(1)}, f32[2,3,4,1152]{3,2,1,0:T(4,128)}, u32[]{:S(2)}) copy-start(f32[2,3,4,1152]{3,2,1,0:T(4,128)} %param.8) | copy-start | bytes 331780
  19.1 3.5 %copy-start = (f32[6,3,4,1152]{3,2,1,0:T(4,128)S(1)}, f32[6,3,4,1152]{3,2,1,0:T(4,128)}, u32[]{:S(2)}) copy-start(f32[6,3,4,1152]{3,2,1,0:T(4,128)} %param.7) | copy-start | bytes 995332
  20.0 3.1 %copy-start.1 = (pred[3,4,1152]{2,0,1:T(4,128)(4,1)}, pred[3,4,1152]{2,0,1:T(4,128)(4,1)S(1)}, u32[]{:S(2)}) copy-start(pred[3,4,1152]{2,0,1:T(4,128)(4,1)S(1)} %copy.186) | copy-start | bytes 41476
  20.0 3.0 %copy-start.3 = (pred[3,4,1152]{2,0,1:T(4,128)(4,1)}, pred[3,4,1152]{2,0,1:T(4,128)(4,1)S(1)}, u32[]{:S(2)}) copy-start(pred[3,4,1152]{2,0,1:T(4,128)(4,1)S(1)} %copy.189) | copy-start | bytes 41476
  20.1 3.0 %copy-start.5 = (pred[3,4,1152]{2,0,1:T(4,128)(4,1)}, pred[3,4,1152]{2,0,1:T(4,128)(4,1)S(1)}, u32[]{:S(2)}) copy-start(pred[3,4,1152]{2,0,1:T(4,128)(4,1)S(1)} %copy.190) | copy-start | bytes 41476
  31.2 12.2 %collective-permute-start.2 = (f32[6,1,4,1152]{3,0,1,2:T(8,128)S(1)}, f32[6,1,4,1152]{3,0,1,2:T(8,128)S(1)}, u32[]{:S(2)}, u32[]{:S(2)}) collective-permute-start(f32[6,1,4,1152]{3,0,1,2:T(8,128)S(1)} %slice.291), channel_id=1, source_target_pairs={{0,32},{32,64},{64,96},{96,128},{128,160},{160,192},{192,224},{224... | collective-permute-start | bytes 331784 | tf_op jit(solution)/shard_map/ppermute | solution.py:25
  43.8 17.9 %copy-start.7 = (pred[3,4,1152]{2,0,1:T(4,128)(4,1)S(1)}, pred[3,4,1152]{2,0,1:T(4,128)(4,1)}, u32[]{:S(2)}) copy-start(pred[3,4,1152]{2,0,1:T(4,128)(4,1)} %copy.172) | copy-start | bytes 41476
  43.8 17.9 %copy-start.8 = (pred[3,4,1152]{2,0,1:T(4,128)(4,1)S(1)}, pred[3,4,1152]{2,0,1:T(4,128)(4,1)}, u32[]{:S(2)}) copy-start(pred[3,4,1152]{2,0,1:T(4,128)(4,1)} %copy.175) | copy-start | bytes 41476
  43.8 17.9 %copy-start.9 = (pred[3,4,1152]{2,0,1:T(4,128)(4,1)S(1)}, pred[3,4,1152]{2,0,1:T(4,128)(4,1)}, u32[]{:S(2)}) copy-start(pred[3,4,1152]{2,0,1:T(4,128)(4,1)} %copy.176) | copy-start | bytes 41476
  43.8 17.9 %copy-start.10 = (pred[3,4,1152]{2,0,1:T(4,128)(4,1)S(1)}, pred[3,4,1152]{2,0,1:T(4,128)(4,1)}, u32[]{:S(2)}) copy-start(pred[3,4,1152]{2,0,1:T(4,128)(4,1)} %copy.177) | copy-start | bytes 41476
  44.1 19.8 %copy-start.2 = (pred[3,4,1152]{2,0,1:T(4,128)(4,1)S(1)}, pred[3,4,1152]{2,0,1:T(4,128)(4,1)}, u32[]{:S(2)}) copy-start(pred[3,4,1152]{2,0,1:T(4,128)(4,1)} %copy-done.1) | copy-start | bytes 41476
  44.1 19.8 %copy-start.4 = (pred[3,4,1152]{2,0,1:T(4,128)(4,1)S(1)}, pred[3,4,1152]{2,0,1:T(4,128)(4,1)}, u32[]{:S(2)}) copy-start(pred[3,4,1152]{2,0,1:T(4,128)(4,1)} %copy-done.3) | copy-start | bytes 41476
  44.1 19.8 %copy-start.6 = (pred[3,4,1152]{2,0,1:T(4,128)(4,1)S(1)}, pred[3,4,1152]{2,0,1:T(4,128)(4,1)}, u32[]{:S(2)}) copy-start(pred[3,4,1152]{2,0,1:T(4,128)(4,1)} %copy-done.5) | copy-start | bytes 41476
  44.1 9.8 %collective-permute-start.3 = (f32[6,2,4,1152]{3,0,1,2:T(8,128)S(1)}, f32[6,2,4,1152]{3,0,1,2:T(8,128)S(1)}, u32[]{:S(2)}, u32[]{:S(2)}) collective-permute-start(f32[6,2,4,1152]{3,0,1,2:T(8,128)S(1)} %get-tuple-element.21), channel_id=1, source_target_pairs={{32,0},{64,32},{96,64},{128,96},{160,128},{192,160},{224,192},{256... | collective-permute-start | bytes 663560 | tf_op jit(solution)/shard_map/ppermute | solution.py:17
  47.1 14.6 %collective-permute-start.4 = (f32[6,2,4,1152]{3,0,1,2:T(8,128)S(1)}, f32[6,2,4,1152]{3,0,1,2:T(8,128)S(1)}, u32[]{:S(2)}, u32[]{:S(2)}) collective-permute-start(f32[6,2,4,1152]{3,0,1,2:T(8,128)S(1)} %get-tuple-element.20), channel_id=1, source_target_pairs={{0,32},{32,64},{64,96},{96,128},{128,160},{160,192},{192,224},{224... | collective-permute-start | bytes 663560 | tf_op jit(solution)/shard_map/ppermute | solution.py:14
  62.0 11.3 %collective-permute-start.5 = (f32[6,1,4,1152]{3,0,1,2:T(8,128)S(1)}, f32[6,1,4,1152]{3,0,1,2:T(8,128)S(1)}, u32[]{:S(2)}, u32[]{:S(2)}) collective-permute-start(f32[6,1,4,1152]{3,0,1,2:T(8,128)S(1)} %slice.305), channel_id=1, source_target_pairs={{0,32},{32,64},{64,96},{96,128},{128,160},{160,192},{192,224},{224... | collective-permute-start | bytes 331784 | tf_op jit(solution)/shard_map/ppermute | solution.py:25
  73.3 11.8 %copy-start.18 = (f32[3,4,1152]{2,1,0:T(4,128)S(1)}, f32[3,4,1152]{2,1,0:T(4,128)}, u32[]{:S(2)}) copy-start(f32[3,4,1152]{2,1,0:T(4,128)} %param.10) | copy-start | bytes 165892
  73.5 22.9 %collective-permute-start.6 = (f32[6,3,4,1152]{3,0,1,2:T(8,128)S(1)}, f32[6,3,4,1152]{3,0,1,2:T(8,128)S(1)}, u32[]{:S(2)}, u32[]{:S(2)}) collective-permute-start(f32[6,3,4,1152]{3,0,1,2:T(8,128)S(1)} %fusion.33), channel_id=1, source_target_pairs={{0,1},{1,2},{2,3},{3,4},{4,5},{5,6},{6,7},{7,8},{8,9},{9,10},{10,1... | collective-permute-start | bytes 995336 | tf_op jit(solution)/shard_map/ppermute | solution.py:25
  75.4 21.0 %collective-permute-start.7 = (f32[6,3,4,1152]{3,0,1,2:T(8,128)S(1)}, f32[6,3,4,1152]{3,0,1,2:T(8,128)S(1)}, u32[]{:S(2)}, u32[]{:S(2)}) collective-permute-start(f32[6,3,4,1152]{3,0,1,2:T(8,128)S(1)} %fusion.33), channel_id=1, source_target_pairs={{1,0},{2,1},{3,2},{4,3},{5,4},{6,5},{7,6},{8,7},{9,8},{10,9},{11,1... | collective-permute-start | bytes 995336 | tf_op jit(solution)/shard_map/ppermute | solution.py:25
  86.0 28.7 %all-to-all-start.1 = ((f32[32,3,1152]{2,1,0:T(4,128)}), f32[32,3,1152]{2,1,0:T(4,128)S(1)}, u32[]{:S(2)}, u32[]{:S(2)}) async-start(f32[32,3,1152]{2,1,0:T(4,128)} %broadcast_in_dim.209), calls=%async_computation.1 | async-start | bytes 1179648 | tf_op jit(solution)/shard_map/all_to_all | solution.py:30
  98.1 0.7 copy-start.13
  98.1 0.7 copy-start.14
  98.1 0.7 copy-start.15
  114.9 0.7 copy-start.19
where the time goes:
time: 117 us; the launch traced here: 116 us
  waiting for transfers between devices  47.6 us (41%)
  starting transfers between devices  43.9 us (38%)
  local copies, waits for them, and re-layouts  16.2 us (14%)
  other arithmetic  7.21 us (6%)
  between operations  1.4 us (1%)
    ppermute x4, waiting for transfers between devices, from_behind(): return lax.ppermute(x, axis, pairs)  17.5 us
    all_to_all x1, waiting for transfers between devices, from_everyone(): lax.all_to_all(jnp.broadcast_to(x[None], (count, *x.shape)), axis, 0, 0,...  14.5 us
    ppermute x4, starting transfers between devices, from_behind(): return lax.ppermute(x, axis, pairs)  13.8 us
    all_to_all x1, starting transfers between devices, from_everyone(): lax.all_to_all(jnp.broadcast_to(x[None], (count, *x.shape)), axis, 0, 0,...  9.62 us
    all_to_all x1, starting transfers between devices, per_device(): lax.all_to_all(jnp.stack([delta_col, remap_weight]), 'lev', split_axis=2,...  8.72 us
    ppermute x2, waiting for transfers between devices, extended_2(): lax.ppermute(lax.slice_in_dim(block, block.shape[dim] - width, None, axis...  7.73 us
    ppermute x2, starting transfers between devices, extended_2(): lax.ppermute(lax.slice_in_dim(block, 0, width, axis=dim), axis, backward)  6.69 us
    unnamed x44, local copies, waits for them, and re-layouts  5.18 us
  transfers between devices with their start and end apart: 10, of which 6 were waited for; matrix products, arithmetic and copies ran while one was open for 14% of the time, Pallas kernels for 0%

commit v1 on v0

v1 whole, which is shorter than its diff:
```python
import functools

import jax
import jax.numpy as jnp
from jax import lax
from jax.experimental import pallas as pl
from jax.experimental.pallas import tpu as pltpu
from jax.sharding import PartitionSpec as P


def pick(offset, behind, here, ahead, beyond):
    return jnp.where(
        offset == -1,
        behind,
        jnp.where(offset == 0, here, jnp.where(offset == 1, ahead, beyond)),
    )


def east_kernel(q_ref, courant_ref, offsets_ref, base_ref):
    count, rows, _, width = q_ref.shape
    for row in range(rows):
        offset = offsets_ref[1, row]
        weight = courant_ref[1, row]
        for f in range(count):
            q = q_ref[f, row]
            moved = pick(
                offset,
                pltpu.roll(q, 1, 1),
                q,
                pltpu.roll(q, width - 1, 1),
                pltpu.roll(q, width - 2, 1),
            )
            east = weight * moved
            base_ref[f, row] = q - (east - pltpu.roll(east, 1, 1))


def advected(f, base_ref, q_ref, low_ref, high_ref, face_ref, courant_ref, offsets_ref):
    rows = q_ref.shape[1]
    around = (
        [low_ref[f, 0], low_ref[f, 1]]
        + [q_ref[f, row] for row in range(rows)]
        + [high_ref[f, 0], high_ref[f, 1]]
    )
    south = face_ref[6, 0] * pick(face_ref[6, 1].astype(jnp.int32), *around[0:4])
    result = []
    for row in range(rows):
        north = courant_ref[0, row] * pick(offsets_ref[0, row], *around[row + 1 : row + 5])
        result.append(base_ref[f, row] - (north - south))
        south = north
    return result


def first_kernel(base_ref, q_ref, low_ref, high_ref, courant_ref, offsets_ref, out_ref, up_ref, down_ref):
    count, rows = q_ref.shape[:2]
    for f in range(count):
        new = advected(f, base_ref, q_ref, low_ref, high_ref, low_ref, courant_ref, offsets_ref)
        for row in range(rows):
            out_ref[f, row] = new[row]
        for k in range(2):
            up_ref[f, k] = new[rows - 2 + k]
            down_ref[f, k] = new[k]


def second_kernel(
    base_ref,
    q_ref,
    low_ref,
    high_ref,
    face_ref,
    courant_ref,
    offsets_ref,
    thickness_ref,
    surface_ref,
    out_ref,
    part_ref,
    sums_ref,
):
    count, rows, levels, width = q_ref.shape
    sums = []
    for f in range(count):
        new = advected(f, base_ref, q_ref, low_ref, high_ref, face_ref, courant_ref, offsets_ref)
        for row in range(rows):
            out_ref[f, row] = new[row]
            if f == 0:
                heating = new[row] * thickness_ref[row]
                below = jnp.zeros((1, width), jnp.float32)
                deeper = []
                for k in range(levels - 1, -1, -1):
                    deeper.insert(0, below)
                    below = below + heating[k : k + 1]
                part_ref[row] = (
                    jnp.concatenate(deeper, axis=0) + 0.5 * heating + surface_ref[row : row + 1]
                )
                sums.append(below)
    sums = jnp.concatenate(sums, axis=0)
    for k in range(sums_ref.shape[0]):
        sums_ref[k] = sums


def remap_kernel(q_ref, above_ref, under_ref, delta_ref, weight_ref, out_ref):
    count, rows, levels, width = q_ref.shape
    me = lax.axis_index("lev")
    is_first = me == 0
    is_last = me == lax.axis_size("lev") - 1
    sub = lax.broadcasted_iota(jnp.int32, (8, width), 0)
    for row in range(rows):
        delta = delta_ref[row].astype(jnp.int32)
        source = jnp.concatenate([delta, delta], axis=0) + (sub & 3) + 2
        t = weight_ref[row]
        for f in range(count):
            own = q_ref[f, row]
            above = jnp.where(is_first, jnp.broadcast_to(own[0:1], own.shape), above_ref[f, row])
            under = jnp.where(is_last, jnp.broadcast_to(own[levels - 1 :], own.shape), under_ref[f, row])
            early = jnp.concatenate([above, own], axis=0)
            late = jnp.concatenate([own, under], axis=0)
            windows = [early]
            for k in range(1, 4):
                windows.append(
                    jnp.where(sub < 4, pltpu.roll(early, 8 - k, 0), pltpu.roll(late, 4 - k, 0))
                )
            windows.append(late)
            w0, w1, w2, w3, w4 = windows
            left = (7.0 * (w1 + w2) - (w0 + w3)) * (1.0 / 12.0)
            right = (7.0 * (w2 + w3) - (w1 + w4)) * (1.0 / 12.0)
            slope = right - left
            curve = 6.0 * w2 - 3.0 * (left + right)
            left, slope, curve = (
                jnp.take_along_axis(x, source, axis=0)[:levels] for x in (left, slope, curve)
            )
            out_ref[f, row] = left + t * (slope + curve * (1.0 - t))


def close_kernel(part_ref, sums_ref, out_ref):
    rows = part_ref.shape[0]
    me = lax.axis_index("lev")
    total = jnp.zeros(sums_ref.shape[1:], jnp.float32)
    for k in range(sums_ref.shape[0]):
        total = total + jnp.where(k > me, sums_ref[k], 0.0)
    for row in range(rows):
        out_ref[row] = part_ref[row] + total[row : row + 1]


def call(kernel, out, flops, *args):
    shapes = [jax.ShapeDtypeStruct(s, jnp.float32) for s in out]
    size = sum(x.size for x in args) + sum(s.size for s in shapes)
    return pl.pallas_call(
        kernel,
        out_shape=shapes,
        in_specs=[pl.BlockSpec(memory_space=pltpu.VMEM)] * len(args),
        out_specs=[pl.BlockSpec(memory_space=pltpu.VMEM)] * len(out),
        cost_estimate=pl.CostEstimate(flops=flops, bytes_accessed=4 * size, transcendentals=0),
    )(*args)


def per_device(state, courant, offsets, log_thickness, surface, remap_level, remap_weight):
    count, rows, levels, width = state.shape
    lats, groups = lax.axis_size("lat"), lax.axis_size("lev")

    def ahead(n):
        return [(i, i + 1) for i in range(n - 1)]

    def back(n):
        return [(i + 1, i) for i in range(n - 1)]

    work = 20 * state.size
    face = jnp.stack([courant[0, rows - 1], offsets[0, rows - 1].astype(jnp.float32)])
    up = jnp.concatenate([state[:, rows - 2 :], face[None]], axis=0)
    low = lax.ppermute(up, "lat", ahead(lats))
    high = lax.ppermute(state[:, :2], "lat", back(lats))

    total_levels = remap_level.shape[1]
    delta_col = (remap_level - jnp.arange(total_levels, dtype=jnp.int32)[None, :, None]).astype(
        jnp.float32
    )
    inputs = lax.all_to_all(
        jnp.stack([delta_col, remap_weight]), "lev", split_axis=2, concat_axis=3, tiled=True
    )

    (base,) = call(east_kernel, [state.shape], work, state, courant, offsets)
    edge = (count, 2, levels, width)
    field, up, down = call(
        first_kernel, [state.shape, edge, edge], work, base, state, low, high, courant, offsets
    )
    low2 = lax.ppermute(up, "lat", ahead(lats))
    high2 = lax.ppermute(down, "lat", back(lats))
    (base,) = call(east_kernel, [state.shape], work, field, courant, offsets)
    field, part, sums = call(
        second_kernel,
        [state.shape, log_thickness.shape, (groups, rows, width)],
        work,
        base,
        field,
        low2,
        high2,
        low,
        courant,
        offsets,
        log_thickness,
        surface,
    )
    above = lax.ppermute(field, "lev", ahead(groups))
    under = lax.ppermute(field, "lev", back(groups))
    sums = lax.all_to_all(sums, "lev", 0, 0, tiled=True)
    (remapped,) = call(
        remap_kernel, [state.shape], 2 * work, field, above, under, inputs[0], inputs[1]
    )
    (geopotential,) = call(close_kernel, [log_thickness.shape], sums.size, part, sums)
    return (remapped, geopotential)


def solution(mesh):
    in_specs = (
        P(None, "lat", "lev", None),
        P(None, "lat", "lev", None),
        P(None, "lat", "lev", None),
        P("lat", "lev", None),
        P("lat", None),
        P("lat", None, "lev"),
        P("lat", None, "lev"),
    )
    out_specs = (P(None, "lat", "lev", None), P("lat", "lev", None))
    return jax.shard_map(
        per_device, mesh=mesh, in_specs=in_specs, out_specs=out_specs, check_vma=False
    )
```

time: 117 us -> 89.8 us (0.77)
  the two profiles are of different devices: /device:TPU:320 before, /device:TPU:174 now
where the time goes in v1:
time: 89.8 us; the launch traced here: 89 us
  starting transfers between devices  37.1 us (41%)
  waiting for transfers between devices  21 us (23%)
  Pallas kernels  16.5 us (18%)
  local copies, waits for them, and re-layouts  11.7 us (13%)
  other arithmetic  1.83 us (2%)
    pallas_call x6, Pallas kernels, call(): pl.pallas_call(kernel, out_shape=shapes, in_specs=[pl.BlockSpec(memory_sp...  16.5 us
    ppermute x1, waiting for transfers between devices, per_device(): high = lax.ppermute(state[:, :2], 'lat', back(lats))  11.4 us
    ppermute x1, waiting for transfers between devices, per_device(): above = lax.ppermute(field, 'lev', ahead(groups))  9.38 us
    all_to_all x1, starting transfers between devices, per_device(): sums = lax.all_to_all(sums, 'lev', 0, 0, tiled=True)  8.41 us
    unnamed x22, local copies, waits for them, and re-layouts  7.39 us
    all_to_all x1, starting transfers between devices, per_device(): lax.all_to_all(jnp.stack([delta_col, remap_weight]), 'lev', split_axis=2,...  7.26 us
    ppermute x1, starting transfers between devices, per_device(): low = lax.ppermute(up, 'lat', ahead(lats))  7.21 us
    ppermute x1, starting transfers between devices, per_device(): under = lax.ppermute(field, 'lev', back(groups))  4.43 us
  transfers between devices with their start and end apart: 8, of which 3 were waited for; matrix products, arithmetic and copies ran while one was open for 6% of the time, Pallas kernels for 14%

profile of v1, /device:TPU:174, one launch (start us, length us, event | category | flops | bytes accessed | tf_op | source)
XLA Modules:
  0.0 89.0 jit_solution(8410210189180622171)
XLA Ops:
  0.6 1.1 %fusion.1 = (f32[6,2,4,1152]{3,2,1,0:T(4,128)S(1)}, f32[6,2,4,1152]{3,2,1,0:T(4,128)S(1)}) fusion(f32[6,3,4,1152]{3,2,1,0:T(4,128)} %q_ref.3), kind=kLoop, calls=%fused_computation.7 | loop fusion | bytes 884736 | tf_op jit(solution)/shard_map/slice | solution.py:169
  1.7 0.7 convert_bitcast_fusion
  2.4 0.7 slice_bitcast_fusion
  3.2 0.0 copy-start.9
  3.2 0.1 pad_maximum_fusion
  3.3 7.2 %collective-permute-start = (f32[7,2,4,1152]{3,2,1,0:T(4,128)S(1)}, f32[7,2,4,1152]{3,2,1,0:T(4,128)S(1)}, u32[]{:S(2)}, u32[]{:S(2)}) collective-permute-start(f32[7,2,4,1152]{3,2,1,0:T(4,128)S(1)} %pad_maximum_fusion), channel_id=1, source_target_pairs={{0,32},{32,64},{64,96},{96,128},{128,160},{160,192},{192,224},{224... | collective-permute-start | bytes 774152 | tf_op jit(solution)/shard_map/ppermute | solution.py:168
  10.5 1.9 %collective-permute-start.1 = (f32[6,2,4,1152]{3,2,1,0:T(4,128)S(1)}, f32[6,2,4,1152]{3,2,1,0:T(4,128)S(1)}, u32[]{:S(2)}, u32[]{:S(2)}) collective-permute-start(f32[6,2,4,1152]{3,2,1,0:T(4,128)S(1)} %get-tuple-element.16), channel_id=1, source_target_pairs={{32,0},{64,32},{96,64},{128,96},{160,128},{192,160},{224,192},{256... | collective-permute-start | bytes 663560 | tf_op jit(solution)/shard_map/ppermute | solution.py:169
  12.4 0.0 copy-done.9
  12.4 0.0 copy-start.8
  12.5 0.8 copy-done.8
  13.3 3.6 %shard_map.86.base_ref = f32[6,3,4,1152]{3,2,1,0:T(4,128)} custom-call(f32[6,3,4,1152]{3,2,1,0:T(4,128)} %q_ref.3, f32[2,3,4,1152]{3,2,1,0:T(4,128)} %courant_ref.7, s32[2,3,4,1152]{3,2,1,0:T(4,128)} %offsets_ref.7), custom_call_target="tpu_custom_call" | custom-call | flops 1658880 | bytes 884736 | tf_op jit(solution)/shard_map/pallas_call | solution.py:146
  16.9 11.4 %collective-permute-done.1.high_ref = f32[6,2,4,1152]{3,2,1,0:T(4,128)S(1)} collective-permute-done((f32[6,2,4,1152]{3,2,1,0:T(4,128)S(1)}, f32[6,2,4,1152]{3,2,1,0:T(4,128)S(1)}, u32[]{:S(2)}, u32[]{:S(2)}) %collective-permute-start.1) | collective-permute-done | bytes 221216 | tf_op jit(solution)/shard_map/ppermute | solution.py:169
  28.2 0.0 copy-start.7
  28.2 0.0 collective-permute-done.low_ref.face_ref
  28.2 0.7 copy-done.7
  28.9 0.0 copy-start.1
  28.9 0.7 copy-done.1
  29.6 2.3 %shard_map.87 = (f32[6,3,4,1152]{3,2,1,0:T(4,128)}, f32[6,2,4,1152]{3,2,1,0:T(4,128)}, f32[6,2,4,1152]{3,2,1,0:T(4,128)}) custom-call(f32[6,3,4,1152]{3,2,1,0:T(4,128)} %shard_map.86.base_ref, f32[6,3,4,1152]{3,2,1,0:T(4,128)} %q_ref.3, f32[7,2,4,1152]{3,2,1,0:T(4,128)} %copy-done.1, f32[6,2,4,1152]{3,2,1,0:T(4,128)} %copy-done.7, ...), custom_call_target="tpu_custom_call" | custom-call | flops 1658880 | bytes 2138112 | tf_op jit(solution)/shard_map/pallas_call | solution.py:146
  31.9 1.9 %collective-permute-start.2 = (f32[6,2,4,1152]{3,2,1,0:T(4,128)}, f32[6,2,4,1152]{3,2,1,0:T(4,128)S(1)}, u32[]{:S(2)}, u32[]{:S(2)}) collective-permute-start(f32[6,2,4,1152]{3,2,1,0:T(4,128)} %get-tuple-element.9), channel_id=1, source_target_pairs={{0,32},{32,64},{64,96},{96,128},{128,160},{160,192},{192,224},{224... | collective-permute-start | bytes 663560 | tf_op jit(solution)/shard_map/ppermute | solution.py:184
  33.8 3.9 %collective-permute-start.3 = (f32[6,2,4,1152]{3,2,1,0:T(4,128)}, f32[6,2,4,1152]{3,2,1,0:T(4,128)S(1)}, u32[]{:S(2)}, u32[]{:S(2)}) collective-permute-start(f32[6,2,4,1152]{3,2,1,0:T(4,128)} %get-tuple-element.10), channel_id=1, source_target_pairs={{32,0},{64,32},{96,64},{128,96},{160,128},{192,160},{224,192},{256... | collective-permute-start | bytes 663560 | tf_op jit(solution)/shard_map/ppermute | solution.py:185
  37.7 0.1 pad_maximum_fusion.1
  37.9 0.3 copy.18
  38.1 1.2 %reshape.19 = f32[32,1,864]{2,1,0:T(1,128)} reshape(f32[128,3,2,36]{3,2,1,0:T(2,128)S(1)} %bitcast.21) | data formatting | bytes 221184
  39.4 7.3 %all-to-all-start = ((f32[32,1,864]{2,1,0:T(1,128)}), f32[32,1,864]{2,1,0:T(1,128)S(1)}, u32[]{:S(2)}, u32[]{:S(2)}) async-start(f32[32,1,864]{2,1,0:T(1,128)} %reshape.19), calls=%async_computation | async-start | bytes 229376 | tf_op jit(solution)/shard_map/all_to_all | solution.py:175
  46.6 3.6 %shard_map.88.base_ref = f32[6,3,4,1152]{3,2,1,0:T(4,128)} custom-call(f32[6,3,4,1152]{3,2,1,0:T(4,128)} %get-tuple-element.8.q_ref, f32[2,3,4,1152]{3,2,1,0:T(4,128)} %courant_ref.7, s32[2,3,4,1152]{3,2,1,0:T(4,128)} %offsets_ref.7), custom_call_target="tpu_custom_call" | custom-call | flops 1658880 | bytes 884736 | tf_op jit(solution)/shard_map/pallas_call | solution.py:146
  50.2 0.0 collective-permute-done.2.low_ref
  50.2 0.3 collective-permute-done.3.high_ref
  50.5 0.4 copy-done.5
  50.9 0.7 copy-done.6
  51.6 2.5 %shard_map.89 = (f32[6,3,4,1152]{3,2,1,0:T(4,128)}, f32[3,4,1152]{2,1,0:T(4,128)}, f32[32,3,1152]{2,1,0:T(4,128)}) custom-call(f32[6,3,4,1152]{3,2,1,0:T(4,128)} %shard_map.88.base_ref, f32[6,3,4,1152]{3,2,1,0:T(4,128)} %get-tuple-element.8.q_ref, f32[6,2,4,1152]{3,2,1,0:T(4,128)} %copy-done.5, f32[6,2,4,1152]{3,2,1,0:T(4,128)} %copy-done.6, ...), custom_call_target="tpu_custom_call" | custom-call | flops 1658880 | bytes 2483712 | tf_op jit(solution)/shard_map/pallas_call | solution.py:146
  54.1 0.0 all-to-all-done
  54.1 8.4 %all-to-all-start.1 = ((f32[32,3,1152]{2,1,0:T(4,128)}), f32[32,3,1152]{2,1,0:T(4,128)S(1)}, u32[]{:S(2)}, u32[]{:S(2)}) async-start(f32[32,3,1152]{2,1,0:T(4,128)} %get-tuple-element.13), calls=%async_computation.1 | async-start | bytes 1179648 | tf_op jit(solution)/shard_map/all_to_all | solution.py:203
  62.5 0.0 copy-done.2
  62.5 2.0 %collective-permute-start.4 = (f32[6,3,4,1152]{3,2,1,0:T(4,128)S(1)}, f32[6,3,4,1152]{3,2,1,0:T(4,128)S(1)}, u32[]{:S(2)}, u32[]{:S(2)}) collective-permute-start(f32[6,3,4,1152]{3,2,1,0:T(4,128)S(1)} %copy-done.2), channel_id=1, source_target_pairs={{0,1},{1,2},{2,3},{3,4},{4,5},{5,6},{6,7},{7,8},{8,9},{9,10},{10,1... | collective-permute-start | bytes 995336 | tf_op jit(solution)/shard_map/ppermute | solution.py:201
  64.6 4.4 %collective-permute-start.5 = (f32[6,3,4,1152]{3,2,1,0:T(4,128)S(1)}, f32[6,3,4,1152]{3,2,1,0:T(4,128)S(1)}, u32[]{:S(2)}, u32[]{:S(2)}) collective-permute-start(f32[6,3,4,1152]{3,2,1,0:T(4,128)S(1)} %copy-done.2), channel_id=1, source_target_pairs={{1,0},{2,1},{3,2},{4,3},{5,4},{6,5},{7,6},{8,7},{9,8},{10,9},{11,1... | collective-permute-start | bytes 995336 | tf_op jit(solution)/shard_map/ppermute | solution.py:202
  69.0 0.5 broadcast
  69.5 0.9 %reduce = f32[32,864]{1,0:T(8,128)S(1)} reduce(f32[32,1,864]{2,1,0:T(1,128)S(1)} %all-to-all-done, f32[]{:T(128)} %broadcast), dimensions={1}, to_apply=%all_to_all.14.reduce_sub_computation | reduce | bytes 221188 | tf_op jit(solution)/shard_map/all_to_all | solution.py:175
  70.4 0.6 reshape.20
  71.1 0.8 squeeze.7.delta_ref
  71.9 0.8 squeeze.8.weight_ref
  72.7 9.4 %collective-permute-done.4.above_ref = f32[6,3,4,1152]{3,2,1,0:T(4,128)S(1)} collective-permute-done((f32[6,3,4,1152]{3,2,1,0:T(4,128)S(1)}, f32[6,3,4,1152]{3,2,1,0:T(4,128)S(1)}, u32[]{:S(2)}, u32[]{:S(2)}) %collective-permute-start.4) | collective-permute-done | bytes 331808 | tf_op jit(solution)/shard_map/ppermute | solution.py:201
  82.1 0.0 collective-permute-done.5.under_ref
  82.1 0.7 copy-done.3
  82.9 0.7 copy-done.4
  83.6 2.8 %shard_map.90 = f32[6,3,4,1152]{3,2,1,0:T(4,128)} custom-call(f32[6,3,4,1152]{3,2,1,0:T(4,128)} %get-tuple-element.11.q_ref, f32[6,3,4,1152]{3,2,1,0:T(4,128)} %copy-done.3, f32[6,3,4,1152]{3,2,1,0:T(4,128)} %copy-done.4, f32[3,4,1152]{2,1,0:T(4,128)} %squeeze.7.delta_ref, f32[3,4,1152]{2,1,0:T(4,128)} %squeeze.8.weight_ref), custom_call_target="tpu_custom_call" | custom-call | flops 3317760 | bytes 1437696 | tf_op jit(solution)/shard_map/pallas_call | solution.py:146
  86.4 0.0 all-to-all-done.1.sums_ref
  86.4 0.8 copy-done
  87.2 1.8 %shard_map.91 = f32[3,4,1152]{2,1,0:T(4,128)} custom-call(f32[3,4,1152]{2,1,0:T(4,128)} %get-tuple-element.12.part_ref, f32[32,3,1152]{2,1,0:T(4,128)} %copy-done), custom_call_target="tpu_custom_call" | custom-call | flops 110592 | bytes 552960 | tf_op jit(solution)/shard_map/pallas_call | solution.py:146
  (14 shorter events, 0.2 us)
Async XLA Ops:
  3.2 9.2 %copy-start.9 = (s32[3,128,36]{1,2,0:T(8,128)S(1)}, s32[3,128,36]{1,2,0:T(8,128)}, u32[]{:S(2)}) copy-start(s32[3,128,36]{1,2,0:T(8,128)} %param.12) | copy-start | bytes 165892
  3.3 25.0 %collective-permute-start = (f32[7,2,4,1152]{3,2,1,0:T(4,128)S(1)}, f32[7,2,4,1152]{3,2,1,0:T(4,128)S(1)}, u32[]{:S(2)}, u32[]{:S(2)}) collective-permute-start(f32[7,2,4,1152]{3,2,1,0:T(4,128)S(1)} %pad_maximum_fusion), channel_id=1, source_target_pairs={{0,32},{32,64},{64,96},{96,128},{128,160},{160,192},{192,224},{224... | collective-permute-start | bytes 774152 | tf_op jit(solution)/shard_map/ppermute | solution.py:168
  10.5 17.7 %collective-permute-start.1 = (f32[6,2,4,1152]{3,2,1,0:T(4,128)S(1)}, f32[6,2,4,1152]{3,2,1,0:T(4,128)S(1)}, u32[]{:S(2)}, u32[]{:S(2)}) collective-permute-start(f32[6,2,4,1152]{3,2,1,0:T(4,128)S(1)} %get-tuple-element.16), channel_id=1, source_target_pairs={{32,0},{64,32},{96,64},{128,96},{160,128},{192,160},{224,192},{256... | collective-permute-start | bytes 663560 | tf_op jit(solution)/shard_map/ppermute | solution.py:169
  12.4 0.8 copy-start.8
  28.2 0.7 copy-start.7
  28.9 0.7 copy-start.1
  31.9 18.3 %collective-permute-start.2 = (f32[6,2,4,1152]{3,2,1,0:T(4,128)}, f32[6,2,4,1152]{3,2,1,0:T(4,128)S(1)}, u32[]{:S(2)}, u32[]{:S(2)}) collective-permute-start(f32[6,2,4,1152]{3,2,1,0:T(4,128)} %get-tuple-element.9), channel_id=1, source_target_pairs={{0,32},{32,64},{64,96},{96,128},{128,160},{160,192},{192,224},{224... | collective-permute-start | bytes 663560 | tf_op jit(solution)/shard_map/ppermute | solution.py:184
  33.8 16.7 %collective-permute-start.3 = (f32[6,2,4,1152]{3,2,1,0:T(4,128)}, f32[6,2,4,1152]{3,2,1,0:T(4,128)S(1)}, u32[]{:S(2)}, u32[]{:S(2)}) collective-permute-start(f32[6,2,4,1152]{3,2,1,0:T(4,128)} %get-tuple-element.10), channel_id=1, source_target_pairs={{32,0},{64,32},{96,64},{128,96},{160,128},{192,160},{224,192},{256... | collective-permute-start | bytes 663560 | tf_op jit(solution)/shard_map/ppermute | solution.py:185
  39.4 14.7 %all-to-all-start = ((f32[32,1,864]{2,1,0:T(1,128)}), f32[32,1,864]{2,1,0:T(1,128)S(1)}, u32[]{:S(2)}, u32[]{:S(2)}) async-start(f32[32,1,864]{2,1,0:T(1,128)} %reshape.19), calls=%async_computation | async-start | bytes 229376 | tf_op jit(solution)/shard_map/all_to_all | solution.py:175
  50.2 0.7 copy-start.5
  50.9 0.7 copy-start.6
  54.1 8.4 %copy-start.2 = (f32[6,3,4,1152]{3,2,1,0:T(4,128)S(1)}, f32[6,3,4,1152]{3,2,1,0:T(4,128)}, u32[]{:S(2)}) copy-start(f32[6,3,4,1152]{3,2,1,0:T(4,128)} %get-tuple-element.11.q_ref) | copy-start | bytes 995332
  54.1 32.3 %all-to-all-start.1 = ((f32[32,3,1152]{2,1,0:T(4,128)}), f32[32,3,1152]{2,1,0:T(4,128)S(1)}, u32[]{:S(2)}, u32[]{:S(2)}) async-start(f32[32,3,1152]{2,1,0:T(4,128)} %get-tuple-element.13), calls=%async_computation.1 | async-start | bytes 1179648 | tf_op jit(solution)/shard_map/all_to_all | solution.py:203
  62.5 19.6 %collective-permute-start.4 = (f32[6,3,4,1152]{3,2,1,0:T(4,128)S(1)}, f32[6,3,4,1152]{3,2,1,0:T(4,128)S(1)}, u32[]{:S(2)}, u32[]{:S(2)}) collective-permute-start(f32[6,3,4,1152]{3,2,1,0:T(4,128)S(1)} %copy-done.2), channel_id=1, source_target_pairs={{0,1},{1,2},{2,3},{3,4},{4,5},{5,6},{6,7},{7,8},{8,9},{9,10},{10,1... | collective-permute-start | bytes 995336 | tf_op jit(solution)/shard_map/ppermute | solution.py:201
  64.6 17.6 %collective-permute-start.5 = (f32[6,3,4,1152]{3,2,1,0:T(4,128)S(1)}, f32[6,3,4,1152]{3,2,1,0:T(4,128)S(1)}, u32[]{:S(2)}, u32[]{:S(2)}) collective-permute-start(f32[6,3,4,1152]{3,2,1,0:T(4,128)S(1)} %copy-done.2), channel_id=1, source_target_pairs={{1,0},{2,1},{3,2},{4,3},{5,4},{6,5},{7,6},{8,7},{9,8},{10,9},{11,1... | collective-permute-start | bytes 995336 | tf_op jit(solution)/shard_map/ppermute | solution.py:202
  82.1 0.7 copy-start.3
  82.9 0.7 copy-start.4
  86.4 0.8 copy-start

commit v2 on v1

v2 whole, which is shorter than its diff:
```python
import jax
import jax.numpy as jnp
from jax import lax
from jax.experimental import pallas as pl
from jax.experimental.pallas import tpu as pltpu
from jax.sharding import PartitionSpec as P


NEAR = 4


def pick(offset, behind, here, ahead, beyond):
    return jnp.where(
        offset == -1,
        behind,
        jnp.where(offset == 0, here, jnp.where(offset == 1, ahead, beyond)),
    )


def east_kernel(q_ref, courant_ref, offsets_ref, base_ref):
    count, rows, _, width = q_ref.shape
    for row in range(rows):
        offset = offsets_ref[1, row]
        weight = courant_ref[1, row]
        for f in range(count):
            q = q_ref[f, row]
            moved = pick(
                offset,
                pltpu.roll(q, 1, 1),
                q,
                pltpu.roll(q, width - 1, 1),
                pltpu.roll(q, width - 2, 1),
            )
            east = weight * moved
            base_ref[f, row] = q - (east - pltpu.roll(east, 1, 1))


def is_even():
    return lax.rem(lax.axis_index("lat"), 2) == 0


def advected(f, base_ref, q_ref, slow_ref, fast_ref, face, courant_ref, offsets_ref):
    rows = q_ref.shape[1]
    even = is_even()
    low, high = [], []
    for k in range(2):
        slow, fast = slow_ref[f, k], fast_ref[f, k]
        low.append(jnp.where(even, slow, fast))
        high.append(jnp.where(even, fast, slow))
    around = low + [q_ref[f, row] for row in range(rows)] + high
    south = face[0] * pick(face[1], *around[0:4])
    result = []
    for row in range(rows):
        north = courant_ref[0, row] * pick(offsets_ref[0, row], *around[row + 1 : row + 5])
        result.append(base_ref[f, row] - (north - south))
        south = north
    return result


def send(f, new, slow_ref, fast_ref):
    even = is_even()
    for k in range(2):
        up, down = new[len(new) - 2 + k], new[k]
        slow_ref[f, k] = jnp.where(even, down, up)
        fast_ref[f, k] = jnp.where(even, up, down)


def edges_kernel(q_ref, courant_ref, offsets_ref, slow_ref, fast_ref):
    count, rows = q_ref.shape[:2]
    for f in range(count):
        send(f, [q_ref[f, row] for row in range(rows)], slow_ref, fast_ref)
    for k, value in enumerate((courant_ref[0, rows - 1], offsets_ref[0, rows - 1].astype(jnp.float32))):
        slow_ref[count, k] = value
        fast_ref[count, k] = value


def first_kernel(
    base_ref, q_ref, slow_ref, fast_ref, courant_ref, offsets_ref, out_ref, face_ref, next_slow_ref, next_fast_ref
):
    count, rows = q_ref.shape[:2]
    face = [jnp.where(is_even(), slow_ref[count, k], fast_ref[count, k]) for k in range(2)]
    for k in range(2):
        face_ref[k] = face[k]
    face[1] = face[1].astype(jnp.int32)
    for f in range(count):
        new = advected(f, base_ref, q_ref, slow_ref, fast_ref, face, courant_ref, offsets_ref)
        for row in range(rows):
            out_ref[f, row] = new[row]
        send(f, new, next_slow_ref, next_fast_ref)


def heat(new, thickness_ref, surface_ref, part_ref, sums_ref):
    sums = []
    for row, value in enumerate(new):
        levels, width = value.shape
        heating = value * thickness_ref[row]
        below = jnp.zeros((1, width), jnp.float32)
        deeper = []
        for k in range(levels - 1, -1, -1):
            deeper.insert(0, below)
            below = below + heating[k : k + 1]
        part_ref[row] = jnp.concatenate(deeper, axis=0) + 0.5 * heating + surface_ref[row : row + 1]
        sums.append(below)
    sums = jnp.concatenate(sums, axis=0)
    for k in range(sums_ref.shape[0]):
        sums_ref[k] = sums


def second_kernel(
    base_ref, q_ref, slow_ref, fast_ref, face_ref, courant_ref, offsets_ref, thickness_ref, surface_ref,
    out_ref, part_ref, sums_ref,
):
    count, rows = q_ref.shape[:2]
    face = face_ref[0], face_ref[1].astype(jnp.int32)
    for f in range(count):
        new = advected(f, base_ref, q_ref, slow_ref, fast_ref, face, courant_ref, offsets_ref)
        for row in range(rows):
            out_ref[f, row] = new[row]
        if f == 0:
            heat(new, thickness_ref, surface_ref, part_ref, sums_ref)


def remap_kernel(q_ref, chip_ref, other_ref, delta_ref, weight_ref, out_ref):
    count, rows, levels, width = q_ref.shape
    me = lax.axis_index("lev")
    is_first = me == 0
    even = lax.rem(me, 2) == 0
    is_last = me == lax.axis_size("lev") - 1
    sub = lax.broadcasted_iota(jnp.int32, (8, width), 0)
    for row in range(rows):
        delta = delta_ref[row].astype(jnp.int32)
        source = jnp.concatenate([delta, delta], axis=0) + (sub & 3) + 2
        t = weight_ref[row]
        for f in range(count):
            own = q_ref[f, row]
            above, under = chip_ref[f, row], other_ref[f, row]
            above, under = jnp.where(even, under, above), jnp.where(even, above, under)
            above = jnp.where(is_first, jnp.broadcast_to(own[0:1], own.shape), above)
            under = jnp.where(is_last, jnp.broadcast_to(own[levels - 1 :], own.shape), under)
            early = jnp.concatenate([above, own], axis=0)
            late = jnp.concatenate([own, under], axis=0)
            windows = [early]
            for k in range(1, 4):
                windows.append(
                    jnp.where(sub < 4, pltpu.roll(early, 8 - k, 0), pltpu.roll(late, 4 - k, 0))
                )
            windows.append(late)
            w0, w1, w2, w3, w4 = windows
            left = (7.0 * (w1 + w2) - (w0 + w3)) * (1.0 / 12.0)
            right = (7.0 * (w2 + w3) - (w1 + w4)) * (1.0 / 12.0)
            slope = right - left
            curve = 6.0 * w2 - 3.0 * (left + right)
            left, slope, curve = (
                jnp.take_along_axis(x, source, axis=0)[:levels] for x in (left, slope, curve)
            )
            out_ref[f, row] = left + t * (slope + curve * (1.0 - t))


def columns_kernel(level_ref, weight_ref, out_ref, held):
    rows, width, total = level_ref.shape
    at = lax.broadcasted_iota(jnp.int32, (width, total), 1)
    held[...] = jnp.zeros_like(held)
    for row in range(rows):
        held[row * width : (row + 1) * width] = (level_ref[row] - at).astype(jnp.float32)
        start = (rows + row) * width
        held[start : start + width] = weight_ref[row]
    turned = held[...].T
    count, levels, _ = out_ref.shape
    for k in range(count):
        out_ref[k] = turned[k * levels : (k + 1) * levels]


def join_kernel(in_ref, delta_ref, weight_ref):
    count = in_ref.shape[0]
    rows = delta_ref.shape[0]
    width = delta_ref.shape[2] // count
    for k in range(count):
        to = k * width
        for row in range(rows):
            delta_ref[row, :, to : to + width] = in_ref[k, :, row * width : (row + 1) * width]
            start = (rows + row) * width
            weight_ref[row, :, to : to + width] = in_ref[k, :, start : start + width]


def group_kernel(sums_ref, own_ref, out_ref):
    near = sums_ref.shape[0]
    me = lax.rem(lax.axis_index("lev"), near)
    own = jnp.zeros(sums_ref.shape[1:], jnp.float32)
    total = own
    for k in range(near):
        own = own + jnp.where(k > me, sums_ref[k], 0.0)
        total = total + sums_ref[k]
    own_ref[...] = own
    for k in range(out_ref.shape[0]):
        out_ref[k] = total


def close_kernel(part_ref, own_ref, sums_ref, out_ref):
    rows = part_ref.shape[0]
    me = lax.axis_index("lev") // NEAR
    total = own_ref[...]
    for k in range(sums_ref.shape[0]):
        total = total + jnp.where(k > me, sums_ref[k], 0.0)
    for row in range(rows):
        out_ref[row] = part_ref[row] + total[row : row + 1]


def call(kernel, out, flops, *args, scratch=()):
    shapes = [jax.ShapeDtypeStruct(s, jnp.float32) for s in out]
    size = sum(x.size for x in args) + sum(s.size for s in shapes)
    return pl.pallas_call(
        kernel,
        out_shape=shapes,
        scratch_shapes=scratch,
        in_specs=[pl.BlockSpec(memory_space=pltpu.VMEM)] * len(args),
        out_specs=[pl.BlockSpec(memory_space=pltpu.VMEM)] * len(out),
        compiler_params=pltpu.CompilerParams(vmem_limit_bytes=16 << 20),
        cost_estimate=pl.CostEstimate(flops=flops, bytes_accessed=4 * size, transcendentals=0),
    )(*args)


def per_device(state, courant, offsets, log_thickness, surface, remap_level, remap_weight):
    count, rows, levels, width = state.shape
    lats, groups = lax.axis_size("lat"), lax.axis_size("lev")

    def swaps(n, first):
        return [p for i in range(first, n - 1, 2) for p in ((i, i + 1), (i + 1, i))]

    work = 20 * state.size
    edge = (count, 2, levels, width)
    slow, fast = call(
        edges_kernel, [(count + 1, *edge[1:])] * 2, 1, state, courant, offsets
    )
    slow = lax.ppermute(slow, "lat", swaps(lats, 1))
    fast = lax.ppermute(fast, "lat", swaps(lats, 0))
    far = groups // NEAR
    close = [[j * NEAR + i for i in range(NEAR)] for j in range(far)]
    distant = [[j * NEAR + i for j in range(far)] for i in range(NEAR)]

    def exchange(x, among):
        return lax.all_to_all(x, "lev", 0, 0, tiled=True, axis_index_groups=among)

    (columns,) = call(
        columns_kernel,
        [(groups, levels, 256)],
        remap_level.size,
        jnp.transpose(remap_level, (0, 2, 1)),
        jnp.transpose(remap_weight, (0, 2, 1)),
        scratch=[pltpu.VMEM((256, remap_level.shape[1]), jnp.float32)],
    )
    columns = lax.all_to_all(columns, "lev", 0, 0, tiled=True)

    (base,) = call(east_kernel, [state.shape], work, state, courant, offsets)
    field, face, slow, fast = call(
        first_kernel, [state.shape, (2, levels, width), edge, edge], work, base, state, slow, fast, courant, offsets
    )
    slow = lax.ppermute(slow, "lat", swaps(lats, 1))
    fast = lax.ppermute(fast, "lat", swaps(lats, 0))
    (base,) = call(east_kernel, [state.shape], work, field, courant, offsets)
    delta, weight = call(join_kernel, [log_thickness.shape] * 2, columns.size, columns)
    delta, weight = call(join_kernel, [log_thickness.shape] * 2, columns.size, columns)
    field, part, sums = call(
        second_kernel, [state.shape, log_thickness.shape, (NEAR, rows, width)], work, base, field, slow, fast, face,
        courant, offsets, log_thickness, surface,
    )
    sums = exchange(sums, close)
    own, sums = call(group_kernel, [(rows, width), (far, rows, width)], sums.size, sums)
    above = lax.ppermute(field, "lev", swaps(groups, 0))
    under = lax.ppermute(field, "lev", swaps(groups, 1))
    sums = exchange(sums, distant)
    (remapped,) = call(
        remap_kernel, [state.shape], 2 * work, field, above, under, delta, weight
    )
    (geopotential,) = call(close_kernel, [log_thickness.shape], sums.size, part, own, sums)
    return (remapped, geopotential)


def solution(mesh):
    in_specs = (
        P(None, "lat", "lev", None),
        P(None, "lat", "lev", None),
        P(None, "lat", "lev", None),
        P("lat", "lev", None),
        P("lat", None),
        P("lat", None, "lev"),
        P("lat", None, "lev"),
    )
    out_specs = (P(None, "lat", "lev", None), P("lat", "lev", None))

    return jax.shard_map(per_device, mesh=mesh, in_specs=in_specs, out_specs=out_specs, check_vma=False)
```

time: 89.8 us -> 80.4 us (0.90)
  the two profiles are of different devices: /device:TPU:174 before, /device:TPU:134 now
where the time goes in v2:
time: 80.4 us; the launch traced here: 79.8 us
  starting transfers between devices  35.7 us (44%)
  waiting for transfers between devices  31.9 us (40%)
  Pallas kernels  8.53 us (11%)
  local copies, waits for them, and re-layouts  2.79 us (3%)
  between operations  0.81 us (1%)
    ppermute x2, starting transfers between devices, per_device(): slow = lax.ppermute(slow, 'lat', swaps(lats, 1))  14.5 us
    ppermute x2, waiting for transfers between devices, per_device(): slow = lax.ppermute(slow, 'lat', swaps(lats, 1))  13.2 us
    all_to_all x2, waiting for transfers between devices, exchange(): return lax.all_to_all(x, 'lev', 0, 0, tiled=True, axis_index_groups=among)  12.8 us
    pallas_call x10, Pallas kernels, call(): pl.pallas_call(kernel, out_shape=shapes, scratch_shapes=scratch, in_specs...  8.53 us
    all_to_all x1, starting transfers between devices, per_device(): columns = lax.all_to_all(columns, 'lev', 0, 0, tiled=True)  7.49 us
    all_to_all x2, starting transfers between devices, exchange(): return lax.all_to_all(x, 'lev', 0, 0, tiled=True, axis_index_groups=among)  7.06 us
    all_to_all x1, waiting for transfers between devices, per_device(): columns = lax.all_to_all(columns, 'lev', 0, 0, tiled=True)  5.88 us
    ppermute x2, starting transfers between devices, per_device(): fast = lax.ppermute(fast, 'lat', swaps(lats, 0))  3.84 us
  transfers between devices with their start and end apart: 9, of which 5 were waited for; matrix products, arithmetic and copies ran while one was open for 0% of the time, Pallas kernels for 7%

profile of v2, /device:TPU:134, one launch (start us, length us, event | category | flops | bytes accessed | tf_op | source)
XLA Modules:
  0.0 79.8 jit_solution(14854509021671329532)
XLA Ops:
  0.6 0.0 copy-start
  0.6 1.0 %copy-done = f32[6,3,4,1152]{3,2,1,0:T(4,128)S(1)} copy-done((f32[6,3,4,1152]{3,2,1,0:T(4,128)S(1)}, f32[6,3,4,1152]{3,2,1,0:T(4,128)}, u32[]{:S(2)}) %copy-start) | copy-done | bytes 331800
  1.6 0.0 copy-start.1
  1.6 0.9 %copy-done.1 = f32[2,3,4,1152]{3,2,1,0:T(4,128)S(1)} copy-done((f32[2,3,4,1152]{3,2,1,0:T(4,128)S(1)}, f32[2,3,4,1152]{3,2,1,0:T(4,128)}, u32[]{:S(2)}) %copy-start.1) | copy-done | bytes 110616
  2.5 0.0 copy-start.3
  2.5 0.9 %copy-done.3 = s32[2,3,4,1152]{3,2,1,0:T(4,128)S(1)} copy-done((s32[2,3,4,1152]{3,2,1,0:T(4,128)S(1)}, s32[2,3,4,1152]{3,2,1,0:T(4,128)}, u32[]{:S(2)}) %copy-start.3) | copy-done | bytes 110616
  3.5 7.2 %collective-permute-start = (f32[7,2,4,1152]{3,2,1,0:T(4,128)S(1)}, f32[7,2,4,1152]{3,2,1,0:T(4,128)S(1)}, u32[]{:S(2)}, u32[]{:S(2)}) collective-permute-start(f32[7,2,4,1152]{3,2,1,0:T(4,128)S(1)} %get-tuple-element.15), channel_id=1, source_target_pairs={{32,64},{64,32},{96,128},{128,96},{160,192},{192,160},{224,256},{2... | collective-permute-start | bytes 774152 | tf_op jit(solution)/shard_map/ppermute | solution.py:234
  10.7 1.9 %collective-permute-start.1 = (f32[7,2,4,1152]{3,2,1,0:T(4,128)S(1)}, f32[7,2,4,1152]{3,2,1,0:T(4,128)S(1)}, u32[]{:S(2)}, u32[]{:S(2)}) collective-permute-start(f32[7,2,4,1152]{3,2,1,0:T(4,128)S(1)} %get-tuple-element.16), channel_id=1, source_target_pairs={{0,32},{32,0},{64,96},{96,64},{128,160},{160,128},{192,224},{224,1... | collective-permute-start | bytes 774152 | tf_op jit(solution)/shard_map/ppermute | solution.py:235
  12.6 1.8 %shard_map.86.base_ref = f32[6,3,4,1152]{3,2,1,0:T(4,128)S(1)} custom-call(f32[6,3,4,1152]{3,2,1,0:T(4,128)S(1)} %copy-done, f32[2,3,4,1152]{3,2,1,0:T(4,128)S(1)} %copy-done.1, s32[2,3,4,1152]{3,2,1,0:T(4,128)S(1)} %copy-done.3), custom_call_target="tpu_custom_call" | custom-call | flops 1658880 | bytes 884736 | tf_op jit(solution)/shard_map/pallas_call | solution.py:211
  14.4 0.0 copy-start.2
  14.4 0.0 copy-start.4
  14.4 8.6 %collective-permute-done.slow_ref = f32[7,2,4,1152]{3,2,1,0:T(4,128)S(1)} collective-permute-done((f32[7,2,4,1152]{3,2,1,0:T(4,128)S(1)}, f32[7,2,4,1152]{3,2,1,0:T(4,128)S(1)}, u32[]{:S(2)}, u32[]{:S(2)}) %collective-permute-start) | collective-permute-done | bytes 258080 | tf_op jit(solution)/shard_map/ppermute | solution.py:234
  23.1 0.0 collective-permute-done.1.fast_ref
  23.1 0.2 shard_map.88
  23.3 7.3 %collective-permute-start.2 = (f32[6,2,4,1152]{3,2,1,0:T(4,128)S(1)}, f32[6,2,4,1152]{3,2,1,0:T(4,128)S(1)}, u32[]{:S(2)}, u32[]{:S(2)}) collective-permute-start(f32[6,2,4,1152]{3,2,1,0:T(4,128)S(1)} %get-tuple-element.18), channel_id=1, source_target_pairs={{32,64},{64,32},{96,128},{128,96},{160,192},{192,160},{224,256},{2... | collective-permute-start | bytes 663560 | tf_op jit(solution)/shard_map/ppermute | solution.py:257
  30.5 1.9 %collective-permute-start.3 = (f32[6,2,4,1152]{3,2,1,0:T(4,128)S(1)}, f32[6,2,4,1152]{3,2,1,0:T(4,128)S(1)}, u32[]{:S(2)}, u32[]{:S(2)}) collective-permute-start(f32[6,2,4,1152]{3,2,1,0:T(4,128)S(1)} %get-tuple-element.19), channel_id=1, source_target_pairs={{0,32},{32,0},{64,96},{96,64},{128,160},{160,128},{192,224},{224,1... | collective-permute-start | bytes 663560 | tf_op jit(solution)/shard_map/ppermute | solution.py:258
  32.5 0.0 copy-done.2
  32.5 0.0 copy-done.4
  32.5 0.0 copy-start.7
  32.5 0.0 copy-start.8
  32.5 1.8 %shard_map.89.base_ref = f32[6,3,4,1152]{3,2,1,0:T(4,128)S(1)} custom-call(f32[6,3,4,1152]{3,2,1,0:T(4,128)S(1)} %get-tuple-element.17.q_ref, f32[2,3,4,1152]{3,2,1,0:T(4,128)S(1)} %copy-done.2, s32[2,3,4,1152]{3,2,1,0:T(4,128)S(1)} %copy-done.4), custom_call_target="tpu_custom_call" | custom-call | flops 1658880 | bytes 884736 | tf_op jit(solution)/shard_map/pallas_call | solution.py:211
  34.3 4.6 %collective-permute-done.2.slow_ref = f32[6,2,4,1152]{3,2,1,0:T(4,128)S(1)} collective-permute-done((f32[6,2,4,1152]{3,2,1,0:T(4,128)S(1)}, f32[6,2,4,1152]{3,2,1,0:T(4,128)S(1)}, u32[]{:S(2)}, u32[]{:S(2)}) %collective-permute-start.2) | collective-permute-done | bytes 221216 | tf_op jit(solution)/shard_map/ppermute | solution.py:257
  38.9 0.0 collective-permute-done.3.fast_ref
  38.9 0.0 copy-done.7
  38.9 0.0 copy-done.8
  38.9 0.7 shard_map.90
  39.6 0.0 copy-start.5
  39.6 0.0 copy-start.6
  39.6 3.4 %all-to-all-start.1 = ((f32[4,3,1152]{2,1,0:T(4,128)}), f32[4,3,1152]{2,1,0:T(4,128)S(1)}, u32[]{:S(2)}, u32[]{:S(2)}) async-start(f32[4,3,1152]{2,1,0:T(4,128)} %get-tuple-element.25), calls=%async_computation.1 | async-start | bytes 147456 | tf_op jit(solution)/shard_map/all_to_all | solution.py:241
  43.1 0.0 copy-done.5
  43.1 0.0 copy-done.6
  43.1 0.8 shard_map.91
  43.9 3.4 %all-to-all-done.1.sums_ref = f32[4,3,1152]{2,1,0:T(4,128)S(1)} async-done(((f32[4,3,1152]{2,1,0:T(4,128)}), f32[4,3,1152]{2,1,0:T(4,128)S(1)}, u32[]{:S(2)}, u32[]{:S(2)}) %all-to-all-start.1) | async-done | bytes 55328 | tf_op jit(solution)/shard_map/all_to_all | solution.py:241
  47.2 7.5 %all-to-all-start = ((f32[32,4,256]{2,1,0:T(4,128)}), f32[32,4,256]{2,1,0:T(4,128)S(1)}, u32[]{:S(2)}, u32[]{:S(2)}) async-start(f32[32,4,256]{2,1,0:T(4,128)} %shard_map.91), calls=%async_computation | async-start | bytes 262144 | tf_op jit(solution)/shard_map/all_to_all | solution.py:251
  54.7 2.2 %collective-permute-start.4 = (f32[6,3,4,1152]{3,2,1,0:T(4,128)S(1)}, f32[6,3,4,1152]{3,2,1,0:T(4,128)S(1)}, u32[]{:S(2)}, u32[]{:S(2)}) collective-permute-start(f32[6,3,4,1152]{3,2,1,0:T(4,128)S(1)} %get-tuple-element.21.q_ref), channel_id=1, source_target_pairs={{0,1},{1,0},{2,3},{3,2},{4,5},{5,4},{6,7},{7,6},{8,9},{9,8},{10,11... | collective-permute-start | bytes 995336 | tf_op jit(solution)/shard_map/ppermute | solution.py:268
  56.9 0.7 collective-permute-start.5
  57.6 0.7 shard_map.94
  58.3 5.9 %all-to-all-done.in_ref = f32[32,4,256]{2,1,0:T(4,128)S(1)} async-done(((f32[32,4,256]{2,1,0:T(4,128)}), f32[32,4,256]{2,1,0:T(4,128)S(1)}, u32[]{:S(2)}, u32[]{:S(2)}) %all-to-all-start) | async-done | bytes 131104 | tf_op jit(solution)/shard_map/all_to_all | solution.py:251
  64.1 3.6 %all-to-all-start.2 = ((f32[8,3,1152]{2,1,0:T(4,128)}), f32[8,3,1152]{2,1,0:T(4,128)S(1)}, u32[]{:S(2)}, u32[]{:S(2)}) async-start(f32[8,3,1152]{2,1,0:T(4,128)} %get-tuple-element.27), calls=%async_computation.2 | async-start | bytes 294912 | tf_op jit(solution)/shard_map/all_to_all | solution.py:241
  67.8 0.3 shard_map.92
  68.0 9.4 %all-to-all-done.2.sums_ref = f32[8,3,1152]{2,1,0:T(4,128)S(1)} async-done(((f32[8,3,1152]{2,1,0:T(4,128)}), f32[8,3,1152]{2,1,0:T(4,128)S(1)}, u32[]{:S(2)}, u32[]{:S(2)}) %all-to-all-start.2) | async-done | bytes 110624 | tf_op jit(solution)/shard_map/all_to_all | solution.py:241
  77.5 0.7 shard_map.95
  78.1 0.0 collective-permute-done.4.chip_ref
  78.1 0.0 collective-permute-done.5.other_ref
  78.1 1.6 %shard_map.93 = f32[6,3,4,1152]{3,2,1,0:T(4,128)} custom-call(f32[6,3,4,1152]{3,2,1,0:T(4,128)S(1)} %get-tuple-element.21.q_ref, f32[6,3,4,1152]{3,2,1,0:T(4,128)S(1)} %collective-permute-done.4.chip_ref, f32[6,3,4,1152]{3,2,1,0:T(4,128)S(1)} %collective-permute-done.5.other_ref, f32[3,4,1152]{2,1,0:T(4,128)S(1)} %get-tuple-element.22.delta_ref, ...), custom_call_target="tpu_custom_call" | custom-call | flops 3317760 | bytes 1437696 | tf_op jit(solution)/shard_map/pallas_call | solution.py:211
  (1 shorter events, 0.0 us)
Async XLA Ops:
  0.6 1.0 %copy-start = (f32[6,3,4,1152]{3,2,1,0:T(4,128)S(1)}, f32[6,3,4,1152]{3,2,1,0:T(4,128)}, u32[]{:S(2)}) copy-start(f32[6,3,4,1152]{3,2,1,0:T(4,128)} %q_ref.5) | copy-start | bytes 995332
  1.6 0.9 %copy-start.1 = (f32[2,3,4,1152]{3,2,1,0:T(4,128)S(1)}, f32[2,3,4,1152]{3,2,1,0:T(4,128)}, u32[]{:S(2)}) copy-start(f32[2,3,4,1152]{3,2,1,0:T(4,128)} %courant_ref.9) | copy-start | bytes 331780
  2.5 0.9 %copy-start.3 = (s32[2,3,4,1152]{3,2,1,0:T(4,128)S(1)}, s32[2,3,4,1152]{3,2,1,0:T(4,128)}, u32[]{:S(2)}) copy-start(s32[2,3,4,1152]{3,2,1,0:T(4,128)} %offsets_ref.9) | copy-start | bytes 331780
  3.5 19.6 %collective-permute-start = (f32[7,2,4,1152]{3,2,1,0:T(4,128)S(1)}, f32[7,2,4,1152]{3,2,1,0:T(4,128)S(1)}, u32[]{:S(2)}, u32[]{:S(2)}) collective-permute-start(f32[7,2,4,1152]{3,2,1,0:T(4,128)S(1)} %get-tuple-element.15), channel_id=1, source_target_pairs={{32,64},{64,32},{96,128},{128,96},{160,192},{192,160},{224,256},{2... | collective-permute-start | bytes 774152 | tf_op jit(solution)/shard_map/ppermute | solution.py:234
  10.7 12.4 %collective-permute-start.1 = (f32[7,2,4,1152]{3,2,1,0:T(4,128)S(1)}, f32[7,2,4,1152]{3,2,1,0:T(4,128)S(1)}, u32[]{:S(2)}, u32[]{:S(2)}) collective-permute-start(f32[7,2,4,1152]{3,2,1,0:T(4,128)S(1)} %get-tuple-element.16), channel_id=1, source_target_pairs={{0,32},{32,0},{64,96},{96,64},{128,160},{160,128},{192,224},{224,1... | collective-permute-start | bytes 774152 | tf_op jit(solution)/shard_map/ppermute | solution.py:235
  14.4 18.1 %copy-start.2 = (f32[2,3,4,1152]{3,2,1,0:T(4,128)S(1)}, f32[2,3,4,1152]{3,2,1,0:T(4,128)}, u32[]{:S(2)}) copy-start(f32[2,3,4,1152]{3,2,1,0:T(4,128)} %courant_ref.9) | copy-start | bytes 331780
  14.4 18.1 %copy-start.4 = (s32[2,3,4,1152]{3,2,1,0:T(4,128)S(1)}, s32[2,3,4,1152]{3,2,1,0:T(4,128)}, u32[]{:S(2)}) copy-start(s32[2,3,4,1152]{3,2,1,0:T(4,128)} %offsets_ref.9) | copy-start | bytes 331780
  23.3 15.6 %collective-permute-start.2 = (f32[6,2,4,1152]{3,2,1,0:T(4,128)S(1)}, f32[6,2,4,1152]{3,2,1,0:T(4,128)S(1)}, u32[]{:S(2)}, u32[]{:S(2)}) collective-permute-start(f32[6,2,4,1152]{3,2,1,0:T(4,128)S(1)} %get-tuple-element.18), channel_id=1, source_target_pairs={{32,64},{64,32},{96,128},{128,96},{160,192},{192,160},{224,256},{2... | collective-permute-start | bytes 663560 | tf_op jit(solution)/shard_map/ppermute | solution.py:257
  30.5 8.4 %collective-permute-start.3 = (f32[6,2,4,1152]{3,2,1,0:T(4,128)S(1)}, f32[6,2,4,1152]{3,2,1,0:T(4,128)S(1)}, u32[]{:S(2)}, u32[]{:S(2)}) collective-permute-start(f32[6,2,4,1152]{3,2,1,0:T(4,128)S(1)} %get-tuple-element.19), channel_id=1, source_target_pairs={{0,32},{32,0},{64,96},{96,64},{128,160},{160,128},{192,224},{224,1... | collective-permute-start | bytes 663560 | tf_op jit(solution)/shard_map/ppermute | solution.py:258
  32.5 6.4 %copy-start.7 = (f32[3,4,1152]{2,1,0:T(4,128)S(1)}, f32[3,4,1152]{2,1,0:T(4,128)}, u32[]{:S(2)}) copy-start(f32[3,4,1152]{2,1,0:T(4,128)} %thickness_ref.1) | copy-start | bytes 165892
  32.5 6.4 %copy-start.8 = (f32[3,1152]{1,0:T(4,128)S(1)}, f32[3,1152]{1,0:T(4,128)}, u32[]{:S(2)}) copy-start(f32[3,1152]{1,0:T(4,128)} %surface_ref.1) | copy-start | bytes 41476
  39.6 3.4 %copy-start.5 = (s32[3,128,36]{1,2,0:T(8,128)S(1)}, s32[3,128,36]{1,2,0:T(8,128)}, u32[]{:S(2)}) copy-start(s32[3,128,36]{1,2,0:T(8,128)} %param.12) | copy-start | bytes 165892
  39.6 3.4 %copy-start.6 = (f32[3,128,36]{1,2,0:T(8,128)S(1)}, f32[3,128,36]{1,2,0:T(8,128)}, u32[]{:S(2)}) copy-start(f32[3,128,36]{1,2,0:T(8,128)} %param.13) | copy-start | bytes 165892
  39.6 7.6 %all-to-all-start.1 = ((f32[4,3,1152]{2,1,0:T(4,128)}), f32[4,3,1152]{2,1,0:T(4,128)S(1)}, u32[]{:S(2)}, u32[]{:S(2)}) async-start(f32[4,3,1152]{2,1,0:T(4,128)} %get-tuple-element.25), calls=%async_computation.1 | async-start | bytes 147456 | tf_op jit(solution)/shard_map/all_to_all | solution.py:241
  47.2 16.9 %all-to-all-start = ((f32[32,4,256]{2,1,0:T(4,128)}), f32[32,4,256]{2,1,0:T(4,128)S(1)}, u32[]{:S(2)}, u32[]{:S(2)}) async-start(f32[32,4,256]{2,1,0:T(4,128)} %shard_map.91), calls=%async_computation | async-start | bytes 262144 | tf_op jit(solution)/shard_map/all_to_all | solution.py:251
  54.7 23.4 %collective-permute-start.4 = (f32[6,3,4,1152]{3,2,1,0:T(4,128)S(1)}, f32[6,3,4,1152]{3,2,1,0:T(4,128)S(1)}, u32[]{:S(2)}, u32[]{:S(2)}) collective-permute-start(f32[6,3,4,1152]{3,2,1,0:T(4,128)S(1)} %get-tuple-element.21.q_ref), channel_id=1, source_target_pairs={{0,1},{1,0},{2,3},{3,2},{4,5},{5,4},{6,7},{7,6},{8,9},{9,8},{10,11... | collective-permute-start | bytes 995336 | tf_op jit(solution)/shard_map/ppermute | solution.py:268
  56.9 21.2 %collective-permute-start.5 = (f32[6,3,4,1152]{3,2,1,0:T(4,128)S(1)}, f32[6,3,4,1152]{3,2,1,0:T(4,128)S(1)}, u32[]{:S(2)}, u32[]{:S(2)}) collective-permute-start(f32[6,3,4,1152]{3,2,1,0:T(4,128)S(1)} %get-tuple-element.21.q_ref), channel_id=1, source_target_pairs={{1,2},{2,1},{3,4},{4,3},{5,6},{6,5},{7,8},{8,7},{9,10},{10,9},{11,... | collective-permute-start | bytes 995336 | tf_op jit(solution)/shard_map/ppermute | solution.py:269
  64.1 13.3 %all-to-all-start.2 = ((f32[8,3,1152]{2,1,0:T(4,128)}), f32[8,3,1152]{2,1,0:T(4,128)S(1)}, u32[]{:S(2)}, u32[]{:S(2)}) async-start(f32[8,3,1152]{2,1,0:T(4,128)} %get-tuple-element.27), calls=%async_computation.2 | async-start | bytes 294912 | tf_op jit(solution)/shard_map/all_to_all | solution.py:241

commit v3 on v2

--- a/solution.py
+++ b/solution.py
@@ -65,13 +65,29 @@
         fast_ref[f, k] = jnp.where(even, up, down)
 
 
-def edges_kernel(q_ref, courant_ref, offsets_ref, slow_ref, fast_ref):
+def edges_kernel(q_ref, courant_ref, offsets_ref, slow_ref, fast_ref, held, sems):
     count, rows = q_ref.shape[:2]
-    for f in range(count):
-        send(f, [q_ref[f, row] for row in range(rows)], slow_ref, fast_ref)
-    for k, value in enumerate((courant_ref[0, rows - 1], offsets_ref[0, rows - 1].astype(jnp.float32))):
-        slow_ref[count, k] = value
-        fast_ref[count, k] = value
+    even = is_even()
+    up, down = rows - 2, 0
+    copies = [
+        pltpu.make_async_copy(
+            q_ref.at[:, pl.ds(jnp.where(even, down, up), 2)], slow_ref.at[0:count], sems.at[0]
+        ),
+        pltpu.make_async_copy(
+            q_ref.at[:, pl.ds(jnp.where(even, up, down), 2)], fast_ref.at[0:count], sems.at[1]
+        ),
+        pltpu.make_async_copy(courant_ref.at[0, rows - 1], slow_ref.at[count, 0], sems.at[2]),
+        pltpu.make_async_copy(courant_ref.at[0, rows - 1], fast_ref.at[count, 0], sems.at[3]),
+        pltpu.make_async_copy(offsets_ref.at[0, rows - 1], held, sems.at[4]),
+    ]
+    for copy in copies:
+        copy.start()
+    copies[4].wait()
+    offset = held[...].astype(jnp.float32)
+    slow_ref[count, 1] = offset
+    fast_ref[count, 1] = offset
+    for copy in copies[:4]:
+        copy.wait()
 
 
 def first_kernel(
@@ -182,26 +198,23 @@
             weight_ref[row, :, to : to + width] = in_ref[k, :, start : start + width]
 
 
-def group_kernel(sums_ref, own_ref, out_ref):
-    near = sums_ref.shape[0]
-    me = lax.rem(lax.axis_index("lev"), near)
-    own = jnp.zeros(sums_ref.shape[1:], jnp.float32)
-    total = own
+def group_kernel(sums_ref, out_ref):
+    near = out_ref.shape[0]
+    me = lax.axis_index("lev")
+    group, place = me // near, lax.rem(me, near)
+    deeper = jnp.zeros(sums_ref.shape[1:], jnp.float32)
+    for k in range(sums_ref.shape[0]):
+        deeper = deeper + jnp.where(k > group, sums_ref[k], 0.0)
+    own = sums_ref[group]
     for k in range(near):
-        own = own + jnp.where(k > me, sums_ref[k], 0.0)
+        out_ref[k] = deeper + jnp.where(place > k, own, 0.0)
+
+
+def close_kernel(part_ref, sums_ref, out_ref):
+    total = sums_ref[0]
+    for k in range(1, sums_ref.shape[0]):
         total = total + sums_ref[k]
-    own_ref[...] = own
-    for k in range(out_ref.shape[0]):
-        out_ref[k] = total
-
-
-def close_kernel(part_ref, own_ref, sums_ref, out_ref):
-    rows = part_ref.shape[0]
-    me = lax.axis_index("lev") // NEAR
-    total = own_ref[...]
-    for k in range(sums_ref.shape[0]):
-        total = total + jnp.where(k > me, sums_ref[k], 0.0)
-    for row in range(rows):
+    for row in range(part_ref.shape[0]):
         out_ref[row] = part_ref[row] + total[row : row + 1]
 
 
@@ -228,9 +241,14 @@
 
     work = 20 * state.size
     edge = (count, 2, levels, width)
-    slow, fast = call(
-        edges_kernel, [(count + 1, *edge[1:])] * 2, 1, state, courant, offsets
-    )
+    slow, fast = pl.pallas_call(
+        edges_kernel,
+        out_shape=[jax.ShapeDtypeStruct((count + 1, *edge[1:]), jnp.float32)] * 2,
+        in_specs=[pl.BlockSpec(memory_space=pltpu.HBM)] * 3,
+        out_specs=[pl.BlockSpec(memory_space=pltpu.VMEM)] * 2,
+        scratch_shapes=[pltpu.VMEM((levels, width), jnp.int32), pltpu.SemaphoreType.DMA((5,))],
+        compiler_params=pltpu.CompilerParams(vmem_limit_bytes=16 << 20),
+    )(*(pltpu.with_memory_space_constraint(x, pltpu.HBM) for x in (state, courant, offsets)))
     slow = lax.ppermute(slow, "lat", swaps(lats, 1))
     fast = lax.ppermute(fast, "lat", swaps(lats, 0))
     far = groups // NEAR
@@ -260,18 +278,16 @@
     delta, weight = call(join_kernel, [log_thickness.shape] * 2, columns.size, columns)
     delta, weight = call(join_kernel, [log_thickness.shape] * 2, columns.size, columns)
     field, part, sums = call(
-        second_kernel, [state.shape, log_thickness.shape, (NEAR, rows, width)], work, base, field, slow, fast, face,
+        second_kernel, [state.shape, log_thickness.shape, (far, rows, width)], work, base, field, slow, fast, face,
         courant, offsets, log_thickness, surface,
     )
-    sums = exchange(sums, close)
-    own, sums = call(group_kernel, [(rows, width), (far, rows, width)], sums.size, sums)
+    sums = exchange(sums, distant)
+    (sums,) = call(group_kernel, [(NEAR, rows, width)], sums.size, sums)
     above = lax.ppermute(field, "lev", swaps(groups, 0))
     under = lax.ppermute(field, "lev", swaps(groups, 1))
-    sums = exchange(sums, distant)
-    (remapped,) = call(
-        remap_kernel, [state.shape], 2 * work, field, above, under, delta, weight
-    )
-    (geopotential,) = call(close_kernel, [log_thickness.shape], sums.size, part, own, sums)
+    sums = exchange(sums, close)
+    (remapped,) = call(remap_kernel, [state.shape], 2 * work, field, above, under, delta, weight)
+    (geopotential,) = call(close_kernel, [log_thickness.shape], sums.size, part, sums)
     return (remapped, geopotential)
 
 
@@ -287,4 +303,6 @@
     )
     out_specs = (P(None, "lat", "lev", None), P("lat", "lev", None))
 
-    return jax.shard_map(per_device, mesh=mesh, in_specs=in_specs, out_specs=out_specs, check_vma=False)
+    return jax.shard_map(
+        per_device, mesh=mesh, in_specs=in_specs, out_specs=out_specs, check_vma=False
+    )

time: 80.4 us -> 78.5 us (0.976)
  local copies, waits for them, and re-layouts: 2.79 us -> 0.03 us
  Pallas kernels: 8.53 us -> 9.65 us
    all_to_all x1, starting transfers between devices: 7.49 us -> 3.85 us  [per_device(): columns = lax.all_to_all(columns, 'lev', 0, 0, tiled=True)]
    all_to_all x2, starting transfers between devices: 7.06 us -> 10.5 us  [exchange(): return lax.all_to_all(x, 'lev', 0, 0, tiled=True, axis_index_groups=among)]
    unnamed x18 -> x14, local copies, waits for them, and re-layouts: 2.79 us -> 0.03 us
    pallas_call x0 -> x1, Pallas kernels: none -> 1.16 us  [per_device(): pl.pallas_call(edges_kernel, out_shape=[jax.ShapeDtypeStruct((count + 1,...]
    pallas_call x10 -> x9, Pallas kernels: 8.53 us -> 8.5 us  [call(): pl.pallas_call(kernel, out_shape=shapes, scratch_shapes=scratch, in_specs...]
  transfers between devices with their start and end apart: 9 -> 9, of which waited for: 5 -> 5; matrix products, arithmetic and copies ran while one was open for 0% -> 0% of each run, Pallas kernels for 7% -> 8%
where the time goes in v3:
time: 78.5 us; the launch traced here: 78 us
  starting transfers between devices  35.4 us (45%)
  waiting for transfers between devices  32.1 us (41%)
  Pallas kernels  9.65 us (12%)
  between operations  0.81 us (1%)
    ppermute x2, starting transfers between devices, per_device(): slow = lax.ppermute(slow, 'lat', swaps(lats, 1))  14.5 us
    ppermute x2, waiting for transfers between devices, per_device(): slow = lax.ppermute(slow, 'lat', swaps(lats, 1))  13.3 us
    all_to_all x2, waiting for transfers between devices, exchange(): return lax.all_to_all(x, 'lev', 0, 0, tiled=True, axis_index_groups=among)  12.7 us
    all_to_all x2, starting transfers between devices, exchange(): return lax.all_to_all(x, 'lev', 0, 0, tiled=True, axis_index_groups=among)  10.5 us
    pallas_call x9, Pallas kernels, call(): pl.pallas_call(kernel, out_shape=shapes, scratch_shapes=scratch, in_specs...  8.5 us
    all_to_all x1, waiting for transfers between devices, per_device(): columns = lax.all_to_all(columns, 'lev', 0, 0, tiled=True)  6.1 us
    all_to_all x1, starting transfers between devices, per_device(): columns = lax.all_to_all(columns, 'lev', 0, 0, tiled=True)  3.85 us
    ppermute x2, starting transfers between devices, per_device(): fast = lax.ppermute(fast, 'lat', swaps(lats, 0))  3.84 us
  transfers between devices with their start and end apart: 9, of which 5 were waited for; matrix products, arithmetic and copies ran while one was open for 0% of the time, Pallas kernels for 8%

profile of v3, /device:TPU:134, one launch (start us, length us, event | category | flops | bytes accessed | tf_op | source)
XLA Modules:
  0.0 78.0 jit_solution(13624551442490990301)
XLA Ops:
  0.6 0.0 copy-start
  0.6 0.0 copy-start.1
  0.6 0.0 copy-start.2
  0.7 1.2 %shard_map.87 = (f32[7,2,4,1152]{3,2,1,0:T(4,128)S(1)}, f32[7,2,4,1152]{3,2,1,0:T(4,128)S(1)}) custom-call(f32[6,3,4,1152]{3,2,1,0:T(4,128)} %q_ref.5, f32[2,3,4,1152]{3,2,1,0:T(4,128)} %courant_ref.9, s32[2,3,4,1152]{3,2,1,0:T(4,128)} %offsets_ref.9), custom_call_target="tpu_custom_call" | custom-call | tf_op jit(solution)/shard_map/pallas_call | solution.py:244
  1.8 7.2 %collective-permute-start = (f32[7,2,4,1152]{3,2,1,0:T(4,128)S(1)}, f32[7,2,4,1152]{3,2,1,0:T(4,128)S(1)}, u32[]{:S(2)}, u32[]{:S(2)}) collective-permute-start(f32[7,2,4,1152]{3,2,1,0:T(4,128)S(1)} %get-tuple-element.13), channel_id=1, source_target_pairs={{32,64},{64,32},{96,128},{128,96},{160,192},{192,160},{224,256},{2... | collective-permute-start | bytes 774152 | tf_op jit(solution)/shard_map/ppermute | solution.py:252
  9.0 1.9 %collective-permute-start.1 = (f32[7,2,4,1152]{3,2,1,0:T(4,128)S(1)}, f32[7,2,4,1152]{3,2,1,0:T(4,128)S(1)}, u32[]{:S(2)}, u32[]{:S(2)}) collective-permute-start(f32[7,2,4,1152]{3,2,1,0:T(4,128)S(1)} %get-tuple-element.14), channel_id=1, source_target_pairs={{0,32},{32,0},{64,96},{96,64},{128,160},{160,128},{192,224},{224,1... | collective-permute-start | bytes 774152 | tf_op jit(solution)/shard_map/ppermute | solution.py:253
  11.0 0.0 copy-done
  11.0 0.0 copy-done.1
  11.0 0.0 copy-done.2
  11.0 1.8 %shard_map.86.base_ref = f32[6,3,4,1152]{3,2,1,0:T(4,128)S(1)} custom-call(f32[6,3,4,1152]{3,2,1,0:T(4,128)S(1)} %copy-done, f32[2,3,4,1152]{3,2,1,0:T(4,128)S(1)} %copy-done.1, s32[2,3,4,1152]{3,2,1,0:T(4,128)S(1)} %copy-done.2), custom_call_target="tpu_custom_call" | custom-call | flops 1658880 | bytes 884736 | tf_op jit(solution)/shard_map/pallas_call | solution.py:224
  12.8 8.6 %collective-permute-done.slow_ref = f32[7,2,4,1152]{3,2,1,0:T(4,128)S(1)} collective-permute-done((f32[7,2,4,1152]{3,2,1,0:T(4,128)S(1)}, f32[7,2,4,1152]{3,2,1,0:T(4,128)S(1)}, u32[]{:S(2)}, u32[]{:S(2)}) %collective-permute-start) | collective-permute-done | bytes 258080 | tf_op jit(solution)/shard_map/ppermute | solution.py:252
  21.4 0.0 collective-permute-done.1.fast_ref
  21.4 0.2 shard_map.88
  21.6 7.3 %collective-permute-start.2 = (f32[6,2,4,1152]{3,2,1,0:T(4,128)S(1)}, f32[6,2,4,1152]{3,2,1,0:T(4,128)S(1)}, u32[]{:S(2)}, u32[]{:S(2)}) collective-permute-start(f32[6,2,4,1152]{3,2,1,0:T(4,128)S(1)} %get-tuple-element.16), channel_id=1, source_target_pairs={{32,64},{64,32},{96,128},{128,96},{160,192},{192,160},{224,256},{2... | collective-permute-start | bytes 663560 | tf_op jit(solution)/shard_map/ppermute | solution.py:275
  28.9 1.9 %collective-permute-start.3 = (f32[6,2,4,1152]{3,2,1,0:T(4,128)S(1)}, f32[6,2,4,1152]{3,2,1,0:T(4,128)S(1)}, u32[]{:S(2)}, u32[]{:S(2)}) collective-permute-start(f32[6,2,4,1152]{3,2,1,0:T(4,128)S(1)} %get-tuple-element.17), channel_id=1, source_target_pairs={{0,32},{32,0},{64,96},{96,64},{128,160},{160,128},{192,224},{224,1... | collective-permute-start | bytes 663560 | tf_op jit(solution)/shard_map/ppermute | solution.py:276
  30.8 0.0 copy-start.5
  30.8 0.0 copy-start.6
  30.9 1.8 %shard_map.89.base_ref = f32[6,3,4,1152]{3,2,1,0:T(4,128)S(1)} custom-call(f32[6,3,4,1152]{3,2,1,0:T(4,128)S(1)} %get-tuple-element.15.q_ref, f32[2,3,4,1152]{3,2,1,0:T(4,128)S(1)} %copy-done.1, s32[2,3,4,1152]{3,2,1,0:T(4,128)S(1)} %copy-done.2), custom_call_target="tpu_custom_call" | custom-call | flops 1658880 | bytes 884736 | tf_op jit(solution)/shard_map/pallas_call | solution.py:224
  32.6 4.6 %collective-permute-done.2.slow_ref = f32[6,2,4,1152]{3,2,1,0:T(4,128)S(1)} collective-permute-done((f32[6,2,4,1152]{3,2,1,0:T(4,128)S(1)}, f32[6,2,4,1152]{3,2,1,0:T(4,128)S(1)}, u32[]{:S(2)}, u32[]{:S(2)}) %collective-permute-start.2) | collective-permute-done | bytes 221216 | tf_op jit(solution)/shard_map/ppermute | solution.py:275
  37.3 0.0 collective-permute-done.3.fast_ref
  37.3 0.0 copy-done.5
  37.3 0.0 copy-done.6
  37.3 0.8 shard_map.90
  38.0 0.0 copy-start.3
  38.0 0.0 copy-start.4
  38.1 7.2 %all-to-all-start.1 = ((f32[8,3,1152]{2,1,0:T(4,128)}), f32[8,3,1152]{2,1,0:T(4,128)S(1)}, u32[]{:S(2)}, u32[]{:S(2)}) async-start(f32[8,3,1152]{2,1,0:T(4,128)} %get-tuple-element.23), calls=%async_computation.1 | async-start | bytes 294912 | tf_op jit(solution)/shard_map/all_to_all | solution.py:259
  45.3 0.0 copy-done.3
  45.3 0.0 copy-done.4
  45.3 0.8 shard_map.91
  46.1 8.8 %all-to-all-done.1.sums_ref = f32[8,3,1152]{2,1,0:T(4,128)S(1)} async-done(((f32[8,3,1152]{2,1,0:T(4,128)}), f32[8,3,1152]{2,1,0:T(4,128)S(1)}, u32[]{:S(2)}, u32[]{:S(2)}) %all-to-all-start.1) | async-done | bytes 110624 | tf_op jit(solution)/shard_map/all_to_all | solution.py:259
  54.9 3.9 %all-to-all-start = ((f32[32,4,256]{2,1,0:T(4,128)}), f32[32,4,256]{2,1,0:T(4,128)S(1)}, u32[]{:S(2)}, u32[]{:S(2)}) async-start(f32[32,4,256]{2,1,0:T(4,128)} %shard_map.91), calls=%async_computation | async-start | bytes 262144 | tf_op jit(solution)/shard_map/all_to_all | solution.py:269
  58.7 2.1 %collective-permute-start.4 = (f32[6,3,4,1152]{3,2,1,0:T(4,128)S(1)}, f32[6,3,4,1152]{3,2,1,0:T(4,128)S(1)}, u32[]{:S(2)}, u32[]{:S(2)}) collective-permute-start(f32[6,3,4,1152]{3,2,1,0:T(4,128)S(1)} %get-tuple-element.19.q_ref), channel_id=1, source_target_pairs={{0,1},{1,0},{2,3},{3,2},{4,5},{5,4},{6,7},{7,6},{8,9},{9,8},{10,11... | collective-permute-start | bytes 995336 | tf_op jit(solution)/shard_map/ppermute | solution.py:286
  60.8 0.7 collective-permute-start.5
  61.5 0.7 shard_map.94
  62.2 6.1 %all-to-all-done.in_ref = f32[32,4,256]{2,1,0:T(4,128)S(1)} async-done(((f32[32,4,256]{2,1,0:T(4,128)}), f32[32,4,256]{2,1,0:T(4,128)S(1)}, u32[]{:S(2)}, u32[]{:S(2)}) %all-to-all-start) | async-done | bytes 131104 | tf_op jit(solution)/shard_map/all_to_all | solution.py:269
  68.3 3.3 %all-to-all-start.2 = ((f32[4,3,1152]{2,1,0:T(4,128)}), f32[4,3,1152]{2,1,0:T(4,128)S(1)}, u32[]{:S(2)}, u32[]{:S(2)}) async-start(f32[4,3,1152]{2,1,0:T(4,128)} %shard_map.94), calls=%async_computation.2 | async-start | bytes 147456 | tf_op jit(solution)/shard_map/all_to_all | solution.py:259
  71.6 0.3 shard_map.92
  71.8 3.9 %all-to-all-done.2.sums_ref = f32[4,3,1152]{2,1,0:T(4,128)S(1)} async-done(((f32[4,3,1152]{2,1,0:T(4,128)}), f32[4,3,1152]{2,1,0:T(4,128)S(1)}, u32[]{:S(2)}, u32[]{:S(2)}) %all-to-all-start.2) | async-done | bytes 55328 | tf_op jit(solution)/shard_map/all_to_all | solution.py:259
  75.7 0.6 shard_map.95
  76.3 0.0 collective-permute-done.4.chip_ref
  76.4 0.0 collective-permute-done.5.other_ref
  76.4 1.6 %shard_map.93 = f32[6,3,4,1152]{3,2,1,0:T(4,128)} custom-call(f32[6,3,4,1152]{3,2,1,0:T(4,128)S(1)} %get-tuple-element.19.q_ref, f32[6,3,4,1152]{3,2,1,0:T(4,128)S(1)} %collective-permute-done.4.chip_ref, f32[6,3,4,1152]{3,2,1,0:T(4,128)S(1)} %collective-permute-done.5.other_ref, f32[3,4,1152]{2,1,0:T(4,128)S(1)} %get-tuple-element.20.delta_ref, ...), custom_call_target="tpu_custom_call" | custom-call | flops 3317760 | bytes 1437696 | tf_op jit(solution)/shard_map/pallas_call | solution.py:224
Async XLA Ops:
  0.6 10.3 %copy-start = (f32[6,3,4,1152]{3,2,1,0:T(4,128)S(1)}, f32[6,3,4,1152]{3,2,1,0:T(4,128)}, u32[]{:S(2)}) copy-start(f32[6,3,4,1152]{3,2,1,0:T(4,128)} %q_ref.5) | copy-start | bytes 995332
  0.6 10.3 %copy-start.1 = (f32[2,3,4,1152]{3,2,1,0:T(4,128)S(1)}, f32[2,3,4,1152]{3,2,1,0:T(4,128)}, u32[]{:S(2)}) copy-start(f32[2,3,4,1152]{3,2,1,0:T(4,128)} %courant_ref.9) | copy-start | bytes 331780
  0.6 10.3 %copy-start.2 = (s32[2,3,4,1152]{3,2,1,0:T(4,128)S(1)}, s32[2,3,4,1152]{3,2,1,0:T(4,128)}, u32[]{:S(2)}) copy-start(s32[2,3,4,1152]{3,2,1,0:T(4,128)} %offsets_ref.9) | copy-start | bytes 331780
  1.8 19.6 %collective-permute-start = (f32[7,2,4,1152]{3,2,1,0:T(4,128)S(1)}, f32[7,2,4,1152]{3,2,1,0:T(4,128)S(1)}, u32[]{:S(2)}, u32[]{:S(2)}) collective-permute-start(f32[7,2,4,1152]{3,2,1,0:T(4,128)S(1)} %get-tuple-element.13), channel_id=1, source_target_pairs={{32,64},{64,32},{96,128},{128,96},{160,192},{192,160},{224,256},{2... | collective-permute-start | bytes 774152 | tf_op jit(solution)/shard_map/ppermute | solution.py:252
  9.0 12.4 %collective-permute-start.1 = (f32[7,2,4,1152]{3,2,1,0:T(4,128)S(1)}, f32[7,2,4,1152]{3,2,1,0:T(4,128)S(1)}, u32[]{:S(2)}, u32[]{:S(2)}) collective-permute-start(f32[7,2,4,1152]{3,2,1,0:T(4,128)S(1)} %get-tuple-element.14), channel_id=1, source_target_pairs={{0,32},{32,0},{64,96},{96,64},{128,160},{160,128},{192,224},{224,1... | collective-permute-start | bytes 774152 | tf_op jit(solution)/shard_map/ppermute | solution.py:253
  21.6 15.6 %collective-permute-start.2 = (f32[6,2,4,1152]{3,2,1,0:T(4,128)S(1)}, f32[6,2,4,1152]{3,2,1,0:T(4,128)S(1)}, u32[]{:S(2)}, u32[]{:S(2)}) collective-permute-start(f32[6,2,4,1152]{3,2,1,0:T(4,128)S(1)} %get-tuple-element.16), channel_id=1, source_target_pairs={{32,64},{64,32},{96,128},{128,96},{160,192},{192,160},{224,256},{2... | collective-permute-start | bytes 663560 | tf_op jit(solution)/shard_map/ppermute | solution.py:275
  28.9 8.4 %collective-permute-start.3 = (f32[6,2,4,1152]{3,2,1,0:T(4,128)S(1)}, f32[6,2,4,1152]{3,2,1,0:T(4,128)S(1)}, u32[]{:S(2)}, u32[]{:S(2)}) collective-permute-start(f32[6,2,4,1152]{3,2,1,0:T(4,128)S(1)} %get-tuple-element.17), channel_id=1, source_target_pairs={{0,32},{32,0},{64,96},{96,64},{128,160},{160,128},{192,224},{224,1... | collective-permute-start | bytes 663560 | tf_op jit(solution)/shard_map/ppermute | solution.py:276
  30.8 6.4 %copy-start.5 = (f32[3,4,1152]{2,1,0:T(4,128)S(1)}, f32[3,4,1152]{2,1,0:T(4,128)}, u32[]{:S(2)}) copy-start(f32[3,4,1152]{2,1,0:T(4,128)} %thickness_ref.1) | copy-start | bytes 165892
  30.8 6.4 %copy-start.6 = (f32[3,1152]{1,0:T(4,128)S(1)}, f32[3,1152]{1,0:T(4,128)}, u32[]{:S(2)}) copy-start(f32[3,1152]{1,0:T(4,128)} %surface_ref.1) | copy-start | bytes 41476
  38.0 7.2 %copy-start.3 = (s32[3,128,36]{1,2,0:T(8,128)S(1)}, s32[3,128,36]{1,2,0:T(8,128)}, u32[]{:S(2)}) copy-start(s32[3,128,36]{1,2,0:T(8,128)} %param.12) | copy-start | bytes 165892
  38.0 7.2 %copy-start.4 = (f32[3,128,36]{1,2,0:T(8,128)S(1)}, f32[3,128,36]{1,2,0:T(8,128)}, u32[]{:S(2)}) copy-start(f32[3,128,36]{1,2,0:T(8,128)} %param.13) | copy-start | bytes 165892
  38.1 16.8 %all-to-all-start.1 = ((f32[8,3,1152]{2,1,0:T(4,128)}), f32[8,3,1152]{2,1,0:T(4,128)S(1)}, u32[]{:S(2)}, u32[]{:S(2)}) async-start(f32[8,3,1152]{2,1,0:T(4,128)} %get-tuple-element.23), calls=%async_computation.1 | async-start | bytes 294912 | tf_op jit(solution)/shard_map/all_to_all | solution.py:259
  54.9 13.4 %all-to-all-start = ((f32[32,4,256]{2,1,0:T(4,128)}), f32[32,4,256]{2,1,0:T(4,128)S(1)}, u32[]{:S(2)}, u32[]{:S(2)}) async-start(f32[32,4,256]{2,1,0:T(4,128)} %shard_map.91), calls=%async_computation | async-start | bytes 262144 | tf_op jit(solution)/shard_map/all_to_all | solution.py:269
  58.7 17.6 %collective-permute-start.4 = (f32[6,3,4,1152]{3,2,1,0:T(4,128)S(1)}, f32[6,3,4,1152]{3,2,1,0:T(4,128)S(1)}, u32[]{:S(2)}, u32[]{:S(2)}) collective-permute-start(f32[6,3,4,1152]{3,2,1,0:T(4,128)S(1)} %get-tuple-element.19.q_ref), channel_id=1, source_target_pairs={{0,1},{1,0},{2,3},{3,2},{4,5},{5,4},{6,7},{7,6},{8,9},{9,8},{10,11... | collective-permute-start | bytes 995336 | tf_op jit(solution)/shard_map/ppermute | solution.py:286
  60.8 15.5 %collective-permute-start.5 = (f32[6,3,4,1152]{3,2,1,0:T(4,128)S(1)}, f32[6,3,4,1152]{3,2,1,0:T(4,128)S(1)}, u32[]{:S(2)}, u32[]{:S(2)}) collective-permute-start(f32[6,3,4,1152]{3,2,1,0:T(4,128)S(1)} %get-tuple-element.19.q_ref), channel_id=1, source_target_pairs={{1,2},{2,1},{3,4},{4,3},{5,6},{6,5},{7,8},{8,7},{9,10},{10,9},{11,... | collective-permute-start | bytes 995336 | tf_op jit(solution)/shard_map/ppermute | solution.py:287
  68.3 7.4 %all-to-all-start.2 = ((f32[4,3,1152]{2,1,0:T(4,128)}), f32[4,3,1152]{2,1,0:T(4,128)S(1)}, u32[]{:S(2)}, u32[]{:S(2)}) async-start(f32[4,3,1152]{2,1,0:T(4,128)} %shard_map.94), calls=%async_computation.2 | async-start | bytes 147456 | tf_op jit(solution)/shard_map/all_to_all | solution.py:259

commit v4 on v3

--- a/solution.py
+++ b/solution.py
@@ -18,12 +18,12 @@
 
 
 def east_kernel(q_ref, courant_ref, offsets_ref, base_ref):
-    count, rows, _, width = q_ref.shape
-    for row in range(rows):
-        offset = offsets_ref[1, row]
-        weight = courant_ref[1, row]
-        for f in range(count):
-            q = q_ref[f, row]
+    count, rows, levels, width = q_ref.shape
+    for row in range(rows):
+        offset = jnp.concatenate([offsets_ref[1, row]] * 2, axis=0)
+        weight = jnp.concatenate([courant_ref[1, row]] * 2, axis=0)
+        for f in range(0, count, 2):
+            q = jnp.concatenate([q_ref[f, row], q_ref[f + 1, row]], axis=0)
             moved = pick(
                 offset,
                 pltpu.roll(q, 1, 1),
@@ -32,19 +32,22 @@
                 pltpu.roll(q, width - 2, 1),
             )
             east = weight * moved
-            base_ref[f, row] = q - (east - pltpu.roll(east, 1, 1))
+            base = q - (east - pltpu.roll(east, 1, 1))
+            base_ref[f, row] = base[:levels]
+            base_ref[f + 1, row] = base[levels:]
 
 
 def is_even():
     return lax.rem(lax.axis_index("lat"), 2) == 0
 
 
-def advected(f, base_ref, q_ref, slow_ref, fast_ref, face, courant_ref, offsets_ref):
+def advected(f, base_ref, q_ref, slow_ref, fast_ref, face, courant_ref, offsets_ref, g=None):
+    g = f if g is None else g
     rows = q_ref.shape[1]
     even = is_even()
     low, high = [], []
     for k in range(2):
-        slow, fast = slow_ref[f, k], fast_ref[f, k]
+        slow, fast = slow_ref[g, k], fast_ref[f, k]
         low.append(jnp.where(even, slow, fast))
         high.append(jnp.where(even, fast, slow))
     around = low + [q_ref[f, row] for row in range(rows)] + high
@@ -57,11 +60,12 @@
     return result
 
 
-def send(f, new, slow_ref, fast_ref):
+def send(f, new, slow_ref, fast_ref, g=None):
+    g = f if g is None else g
     even = is_even()
     for k in range(2):
         up, down = new[len(new) - 2 + k], new[k]
-        slow_ref[f, k] = jnp.where(even, down, up)
+        slow_ref[g, k] = jnp.where(even, down, up)
         fast_ref[f, k] = jnp.where(even, up, down)
 
 
@@ -91,7 +95,8 @@
 
 
 def first_kernel(
-    base_ref, q_ref, slow_ref, fast_ref, courant_ref, offsets_ref, out_ref, face_ref, next_slow_ref, next_fast_ref
+    base_ref, q_ref, slow_ref, fast_ref, courant_ref, offsets_ref, out_ref, face_ref, slow0_ref, next_slow_ref,
+    next_fast_ref,
 ):
     count, rows = q_ref.shape[:2]
     face = [jnp.where(is_even(), slow_ref[count, k], fast_ref[count, k]) for k in range(2)]
@@ -102,38 +107,51 @@
         new = advected(f, base_ref, q_ref, slow_ref, fast_ref, face, courant_ref, offsets_ref)
         for row in range(rows):
             out_ref[f, row] = new[row]
-        send(f, new, next_slow_ref, next_fast_ref)
+        if f == 0:
+            send(0, new, slow0_ref, next_fast_ref)
+        else:
+            send(f, new, next_slow_ref, next_fast_ref, f - 1)
 
 
 def heat(new, thickness_ref, surface_ref, part_ref, sums_ref):
     sums = []
     for row, value in enumerate(new):
-        levels, width = value.shape
+        levels = value.shape[0]
         heating = value * thickness_ref[row]
-        below = jnp.zeros((1, width), jnp.float32)
-        deeper = []
-        for k in range(levels - 1, -1, -1):
-            deeper.insert(0, below)
-            below = below + heating[k : k + 1]
-        part_ref[row] = jnp.concatenate(deeper, axis=0) + 0.5 * heating + surface_ref[row : row + 1]
-        sums.append(below)
+        below = jnp.concatenate([heating, jnp.zeros_like(heating)], axis=0)
+        step = 1
+        while step < levels:
+            below = below + pltpu.roll(below, 2 * levels - step, 0)
+            step *= 2
+        part_ref[row] = below[:levels] - 0.5 * heating + surface_ref[row : row + 1]
+        sums.append(below[0:1])
     sums = jnp.concatenate(sums, axis=0)
     for k in range(sums_ref.shape[0]):
         sums_ref[k] = sums
 
 
-def second_kernel(
+def heat_kernel(
     base_ref, q_ref, slow_ref, fast_ref, face_ref, courant_ref, offsets_ref, thickness_ref, surface_ref,
     out_ref, part_ref, sums_ref,
 ):
+    face = face_ref[0], face_ref[1].astype(jnp.int32)
+    new = advected(0, base_ref, q_ref, slow_ref, fast_ref, face, courant_ref, offsets_ref)
+    for row, value in enumerate(new):
+        out_ref[row] = value
+    heat(new, thickness_ref, surface_ref, part_ref, sums_ref)
+
+
+def second_kernel(
+    base_ref, q_ref, slow_ref, fast_ref, face_ref, courant_ref, offsets_ref, done_ref, out_ref
+):
     count, rows = q_ref.shape[:2]
     face = face_ref[0], face_ref[1].astype(jnp.int32)
-    for f in range(count):
-        new = advected(f, base_ref, q_ref, slow_ref, fast_ref, face, courant_ref, offsets_ref)
+    for row in range(rows):
+        out_ref[0, row] = done_ref[row]
+    for f in range(1, count):
+        new = advected(f, base_ref, q_ref, slow_ref, fast_ref, face, courant_ref, offsets_ref, f - 1)
         for row in range(rows):
             out_ref[f, row] = new[row]
-        if f == 0:
-            heat(new, thickness_ref, surface_ref, part_ref, sums_ref)
 
 
 def remap_kernel(q_ref, chip_ref, other_ref, delta_ref, weight_ref, out_ref):
@@ -201,7 +219,7 @@
 def group_kernel(sums_ref, out_ref):
     near = out_ref.shape[0]
     me = lax.axis_index("lev")
-    group, place = me // near, lax.rem(me, near)
+    group, place = lax.div(me, near), lax.rem(me, near)
     deeper = jnp.zeros(sums_ref.shape[1:], jnp.float32)
     for k in range(sums_ref.shape[0]):
         deeper = deeper + jnp.where(k > group, sums_ref[k], 0.0)
@@ -269,17 +287,23 @@
     columns = lax.all_to_all(columns, "lev", 0, 0, tiled=True)
 
     (base,) = call(east_kernel, [state.shape], work, state, courant, offsets)
-    field, face, slow, fast = call(
-        first_kernel, [state.shape, (2, levels, width), edge, edge], work, base, state, slow, fast, courant, offsets
-    )
+    first, rest = (1, *edge[1:]), (count - 1, *edge[1:])
+    field, face, slow0, slow, fast = call(
+        first_kernel, [state.shape, (2, levels, width), first, rest, edge], work, base, state, slow, fast,
+        courant, offsets,
+    )
+    slow0 = lax.ppermute(slow0, "lat", swaps(lats, 1))
+    fast = lax.ppermute(fast, "lat", swaps(lats, 0))
     slow = lax.ppermute(slow, "lat", swaps(lats, 1))
-    fast = lax.ppermute(fast, "lat", swaps(lats, 0))
     (base,) = call(east_kernel, [state.shape], work, field, courant, offsets)
     delta, weight = call(join_kernel, [log_thickness.shape] * 2, columns.size, columns)
     delta, weight = call(join_kernel, [log_thickness.shape] * 2, columns.size, columns)
-    field, part, sums = call(
-        second_kernel, [state.shape, log_thickness.shape, (far, rows, width)], work, base, field, slow, fast, face,
-        courant, offsets, log_thickness, surface,
+    done, part, sums = call(
+        heat_kernel, [log_thickness.shape, log_thickness.shape, (far, rows, width)], work, base, field, slow0, fast,
+        face, courant, offsets, log_thickness, surface,
+    )
+    (field,) = call(
+        second_kernel, [state.shape], work, base, field, slow, fast, face, courant, offsets, done
     )
     sums = exchange(sums, distant)
     (sums,) = call(group_kernel, [(NEAR, rows, width)], sums.size, sums)

time: 78.5 us -> 77 us (0.981)
  starting transfers between devices: 35.4 us -> 45.3 us
  waiting for transfers between devices: 32.1 us -> 22.3 us
  Pallas kernels: 9.65 us -> 7.92 us
    all_to_all x2, waiting for transfers between devices: 12.7 us -> 5.08 us  [exchange(): return lax.all_to_all(x, 'lev', 0, 0, tiled=True, axis_index_groups=among)]
    ppermute x0 -> x1, starting transfers between devices: none -> 7.26 us  [per_device(): slow0 = lax.ppermute(slow0, 'lat', swaps(lats, 1))]
    ppermute x2, waiting for transfers between devices: 13.3 us -> 9.57 us  [per_device(): slow = lax.ppermute(slow, 'lat', swaps(lats, 1))]
    all_to_all x1, starting transfers between devices: 3.85 us -> 6.38 us  [per_device(): columns = lax.all_to_all(columns, 'lev', 0, 0, tiled=True)]
    ppermute x0 -> x1, waiting for transfers between devices: none -> 1.93 us  [per_device(): slow0 = lax.ppermute(slow0, 'lat', swaps(lats, 1))]
    pallas_call x9 -> x10, Pallas kernels: 8.5 us -> 6.76 us  [call(): pl.pallas_call(kernel, out_shape=shapes, scratch_shapes=scratch, in_specs...]
  transfers between devices with their start and end apart: 9 -> 10, of which waited for: 5 -> 5; matrix products, arithmetic and copies ran while one was open for 0% -> 0% of each run, Pallas kernels for 8% -> 5%
where the time goes in v4:
time: 77 us; the launch traced here: 76.4 us
  starting transfers between devices  45.3 us (59%)
  waiting for transfers between devices  22.3 us (29%)
  Pallas kernels  7.92 us (10%)
  between operations  0.84 us (1%)
    ppermute x2, starting transfers between devices, per_device(): slow = lax.ppermute(slow, 'lat', swaps(lats, 1))  14.5 us
    all_to_all x2, starting transfers between devices, exchange(): return lax.all_to_all(x, 'lev', 0, 0, tiled=True, axis_index_groups=among)  10.5 us
    ppermute x2, waiting for transfers between devices, per_device(): slow = lax.ppermute(slow, 'lat', swaps(lats, 1))  9.57 us
    ppermute x1, starting transfers between devices, per_device(): slow0 = lax.ppermute(slow0, 'lat', swaps(lats, 1))  7.26 us
    pallas_call x10, Pallas kernels, call(): pl.pallas_call(kernel, out_shape=shapes, scratch_shapes=scratch, in_specs...  6.76 us
    all_to_all x1, starting transfers between devices, per_device(): columns = lax.all_to_all(columns, 'lev', 0, 0, tiled=True)  6.38 us
    all_to_all x1, waiting for transfers between devices, per_device(): columns = lax.all_to_all(columns, 'lev', 0, 0, tiled=True)  5.71 us
    all_to_all x2, waiting for transfers between devices, exchange(): return lax.all_to_all(x, 'lev', 0, 0, tiled=True, axis_index_groups=among)  5.08 us
  transfers between devices with their start and end apart: 10, of which 5 were waited for; matrix products, arithmetic and copies ran while one was open for 0% of the time, Pallas kernels for 5%

profile of v4, /device:TPU:134, one launch (start us, length us, event | category | flops | bytes accessed | tf_op | source)
XLA Modules:
  0.0 76.4 jit_solution(9958455250762217887)
XLA Ops:
  0.6 0.0 copy-start.2
  0.6 0.0 copy-start
  0.6 0.0 copy-start.1
  0.7 1.2 %shard_map.87 = (f32[7,2,4,1152]{3,2,1,0:T(4,128)S(1)}, f32[7,2,4,1152]{3,2,1,0:T(4,128)S(1)}) custom-call(f32[6,3,4,1152]{3,2,1,0:T(4,128)} %q_ref.5, f32[2,3,4,1152]{3,2,1,0:T(4,128)} %courant_ref.11, s32[2,3,4,1152]{3,2,1,0:T(4,128)} %offsets_ref.11), custom_call_target="tpu_custom_call" | custom-call | tf_op jit(solution)/shard_map/pallas_call | solution.py:262
  1.8 7.2 %collective-permute-start = (f32[7,2,4,1152]{3,2,1,0:T(4,128)S(1)}, f32[7,2,4,1152]{3,2,1,0:T(4,128)S(1)}, u32[]{:S(2)}, u32[]{:S(2)}) collective-permute-start(f32[7,2,4,1152]{3,2,1,0:T(4,128)S(1)} %get-tuple-element.14), channel_id=1, source_target_pairs={{32,64},{64,32},{96,128},{128,96},{160,192},{192,160},{224,256},{2... | collective-permute-start | bytes 774152 | tf_op jit(solution)/shard_map/ppermute | solution.py:270
  9.0 1.9 %collective-permute-start.1 = (f32[7,2,4,1152]{3,2,1,0:T(4,128)S(1)}, f32[7,2,4,1152]{3,2,1,0:T(4,128)S(1)}, u32[]{:S(2)}, u32[]{:S(2)}) collective-permute-start(f32[7,2,4,1152]{3,2,1,0:T(4,128)S(1)} %get-tuple-element.15), channel_id=1, source_target_pairs={{0,32},{32,0},{64,96},{96,64},{128,160},{160,128},{192,224},{224,1... | collective-permute-start | bytes 774152 | tf_op jit(solution)/shard_map/ppermute | solution.py:271
  11.0 0.0 copy-done.2
  11.0 0.0 copy-done
  11.0 0.0 copy-done.1
  11.0 0.8 %shard_map.86.base_ref = f32[6,3,4,1152]{3,2,1,0:T(4,128)S(1)} custom-call(f32[6,3,4,1152]{3,2,1,0:T(4,128)S(1)} %copy-done.2, f32[2,3,4,1152]{3,2,1,0:T(4,128)S(1)} %copy-done, s32[2,3,4,1152]{3,2,1,0:T(4,128)S(1)} %copy-done.1), custom_call_target="tpu_custom_call" | custom-call | flops 1658880 | bytes 884736 | tf_op jit(solution)/shard_map/pallas_call | solution.py:242
  11.9 9.6 %collective-permute-done.slow_ref = f32[7,2,4,1152]{3,2,1,0:T(4,128)S(1)} collective-permute-done((f32[7,2,4,1152]{3,2,1,0:T(4,128)S(1)}, f32[7,2,4,1152]{3,2,1,0:T(4,128)S(1)}, u32[]{:S(2)}, u32[]{:S(2)}) %collective-permute-start) | collective-permute-done | bytes 258080 | tf_op jit(solution)/shard_map/ppermute | solution.py:270
  21.4 0.0 collective-permute-done.1.fast_ref
  21.4 0.2 shard_map.88
  21.6 1.9 %collective-permute-start.3 = (f32[6,2,4,1152]{3,2,1,0:T(4,128)S(1)}, f32[6,2,4,1152]{3,2,1,0:T(4,128)S(1)}, u32[]{:S(2)}, u32[]{:S(2)}) collective-permute-start(f32[6,2,4,1152]{3,2,1,0:T(4,128)S(1)} %get-tuple-element.18), channel_id=1, source_target_pairs={{0,32},{32,0},{64,96},{96,64},{128,160},{160,128},{192,224},{224,1... | collective-permute-start | bytes 663560 | tf_op jit(solution)/shard_map/ppermute | solution.py:296
  23.6 7.3 %collective-permute-start.4 = (f32[1,2,4,1152]{3,2,1,0:T(4,128)S(1)}, f32[1,2,4,1152]{3,2,1,0:T(4,128)S(1)}, u32[]{:S(2)}, u32[]{:S(2)}) collective-permute-start(f32[1,2,4,1152]{3,2,1,0:T(4,128)S(1)} %get-tuple-element.20), channel_id=1, source_target_pairs={{32,64},{64,32},{96,128},{128,96},{160,192},{192,160},{224,256},{2... | collective-permute-start | bytes 110600 | tf_op jit(solution)/shard_map/ppermute | solution.py:295
  30.8 0.0 copy-start.5
  30.8 0.0 copy-start.6
  30.9 0.8 %shard_map.89.base_ref = f32[6,3,4,1152]{3,2,1,0:T(4,128)S(1)} custom-call(f32[6,3,4,1152]{3,2,1,0:T(4,128)S(1)} %get-tuple-element.16.q_ref, f32[2,3,4,1152]{3,2,1,0:T(4,128)S(1)} %copy-done, s32[2,3,4,1152]{3,2,1,0:T(4,128)S(1)} %copy-done.1), custom_call_target="tpu_custom_call" | custom-call | flops 1658880 | bytes 884736 | tf_op jit(solution)/shard_map/pallas_call | solution.py:242
  31.7 1.9 %collective-permute-done.4.slow_ref = f32[1,2,4,1152]{3,2,1,0:T(4,128)S(1)} collective-permute-done((f32[1,2,4,1152]{3,2,1,0:T(4,128)S(1)}, f32[1,2,4,1152]{3,2,1,0:T(4,128)S(1)}, u32[]{:S(2)}, u32[]{:S(2)}) %collective-permute-start.4) | collective-permute-done | bytes 36896 | tf_op jit(solution)/shard_map/ppermute | solution.py:295
  33.6 0.0 collective-permute-done.3.fast_ref
  33.6 0.0 copy-done.5
  33.6 0.0 copy-done.6
  33.7 0.7 shard_map.90
  34.4 0.0 copy-start.3
  34.4 0.0 copy-start.4
  34.4 7.2 %all-to-all-start.1 = ((f32[8,3,1152]{2,1,0:T(4,128)}), f32[8,3,1152]{2,1,0:T(4,128)S(1)}, u32[]{:S(2)}, u32[]{:S(2)}) async-start(f32[8,3,1152]{2,1,0:T(4,128)} %get-tuple-element.25), calls=%async_computation.1 | async-start | bytes 294912 | tf_op jit(solution)/shard_map/all_to_all | solution.py:277
  41.6 7.2 %collective-permute-start.2 = (f32[5,2,4,1152]{3,2,1,0:T(4,128)S(1)}, f32[5,2,4,1152]{3,2,1,0:T(4,128)S(1)}, u32[]{:S(2)}, u32[]{:S(2)}) collective-permute-start(f32[5,2,4,1152]{3,2,1,0:T(4,128)S(1)} %get-tuple-element.17), channel_id=1, source_target_pairs={{32,64},{64,32},{96,128},{128,96},{160,192},{192,160},{224,256},{2... | collective-permute-start | bytes 552968 | tf_op jit(solution)/shard_map/ppermute | solution.py:297
  48.9 0.0 copy-done.3
  48.9 0.0 copy-done.4
  48.9 0.8 %shard_map.92 = f32[32,4,256]{2,1,0:T(4,128)} custom-call(s32[3,36,128]{2,1,0:T(8,128)S(1)} %bitcast.2, f32[3,36,128]{2,1,0:T(8,128)S(1)} %bitcast.3), custom_call_target="tpu_custom_call" | custom-call | flops 13824 | bytes 241664 | tf_op jit(solution)/shard_map/pallas_call | solution.py:242
  49.7 1.2 %all-to-all-done.1.sums_ref = f32[8,3,1152]{2,1,0:T(4,128)S(1)} async-done(((f32[8,3,1152]{2,1,0:T(4,128)}), f32[8,3,1152]{2,1,0:T(4,128)S(1)}, u32[]{:S(2)}, u32[]{:S(2)}) %all-to-all-start.1) | async-done | bytes 110624 | tf_op jit(solution)/shard_map/all_to_all | solution.py:277
  50.9 6.4 %all-to-all-start = ((f32[32,4,256]{2,1,0:T(4,128)}), f32[32,4,256]{2,1,0:T(4,128)S(1)}, u32[]{:S(2)}, u32[]{:S(2)}) async-start(f32[32,4,256]{2,1,0:T(4,128)} %shard_map.92), calls=%async_computation | async-start | bytes 262144 | tf_op jit(solution)/shard_map/all_to_all | solution.py:287
  57.3 0.0 collective-permute-done.2.slow_ref
  57.3 0.2 shard_map.91.q_ref
  57.5 2.2 %collective-permute-start.5 = (f32[6,3,4,1152]{3,2,1,0:T(4,128)S(1)}, f32[6,3,4,1152]{3,2,1,0:T(4,128)S(1)}, u32[]{:S(2)}, u32[]{:S(2)}) collective-permute-start(f32[6,3,4,1152]{3,2,1,0:T(4,128)S(1)} %shard_map.91.q_ref), channel_id=1, source_target_pairs={{0,1},{1,0},{2,3},{3,2},{4,5},{5,4},{6,7},{7,6},{8,9},{9,8},{10,11... | collective-permute-start | bytes 995336 | tf_op jit(solution)/shard_map/ppermute | solution.py:310
  59.6 0.7 collective-permute-start.6
  60.3 0.7 shard_map.95
  61.0 5.7 %all-to-all-done.in_ref = f32[32,4,256]{2,1,0:T(4,128)S(1)} async-done(((f32[32,4,256]{2,1,0:T(4,128)}), f32[32,4,256]{2,1,0:T(4,128)S(1)}, u32[]{:S(2)}, u32[]{:S(2)}) %all-to-all-start) | async-done | bytes 131104 | tf_op jit(solution)/shard_map/all_to_all | solution.py:287
  66.7 3.3 %all-to-all-start.2 = ((f32[4,3,1152]{2,1,0:T(4,128)}), f32[4,3,1152]{2,1,0:T(4,128)S(1)}, u32[]{:S(2)}, u32[]{:S(2)}) async-start(f32[4,3,1152]{2,1,0:T(4,128)} %shard_map.95), calls=%async_computation.2 | async-start | bytes 147456 | tf_op jit(solution)/shard_map/all_to_all | solution.py:277
  70.0 0.3 shard_map.93
  70.3 3.9 %all-to-all-done.2.sums_ref = f32[4,3,1152]{2,1,0:T(4,128)S(1)} async-done(((f32[4,3,1152]{2,1,0:T(4,128)}), f32[4,3,1152]{2,1,0:T(4,128)S(1)}, u32[]{:S(2)}, u32[]{:S(2)}) %all-to-all-start.2) | async-done | bytes 55328 | tf_op jit(solution)/shard_map/all_to_all | solution.py:277
  74.1 0.6 shard_map.96
  74.8 0.0 collective-permute-done.5.chip_ref
  74.8 0.0 collective-permute-done.6.other_ref
  74.8 1.6 %shard_map.94 = f32[6,3,4,1152]{3,2,1,0:T(4,128)} custom-call(f32[6,3,4,1152]{3,2,1,0:T(4,128)S(1)} %shard_map.91.q_ref, f32[6,3,4,1152]{3,2,1,0:T(4,128)S(1)} %collective-permute-done.5.chip_ref, f32[6,3,4,1152]{3,2,1,0:T(4,128)S(1)} %collective-permute-done.6.other_ref, f32[3,4,1152]{2,1,0:T(4,128)S(1)} %get-tuple-element.22.delta_ref, ...), custom_call_target="tpu_custom_call" | custom-call | flops 3317760 | bytes 1437696 | tf_op jit(solution)/shard_map/pallas_call | solution.py:242
Async XLA Ops:
  0.6 10.3 %copy-start.2 = (f32[6,3,4,1152]{3,2,1,0:T(4,128)S(1)}, f32[6,3,4,1152]{3,2,1,0:T(4,128)}, u32[]{:S(2)}) copy-start(f32[6,3,4,1152]{3,2,1,0:T(4,128)} %q_ref.5) | copy-start | bytes 995332
  0.6 10.3 %copy-start = (f32[2,3,4,1152]{3,2,1,0:T(4,128)S(1)}, f32[2,3,4,1152]{3,2,1,0:T(4,128)}, u32[]{:S(2)}) copy-start(f32[2,3,4,1152]{3,2,1,0:T(4,128)} %courant_ref.11) | copy-start | bytes 331780
  0.6 10.3 %copy-start.1 = (s32[2,3,4,1152]{3,2,1,0:T(4,128)S(1)}, s32[2,3,4,1152]{3,2,1,0:T(4,128)}, u32[]{:S(2)}) copy-start(s32[2,3,4,1152]{3,2,1,0:T(4,128)} %offsets_ref.11) | copy-start | bytes 331780
  1.8 19.6 %collective-permute-start = (f32[7,2,4,1152]{3,2,1,0:T(4,128)S(1)}, f32[7,2,4,1152]{3,2,1,0:T(4,128)S(1)}, u32[]{:S(2)}, u32[]{:S(2)}) collective-permute-start(f32[7,2,4,1152]{3,2,1,0:T(4,128)S(1)} %get-tuple-element.14), channel_id=1, source_target_pairs={{32,64},{64,32},{96,128},{128,96},{160,192},{192,160},{224,256},{2... | collective-permute-start | bytes 774152 | tf_op jit(solution)/shard_map/ppermute | solution.py:270
  9.0 12.4 %collective-permute-start.1 = (f32[7,2,4,1152]{3,2,1,0:T(4,128)S(1)}, f32[7,2,4,1152]{3,2,1,0:T(4,128)S(1)}, u32[]{:S(2)}, u32[]{:S(2)}) collective-permute-start(f32[7,2,4,1152]{3,2,1,0:T(4,128)S(1)} %get-tuple-element.15), channel_id=1, source_target_pairs={{0,32},{32,0},{64,96},{96,64},{128,160},{160,128},{192,224},{224,1... | collective-permute-start | bytes 774152 | tf_op jit(solution)/shard_map/ppermute | solution.py:271
  21.6 12.0 %collective-permute-start.3 = (f32[6,2,4,1152]{3,2,1,0:T(4,128)S(1)}, f32[6,2,4,1152]{3,2,1,0:T(4,128)S(1)}, u32[]{:S(2)}, u32[]{:S(2)}) collective-permute-start(f32[6,2,4,1152]{3,2,1,0:T(4,128)S(1)} %get-tuple-element.18), channel_id=1, source_target_pairs={{0,32},{32,0},{64,96},{96,64},{128,160},{160,128},{192,224},{224,1... | collective-permute-start | bytes 663560 | tf_op jit(solution)/shard_map/ppermute | solution.py:296
  23.6 10.1 %collective-permute-start.4 = (f32[1,2,4,1152]{3,2,1,0:T(4,128)S(1)}, f32[1,2,4,1152]{3,2,1,0:T(4,128)S(1)}, u32[]{:S(2)}, u32[]{:S(2)}) collective-permute-start(f32[1,2,4,1152]{3,2,1,0:T(4,128)S(1)} %get-tuple-element.20), channel_id=1, source_target_pairs={{32,64},{64,32},{96,128},{128,96},{160,192},{192,160},{224,256},{2... | collective-permute-start | bytes 110600 | tf_op jit(solution)/shard_map/ppermute | solution.py:295
  30.8 2.8 %copy-start.5 = (f32[3,4,1152]{2,1,0:T(4,128)S(1)}, f32[3,4,1152]{2,1,0:T(4,128)}, u32[]{:S(2)}) copy-start(f32[3,4,1152]{2,1,0:T(4,128)} %thickness_ref.1) | copy-start | bytes 165892
  30.8 2.8 %copy-start.6 = (f32[3,1152]{1,0:T(4,128)S(1)}, f32[3,1152]{1,0:T(4,128)}, u32[]{:S(2)}) copy-start(f32[3,1152]{1,0:T(4,128)} %surface_ref.1) | copy-start | bytes 41476
  34.4 14.5 %copy-start.3 = (s32[3,128,36]{1,2,0:T(8,128)S(1)}, s32[3,128,36]{1,2,0:T(8,128)}, u32[]{:S(2)}) copy-start(s32[3,128,36]{1,2,0:T(8,128)} %param.12) | copy-start | bytes 165892
  34.4 14.5 %copy-start.4 = (f32[3,128,36]{1,2,0:T(8,128)S(1)}, f32[3,128,36]{1,2,0:T(8,128)}, u32[]{:S(2)}) copy-start(f32[3,128,36]{1,2,0:T(8,128)} %param.13) | copy-start | bytes 165892
  34.4 16.5 %all-to-all-start.1 = ((f32[8,3,1152]{2,1,0:T(4,128)}), f32[8,3,1152]{2,1,0:T(4,128)S(1)}, u32[]{:S(2)}, u32[]{:S(2)}) async-start(f32[8,3,1152]{2,1,0:T(4,128)} %get-tuple-element.25), calls=%async_computation.1 | async-start | bytes 294912 | tf_op jit(solution)/shard_map/all_to_all | solution.py:277
  41.6 15.6 %collective-permute-start.2 = (f32[5,2,4,1152]{3,2,1,0:T(4,128)S(1)}, f32[5,2,4,1152]{3,2,1,0:T(4,128)S(1)}, u32[]{:S(2)}, u32[]{:S(2)}) collective-permute-start(f32[5,2,4,1152]{3,2,1,0:T(4,128)S(1)} %get-tuple-element.17), channel_id=1, source_target_pairs={{32,64},{64,32},{96,128},{128,96},{160,192},{192,160},{224,256},{2... | collective-permute-start | bytes 552968 | tf_op jit(solution)/shard_map/ppermute | solution.py:297
  50.9 15.8 %all-to-all-start = ((f32[32,4,256]{2,1,0:T(4,128)}), f32[32,4,256]{2,1,0:T(4,128)S(1)}, u32[]{:S(2)}, u32[]{:S(2)}) async-start(f32[32,4,256]{2,1,0:T(4,128)} %shard_map.92), calls=%async_computation | async-start | bytes 262144 | tf_op jit(solution)/shard_map/all_to_all | solution.py:287
  57.5 17.3 %collective-permute-start.5 = (f32[6,3,4,1152]{3,2,1,0:T(4,128)S(1)}, f32[6,3,4,1152]{3,2,1,0:T(4,128)S(1)}, u32[]{:S(2)}, u32[]{:S(2)}) collective-permute-start(f32[6,3,4,1152]{3,2,1,0:T(4,128)S(1)} %shard_map.91.q_ref), channel_id=1, source_target_pairs={{0,1},{1,0},{2,3},{3,2},{4,5},{5,4},{6,7},{7,6},{8,9},{9,8},{10,11... | collective-permute-start | bytes 995336 | tf_op jit(solution)/shard_map/ppermute | solution.py:310
  59.6 15.1 %collective-permute-start.6 = (f32[6,3,4,1152]{3,2,1,0:T(4,128)S(1)}, f32[6,3,4,1152]{3,2,1,0:T(4,128)S(1)}, u32[]{:S(2)}, u32[]{:S(2)}) collective-permute-start(f32[6,3,4,1152]{3,2,1,0:T(4,128)S(1)} %shard_map.91.q_ref), channel_id=1, source_target_pairs={{1,2},{2,1},{3,4},{4,3},{5,6},{6,5},{7,8},{8,7},{9,10},{10,9},{11,... | collective-permute-start | bytes 995336 | tf_op jit(solution)/shard_map/ppermute | solution.py:311
  66.7 7.4 %all-to-all-start.2 = ((f32[4,3,1152]{2,1,0:T(4,128)}), f32[4,3,1152]{2,1,0:T(4,128)S(1)}, u32[]{:S(2)}, u32[]{:S(2)}) async-start(f32[4,3,1152]{2,1,0:T(4,128)} %shard_map.95), calls=%async_computation.2 | async-start | bytes 147456 | tf_op jit(solution)/shard_map/all_to_all | solution.py:277

commit v5 on v4

--- a/solution.py
+++ b/solution.py
@@ -125,7 +125,7 @@
             step *= 2
         part_ref[row] = below[:levels] - 0.5 * heating + surface_ref[row : row + 1]
         sums.append(below[0:1])
-    sums = jnp.concatenate(sums, axis=0)
+    sums = jnp.concatenate(sums, axis=1)
     for k in range(sums_ref.shape[0]):
         sums_ref[k] = sums
 
@@ -156,38 +156,47 @@
 
 def remap_kernel(q_ref, chip_ref, other_ref, delta_ref, weight_ref, out_ref):
     count, rows, levels, width = q_ref.shape
-    me = lax.axis_index("lev")
-    is_first = me == 0
+    me, last = lax.axis_index("lev"), lax.axis_size("lev") - 1
     even = lax.rem(me, 2) == 0
-    is_last = me == lax.axis_size("lev") - 1
-    sub = lax.broadcasted_iota(jnp.int32, (8, width), 0)
-    for row in range(rows):
-        delta = delta_ref[row].astype(jnp.int32)
-        source = jnp.concatenate([delta, delta], axis=0) + (sub & 3) + 2
-        t = weight_ref[row]
-        for f in range(count):
-            own = q_ref[f, row]
-            above, under = chip_ref[f, row], other_ref[f, row]
-            above, under = jnp.where(even, under, above), jnp.where(even, above, under)
-            above = jnp.where(is_first, jnp.broadcast_to(own[0:1], own.shape), above)
-            under = jnp.where(is_last, jnp.broadcast_to(own[levels - 1 :], own.shape), under)
-            early = jnp.concatenate([above, own], axis=0)
-            late = jnp.concatenate([own, under], axis=0)
-            windows = [early]
-            for k in range(1, 4):
-                windows.append(
-                    jnp.where(sub < 4, pltpu.roll(early, 8 - k, 0), pltpu.roll(late, 4 - k, 0))
+
+    def body(above_ref, under_ref):
+        sub = lax.broadcasted_iota(jnp.int32, (8, width), 0)
+        for row in range(rows):
+            delta = delta_ref[row].astype(jnp.int32)
+            source = jnp.concatenate([delta, delta], axis=0) + (sub & 3) + 2
+            t = weight_ref[row]
+            for f in range(count):
+                own = q_ref[f, row]
+                if above_ref is None:
+                    above = jnp.broadcast_to(own[0:1], own.shape)
+                else:
+                    above = above_ref[f, row]
+                if under_ref is None:
+                    under = jnp.broadcast_to(own[levels - 1 :], own.shape)
+                else:
+                    under = under_ref[f, row]
+                early = jnp.concatenate([above, own], axis=0)
+                late = jnp.concatenate([own, under], axis=0)
+                windows = [early]
+                for k in range(1, 4):
+                    windows.append(
+                        jnp.where(sub < 4, pltpu.roll(early, 8 - k, 0), pltpu.roll(late, 4 - k, 0))
+                    )
+                windows.append(late)
+                w0, w1, w2, w3, w4 = windows
+                left = 7.0 * (w1 + w2) - (w0 + w3)
+                right = 7.0 * (w2 + w3) - (w1 + w4)
+                slope = right - left
+                curve = 6.0 * w2 - 0.25 * (left + right)
+                left, slope, curve = (
+                    jnp.take_along_axis(x, source, axis=0)[:levels] for x in (left, slope, curve)
                 )
-            windows.append(late)
-            w0, w1, w2, w3, w4 = windows
-            left = (7.0 * (w1 + w2) - (w0 + w3)) * (1.0 / 12.0)
-            right = (7.0 * (w2 + w3) - (w1 + w4)) * (1.0 / 12.0)
-            slope = right - left
-            curve = 6.0 * w2 - 3.0 * (left + right)
-            left, slope, curve = (
-                jnp.take_along_axis(x, source, axis=0)[:levels] for x in (left, slope, curve)
-            )
-            out_ref[f, row] = left + t * (slope + curve * (1.0 - t))
+                out_ref[f, row] = (left + t * slope) * (1.0 / 12.0) + t * (1.0 - t) * curve
+
+    pl.when(even & (me > 0))(lambda: body(other_ref, chip_ref))
+    pl.when(~even & (me < last))(lambda: body(chip_ref, other_ref))
+    pl.when(me == 0)(lambda: body(None, chip_ref))
+    pl.when(me == last)(lambda: body(chip_ref, None))
 
 
 def columns_kernel(level_ref, weight_ref, out_ref, held):
@@ -232,8 +241,9 @@
     total = sums_ref[0]
     for k in range(1, sums_ref.shape[0]):
         total = total + sums_ref[k]
-    for row in range(part_ref.shape[0]):
-        out_ref[row] = part_ref[row] + total[row : row + 1]
+    rows, _, width = part_ref.shape
+    for row in range(rows):
+        out_ref[row] = part_ref[row] + total[:, row * width : (row + 1) * width]
 
 
 def call(kernel, out, flops, *args, scratch=()):
@@ -299,14 +309,14 @@
     delta, weight = call(join_kernel, [log_thickness.shape] * 2, columns.size, columns)
     delta, weight = call(join_kernel, [log_thickness.shape] * 2, columns.size, columns)
     done, part, sums = call(
-        heat_kernel, [log_thickness.shape, log_thickness.shape, (far, rows, width)], work, base, field, slow0, fast,
+        heat_kernel, [log_thickness.shape, log_thickness.shape, (far, 1, rows * width)], work, base, field, slow0, fast,
         face, courant, offsets, log_thickness, surface,
     )
     (field,) = call(
         second_kernel, [state.shape], work, base, field, slow, fast, face, courant, offsets, done
     )
     sums = exchange(sums, distant)
-    (sums,) = call(group_kernel, [(NEAR, rows, width)], sums.size, sums)
+    (sums,) = call(group_kernel, [(NEAR, 1, rows * width)], sums.size, sums)
     above = lax.ppermute(field, "lev", swaps(groups, 0))
     under = lax.ppermute(field, "lev", swaps(groups, 1))
     sums = exchange(sums, close)

time: 77 us -> 76.8 us (level)
  no operation moved by 1% of the time
where the time goes in v5:
time: 76.8 us; the launch traced here: 76.2 us
  starting transfers between devices  45.7 us (60%)
  waiting for transfers between devices  21.8 us (28%)
  Pallas kernels  7.77 us (10%)
  between operations  0.84 us (1%)
    ppermute x2, starting transfers between devices, per_device(): slow = lax.ppermute(slow, 'lat', swaps(lats, 1))  14.5 us
    all_to_all x2, starting transfers between devices, exchange(): return lax.all_to_all(x, 'lev', 0, 0, tiled=True, axis_index_groups=among)  10.5 us
    ppermute x2, waiting for transfers between devices, per_device(): slow = lax.ppermute(slow, 'lat', swaps(lats, 1))  9.57 us
    ppermute x1, starting transfers between devices, per_device(): slow0 = lax.ppermute(slow0, 'lat', swaps(lats, 1))  7.26 us
    all_to_all x1, starting transfers between devices, per_device(): columns = lax.all_to_all(columns, 'lev', 0, 0, tiled=True)  6.78 us
    pallas_call x10, Pallas kernels, call(): pl.pallas_call(kernel, out_shape=shapes, scratch_shapes=scratch, in_specs...  6.61 us
    all_to_all x1, waiting for transfers between devices, per_device(): columns = lax.all_to_all(columns, 'lev', 0, 0, tiled=True)  5.72 us
    all_to_all x2, waiting for transfers between devices, exchange(): return lax.all_to_all(x, 'lev', 0, 0, tiled=True, axis_index_groups=among)  4.58 us
  transfers between devices with their start and end apart: 10, of which 5 were waited for; matrix products, arithmetic and copies ran while one was open for 0% of the time, Pallas kernels for 5%

profile of v5, /device:TPU:134, one launch (start us, length us, event | category | flops | bytes accessed | tf_op | source)
XLA Modules:
  0.0 76.2 jit_solution(8305703244494813416)
XLA Ops:
  0.6 0.0 copy-start.2
  0.6 0.0 copy-start
  0.6 0.0 copy-start.1
  0.7 1.2 %shard_map.87 = (f32[7,2,4,1152]{3,2,1,0:T(4,128)S(1)}, f32[7,2,4,1152]{3,2,1,0:T(4,128)S(1)}) custom-call(f32[6,3,4,1152]{3,2,1,0:T(4,128)} %q_ref.5, f32[2,3,4,1152]{3,2,1,0:T(4,128)} %courant_ref.11, s32[2,3,4,1152]{3,2,1,0:T(4,128)} %offsets_ref.11), custom_call_target="tpu_custom_call" | custom-call | tf_op jit(solution)/shard_map/pallas_call | solution.py:272
  1.8 7.2 %collective-permute-start = (f32[7,2,4,1152]{3,2,1,0:T(4,128)S(1)}, f32[7,2,4,1152]{3,2,1,0:T(4,128)S(1)}, u32[]{:S(2)}, u32[]{:S(2)}) collective-permute-start(f32[7,2,4,1152]{3,2,1,0:T(4,128)S(1)} %get-tuple-element.14), channel_id=1, source_target_pairs={{32,64},{64,32},{96,128},{128,96},{160,192},{192,160},{224,256},{2... | collective-permute-start | bytes 774152 | tf_op jit(solution)/shard_map/ppermute | solution.py:280
  9.0 1.9 %collective-permute-start.1 = (f32[7,2,4,1152]{3,2,1,0:T(4,128)S(1)}, f32[7,2,4,1152]{3,2,1,0:T(4,128)S(1)}, u32[]{:S(2)}, u32[]{:S(2)}) collective-permute-start(f32[7,2,4,1152]{3,2,1,0:T(4,128)S(1)} %get-tuple-element.15), channel_id=1, source_target_pairs={{0,32},{32,0},{64,96},{96,64},{128,160},{160,128},{192,224},{224,1... | collective-permute-start | bytes 774152 | tf_op jit(solution)/shard_map/ppermute | solution.py:281
  11.0 0.0 copy-done.2
  11.0 0.0 copy-done
  11.0 0.0 copy-done.1
  11.0 0.8 %shard_map.86.base_ref = f32[6,3,4,1152]{3,2,1,0:T(4,128)S(1)} custom-call(f32[6,3,4,1152]{3,2,1,0:T(4,128)S(1)} %copy-done.2, f32[2,3,4,1152]{3,2,1,0:T(4,128)S(1)} %copy-done, s32[2,3,4,1152]{3,2,1,0:T(4,128)S(1)} %copy-done.1), custom_call_target="tpu_custom_call" | custom-call | flops 1658880 | bytes 884736 | tf_op jit(solution)/shard_map/pallas_call | solution.py:252
  11.9 9.6 %collective-permute-done.slow_ref = f32[7,2,4,1152]{3,2,1,0:T(4,128)S(1)} collective-permute-done((f32[7,2,4,1152]{3,2,1,0:T(4,128)S(1)}, f32[7,2,4,1152]{3,2,1,0:T(4,128)S(1)}, u32[]{:S(2)}, u32[]{:S(2)}) %collective-permute-start) | collective-permute-done | bytes 258080 | tf_op jit(solution)/shard_map/ppermute | solution.py:280
  21.4 0.0 collective-permute-done.1.fast_ref
  21.4 0.2 shard_map.88
  21.6 1.9 %collective-permute-start.3 = (f32[6,2,4,1152]{3,2,1,0:T(4,128)S(1)}, f32[6,2,4,1152]{3,2,1,0:T(4,128)S(1)}, u32[]{:S(2)}, u32[]{:S(2)}) collective-permute-start(f32[6,2,4,1152]{3,2,1,0:T(4,128)S(1)} %get-tuple-element.18), channel_id=1, source_target_pairs={{0,32},{32,0},{64,96},{96,64},{128,160},{160,128},{192,224},{224,1... | collective-permute-start | bytes 663560 | tf_op jit(solution)/shard_map/ppermute | solution.py:306
  23.6 7.3 %collective-permute-start.4 = (f32[1,2,4,1152]{3,2,1,0:T(4,128)S(1)}, f32[1,2,4,1152]{3,2,1,0:T(4,128)S(1)}, u32[]{:S(2)}, u32[]{:S(2)}) collective-permute-start(f32[1,2,4,1152]{3,2,1,0:T(4,128)S(1)} %get-tuple-element.20), channel_id=1, source_target_pairs={{32,64},{64,32},{96,128},{128,96},{160,192},{192,160},{224,256},{2... | collective-permute-start | bytes 110600 | tf_op jit(solution)/shard_map/ppermute | solution.py:305
  30.8 0.0 copy-start.5
  30.8 0.0 copy-start.6
  30.9 0.8 %shard_map.89.base_ref = f32[6,3,4,1152]{3,2,1,0:T(4,128)S(1)} custom-call(f32[6,3,4,1152]{3,2,1,0:T(4,128)S(1)} %get-tuple-element.16.q_ref, f32[2,3,4,1152]{3,2,1,0:T(4,128)S(1)} %copy-done, s32[2,3,4,1152]{3,2,1,0:T(4,128)S(1)} %copy-done.1), custom_call_target="tpu_custom_call" | custom-call | flops 1658880 | bytes 884736 | tf_op jit(solution)/shard_map/pallas_call | solution.py:252
  31.7 1.9 %collective-permute-done.4.slow_ref = f32[1,2,4,1152]{3,2,1,0:T(4,128)S(1)} collective-permute-done((f32[1,2,4,1152]{3,2,1,0:T(4,128)S(1)}, f32[1,2,4,1152]{3,2,1,0:T(4,128)S(1)}, u32[]{:S(2)}, u32[]{:S(2)}) %collective-permute-start.4) | collective-permute-done | bytes 36896 | tf_op jit(solution)/shard_map/ppermute | solution.py:305
  33.6 0.0 collective-permute-done.3.fast_ref
  33.6 0.0 copy-done.5
  33.6 0.0 copy-done.6
  33.7 0.7 shard_map.90
  34.4 0.0 copy-start.3
  34.4 0.0 copy-start.4
  34.4 7.2 %all-to-all-start.1 = ((f32[8,1,3456]{2,1,0:T(1,128)}), f32[8,1,3456]{2,1,0:T(1,128)S(1)}, u32[]{:S(2)}, u32[]{:S(2)}) async-start(f32[8,1,3456]{2,1,0:T(1,128)} %get-tuple-element.25), calls=%async_computation.1 | async-start | bytes 221184 | tf_op jit(solution)/shard_map/all_to_all | solution.py:287
  41.6 7.2 %collective-permute-start.2 = (f32[5,2,4,1152]{3,2,1,0:T(4,128)S(1)}, f32[5,2,4,1152]{3,2,1,0:T(4,128)S(1)}, u32[]{:S(2)}, u32[]{:S(2)}) collective-permute-start(f32[5,2,4,1152]{3,2,1,0:T(4,128)S(1)} %get-tuple-element.17), channel_id=1, source_target_pairs={{32,64},{64,32},{96,128},{128,96},{160,192},{192,160},{224,256},{2... | collective-permute-start | bytes 552968 | tf_op jit(solution)/shard_map/ppermute | solution.py:307
  48.9 0.0 copy-done.3
  48.9 0.0 copy-done.4
  48.9 0.8 %shard_map.92 = f32[32,4,256]{2,1,0:T(4,128)} custom-call(s32[3,36,128]{2,1,0:T(8,128)S(1)} %bitcast.2, f32[3,36,128]{2,1,0:T(8,128)S(1)} %bitcast.3), custom_call_target="tpu_custom_call" | custom-call | flops 13824 | bytes 241664 | tf_op jit(solution)/shard_map/pallas_call | solution.py:252
  49.6 0.8 %all-to-all-done.1.sums_ref = f32[8,1,3456]{2,1,0:T(1,128)S(1)} async-done(((f32[8,1,3456]{2,1,0:T(1,128)}), f32[8,1,3456]{2,1,0:T(1,128)S(1)}, u32[]{:S(2)}, u32[]{:S(2)}) %all-to-all-start.1) | async-done | bytes 110624 | tf_op jit(solution)/shard_map/all_to_all | solution.py:287
  50.5 6.8 %all-to-all-start = ((f32[32,4,256]{2,1,0:T(4,128)}), f32[32,4,256]{2,1,0:T(4,128)S(1)}, u32[]{:S(2)}, u32[]{:S(2)}) async-start(f32[32,4,256]{2,1,0:T(4,128)} %shard_map.92), calls=%async_computation | async-start | bytes 262144 | tf_op jit(solution)/shard_map/all_to_all | solution.py:297
  57.3 0.0 collective-permute-done.2.slow_ref
  57.3 0.2 shard_map.91.q_ref
  57.4 2.2 %collective-permute-start.5 = (f32[6,3,4,1152]{3,2,1,0:T(4,128)S(1)}, f32[6,3,4,1152]{3,2,1,0:T(4,128)S(1)}, u32[]{:S(2)}, u32[]{:S(2)}) collective-permute-start(f32[6,3,4,1152]{3,2,1,0:T(4,128)S(1)} %shard_map.91.q_ref), channel_id=1, source_target_pairs={{0,1},{1,0},{2,3},{3,2},{4,5},{5,4},{6,7},{7,6},{8,9},{9,8},{10,11... | collective-permute-start | bytes 995336 | tf_op jit(solution)/shard_map/ppermute | solution.py:320
  59.6 0.7 collective-permute-start.6
  60.3 0.7 shard_map.95
  61.0 5.7 %all-to-all-done.in_ref = f32[32,4,256]{2,1,0:T(4,128)S(1)} async-done(((f32[32,4,256]{2,1,0:T(4,128)}), f32[32,4,256]{2,1,0:T(4,128)S(1)}, u32[]{:S(2)}, u32[]{:S(2)}) %all-to-all-start) | async-done | bytes 131104 | tf_op jit(solution)/shard_map/all_to_all | solution.py:297
  66.7 3.3 %all-to-all-start.2 = ((f32[4,1,3456]{2,1,0:T(1,128)}), f32[4,1,3456]{2,1,0:T(1,128)S(1)}, u32[]{:S(2)}, u32[]{:S(2)}) async-start(f32[4,1,3456]{2,1,0:T(1,128)} %shard_map.95), calls=%async_computation.2 | async-start | bytes 110592 | tf_op jit(solution)/shard_map/all_to_all | solution.py:287
  70.0 0.3 shard_map.93
  70.2 3.8 %all-to-all-done.2.sums_ref = f32[4,1,3456]{2,1,0:T(1,128)S(1)} async-done(((f32[4,1,3456]{2,1,0:T(1,128)}), f32[4,1,3456]{2,1,0:T(1,128)S(1)}, u32[]{:S(2)}, u32[]{:S(2)}) %all-to-all-start.2) | async-done | bytes 55328 | tf_op jit(solution)/shard_map/all_to_all | solution.py:287
  74.0 0.6 shard_map.96
  74.7 0.0 collective-permute-done.5.chip_ref
  74.7 0.0 collective-permute-done.6.other_ref
  74.7 1.5 %shard_map.94 = f32[6,3,4,1152]{3,2,1,0:T(4,128)} custom-call(f32[6,3,4,1152]{3,2,1,0:T(4,128)S(1)} %shard_map.91.q_ref, f32[6,3,4,1152]{3,2,1,0:T(4,128)S(1)} %collective-permute-done.5.chip_ref, f32[6,3,4,1152]{3,2,1,0:T(4,128)S(1)} %collective-permute-done.6.other_ref, f32[3,4,1152]{2,1,0:T(4,128)S(1)} %get-tuple-element.22.delta_ref, ...), custom_call_target="tpu_custom_call" | custom-call | flops 3317760 | bytes 1437696 | tf_op jit(solution)/shard_map/pallas_call | solution.py:252
Async XLA Ops:
  0.6 10.3 %copy-start.2 = (f32[6,3,4,1152]{3,2,1,0:T(4,128)S(1)}, f32[6,3,4,1152]{3,2,1,0:T(4,128)}, u32[]{:S(2)}) copy-start(f32[6,3,4,1152]{3,2,1,0:T(4,128)} %q_ref.5) | copy-start | bytes 995332
  0.6 10.3 %copy-start = (f32[2,3,4,1152]{3,2,1,0:T(4,128)S(1)}, f32[2,3,4,1152]{3,2,1,0:T(4,128)}, u32[]{:S(2)}) copy-start(f32[2,3,4,1152]{3,2,1,0:T(4,128)} %courant_ref.11) | copy-start | bytes 331780
  0.6 10.3 %copy-start.1 = (s32[2,3,4,1152]{3,2,1,0:T(4,128)S(1)}, s32[2,3,4,1152]{3,2,1,0:T(4,128)}, u32[]{:S(2)}) copy-start(s32[2,3,4,1152]{3,2,1,0:T(4,128)} %offsets_ref.11) | copy-start | bytes 331780
  1.8 19.6 %collective-permute-start = (f32[7,2,4,1152]{3,2,1,0:T(4,128)S(1)}, f32[7,2,4,1152]{3,2,1,0:T(4,128)S(1)}, u32[]{:S(2)}, u32[]{:S(2)}) collective-permute-start(f32[7,2,4,1152]{3,2,1,0:T(4,128)S(1)} %get-tuple-element.14), channel_id=1, source_target_pairs={{32,64},{64,32},{96,128},{128,96},{160,192},{192,160},{224,256},{2... | collective-permute-start | bytes 774152 | tf_op jit(solution)/shard_map/ppermute | solution.py:280
  9.0 12.4 %collective-permute-start.1 = (f32[7,2,4,1152]{3,2,1,0:T(4,128)S(1)}, f32[7,2,4,1152]{3,2,1,0:T(4,128)S(1)}, u32[]{:S(2)}, u32[]{:S(2)}) collective-permute-start(f32[7,2,4,1152]{3,2,1,0:T(4,128)S(1)} %get-tuple-element.15), channel_id=1, source_target_pairs={{0,32},{32,0},{64,96},{96,64},{128,160},{160,128},{192,224},{224,1... | collective-permute-start | bytes 774152 | tf_op jit(solution)/shard_map/ppermute | solution.py:281
  21.6 12.0 %collective-permute-start.3 = (f32[6,2,4,1152]{3,2,1,0:T(4,128)S(1)}, f32[6,2,4,1152]{3,2,1,0:T(4,128)S(1)}, u32[]{:S(2)}, u32[]{:S(2)}) collective-permute-start(f32[6,2,4,1152]{3,2,1,0:T(4,128)S(1)} %get-tuple-element.18), channel_id=1, source_target_pairs={{0,32},{32,0},{64,96},{96,64},{128,160},{160,128},{192,224},{224,1... | collective-permute-start | bytes 663560 | tf_op jit(solution)/shard_map/ppermute | solution.py:306
  23.6 10.1 %collective-permute-start.4 = (f32[1,2,4,1152]{3,2,1,0:T(4,128)S(1)}, f32[1,2,4,1152]{3,2,1,0:T(4,128)S(1)}, u32[]{:S(2)}, u32[]{:S(2)}) collective-permute-start(f32[1,2,4,1152]{3,2,1,0:T(4,128)S(1)} %get-tuple-element.20), channel_id=1, source_target_pairs={{32,64},{64,32},{96,128},{128,96},{160,192},{192,160},{224,256},{2... | collective-permute-start | bytes 110600 | tf_op jit(solution)/shard_map/ppermute | solution.py:305
  30.8 2.8 %copy-start.5 = (f32[3,4,1152]{2,1,0:T(4,128)S(1)}, f32[3,4,1152]{2,1,0:T(4,128)}, u32[]{:S(2)}) copy-start(f32[3,4,1152]{2,1,0:T(4,128)} %thickness_ref.1) | copy-start | bytes 165892
  30.8 2.8 %copy-start.6 = (f32[3,1152]{1,0:T(4,128)S(1)}, f32[3,1152]{1,0:T(4,128)}, u32[]{:S(2)}) copy-start(f32[3,1152]{1,0:T(4,128)} %surface_ref.1) | copy-start | bytes 41476
  34.4 14.5 %copy-start.3 = (s32[3,128,36]{1,2,0:T(8,128)S(1)}, s32[3,128,36]{1,2,0:T(8,128)}, u32[]{:S(2)}) copy-start(s32[3,128,36]{1,2,0:T(8,128)} %param.12) | copy-start | bytes 165892
  34.4 14.5 %copy-start.4 = (f32[3,128,36]{1,2,0:T(8,128)S(1)}, f32[3,128,36]{1,2,0:T(8,128)}, u32[]{:S(2)}) copy-start(f32[3,128,36]{1,2,0:T(8,128)} %param.13) | copy-start | bytes 165892
  34.4 16.1 %all-to-all-start.1 = ((f32[8,1,3456]{2,1,0:T(1,128)}), f32[8,1,3456]{2,1,0:T(1,128)S(1)}, u32[]{:S(2)}, u32[]{:S(2)}) async-start(f32[8,1,3456]{2,1,0:T(1,128)} %get-tuple-element.25), calls=%async_computation.1 | async-start | bytes 221184 | tf_op jit(solution)/shard_map/all_to_all | solution.py:287
  41.6 15.7 %collective-permute-start.2 = (f32[5,2,4,1152]{3,2,1,0:T(4,128)S(1)}, f32[5,2,4,1152]{3,2,1,0:T(4,128)S(1)}, u32[]{:S(2)}, u32[]{:S(2)}) collective-permute-start(f32[5,2,4,1152]{3,2,1,0:T(4,128)S(1)} %get-tuple-element.17), channel_id=1, source_target_pairs={{32,64},{64,32},{96,128},{128,96},{160,192},{192,160},{224,256},{2... | collective-permute-start | bytes 552968 | tf_op jit(solution)/shard_map/ppermute | solution.py:307
  50.5 16.2 %all-to-all-start = ((f32[32,4,256]{2,1,0:T(4,128)}), f32[32,4,256]{2,1,0:T(4,128)S(1)}, u32[]{:S(2)}, u32[]{:S(2)}) async-start(f32[32,4,256]{2,1,0:T(4,128)} %shard_map.92), calls=%async_computation | async-start | bytes 262144 | tf_op jit(solution)/shard_map/all_to_all | solution.py:297
  57.4 17.2 %collective-permute-start.5 = (f32[6,3,4,1152]{3,2,1,0:T(4,128)S(1)}, f32[6,3,4,1152]{3,2,1,0:T(4,128)S(1)}, u32[]{:S(2)}, u32[]{:S(2)}) collective-permute-start(f32[6,3,4,1152]{3,2,1,0:T(4,128)S(1)} %shard_map.91.q_ref), channel_id=1, source_target_pairs={{0,1},{1,0},{2,3},{3,2},{4,5},{5,4},{6,7},{7,6},{8,9},{9,8},{10,11... | collective-permute-start | bytes 995336 | tf_op jit(solution)/shard_map/ppermute | solution.py:320
  59.6 15.0 %collective-permute-start.6 = (f32[6,3,4,1152]{3,2,1,0:T(4,128)S(1)}, f32[6,3,4,1152]{3,2,1,0:T(4,128)S(1)}, u32[]{:S(2)}, u32[]{:S(2)}) collective-permute-start(f32[6,3,4,1152]{3,2,1,0:T(4,128)S(1)} %shard_map.91.q_ref), channel_id=1, source_target_pairs={{1,2},{2,1},{3,4},{4,3},{5,6},{6,5},{7,8},{8,7},{9,10},{10,9},{11,... | collective-permute-start | bytes 995336 | tf_op jit(solution)/shard_map/ppermute | solution.py:321
  66.7 7.3 %all-to-all-start.2 = ((f32[4,1,3456]{2,1,0:T(1,128)}), f32[4,1,3456]{2,1,0:T(1,128)S(1)}, u32[]{:S(2)}, u32[]{:S(2)}) async-start(f32[4,1,3456]{2,1,0:T(1,128)} %shard_map.95), calls=%async_computation.2 | async-start | bytes 110592 | tf_op jit(solution)/shard_map/all_to_all | solution.py:287

commit v6 on v5

--- a/solution.py
+++ b/solution.py
@@ -7,6 +7,7 @@
 
 
 NEAR = 4
+EARLY = 3
 
 
 def pick(offset, behind, here, ahead, beyond):
@@ -107,10 +108,10 @@
         new = advected(f, base_ref, q_ref, slow_ref, fast_ref, face, courant_ref, offsets_ref)
         for row in range(rows):
             out_ref[f, row] = new[row]
-        if f == 0:
-            send(0, new, slow0_ref, next_fast_ref)
+        if f < EARLY:
+            send(f, new, slow0_ref, next_fast_ref)
         else:
-            send(f, new, next_slow_ref, next_fast_ref, f - 1)
+            send(f, new, next_slow_ref, next_fast_ref, f - EARLY)
 
 
 def heat(new, thickness_ref, surface_ref, part_ref, sums_ref):
@@ -142,14 +143,15 @@
 
 
 def second_kernel(
-    base_ref, q_ref, slow_ref, fast_ref, face_ref, courant_ref, offsets_ref, done_ref, out_ref
+    base_ref, q_ref, early_ref, slow_ref, fast_ref, face_ref, courant_ref, offsets_ref, done_ref, out_ref
 ):
     count, rows = q_ref.shape[:2]
     face = face_ref[0], face_ref[1].astype(jnp.int32)
     for row in range(rows):
         out_ref[0, row] = done_ref[row]
     for f in range(1, count):
-        new = advected(f, base_ref, q_ref, slow_ref, fast_ref, face, courant_ref, offsets_ref, f - 1)
+        halo_ref, g = (early_ref, f) if f < EARLY else (slow_ref, f - EARLY)
+        new = advected(f, base_ref, q_ref, halo_ref, fast_ref, face, courant_ref, offsets_ref, g)
         for row in range(rows):
             out_ref[f, row] = new[row]
 
@@ -297,7 +299,7 @@
     columns = lax.all_to_all(columns, "lev", 0, 0, tiled=True)
 
     (base,) = call(east_kernel, [state.shape], work, state, courant, offsets)
-    first, rest = (1, *edge[1:]), (count - 1, *edge[1:])
+    first, rest = (EARLY, *edge[1:]), (count - EARLY, *edge[1:])
     field, face, slow0, slow, fast = call(
         first_kernel, [state.shape, (2, levels, width), first, rest, edge], work, base, state, slow, fast,
         courant, offsets,
@@ -313,14 +315,16 @@
         face, courant, offsets, log_thickness, surface,
     )
     (field,) = call(
-        second_kernel, [state.shape], work, base, field, slow, fast, face, courant, offsets, done
+        second_kernel, [state.shape], work, base, field, slow0, slow, fast, face, courant, offsets, done
     )
     sums = exchange(sums, distant)
     (sums,) = call(group_kernel, [(NEAR, 1, rows * width)], sums.size, sums)
     above = lax.ppermute(field, "lev", swaps(groups, 0))
     under = lax.ppermute(field, "lev", swaps(groups, 1))
     sums = exchange(sums, close)
-    (remapped,) = call(remap_kernel, [state.shape], 2 * work, field, above, under, delta, weight)
+    (remapped,) = call(
+        remap_kernel, [state.shape], 2 * work, field, above, under, delta, weight
+    )
     (geopotential,) = call(close_kernel, [log_thickness.shape], sums.size, part, sums)
     return (remapped, geopotential)
 
@@ -337,6 +341,4 @@
     )
     out_specs = (P(None, "lat", "lev", None), P("lat", "lev", None))
 
-    return jax.shard_map(
-        per_device, mesh=mesh, in_specs=in_specs, out_specs=out_specs, check_vma=False
-    )
+    return jax.shard_map(per_device, mesh=mesh, in_specs=in_specs, out_specs=out_specs, check_vma=False)

time: 76.8 us -> 77.6 us (1.010)
  waiting for transfers between devices: 21.8 us -> 23.4 us
    ppermute x1, waiting for transfers between devices: 1.93 us -> 3.1 us  [per_device(): slow0 = lax.ppermute(slow0, 'lat', swaps(lats, 1))]
where the time goes in v6:
time: 77.6 us; the launch traced here: 77 us
  starting transfers between devices  45 us (58%)
  waiting for transfers between devices  23.4 us (30%)
  Pallas kernels  7.77 us (10%)
  between operations  0.84 us (1%)
    ppermute x2, starting transfers between devices, per_device(): slow = lax.ppermute(slow, 'lat', swaps(lats, 1))  14.1 us
    all_to_all x2, starting transfers between devices, exchange(): return lax.all_to_all(x, 'lev', 0, 0, tiled=True, axis_index_groups=among)  10.5 us
    ppermute x2, waiting for transfers between devices, per_device(): slow = lax.ppermute(slow, 'lat', swaps(lats, 1))  9.57 us
    ppermute x1, starting transfers between devices, per_device(): slow0 = lax.ppermute(slow0, 'lat', swaps(lats, 1))  7.26 us
    pallas_call x10, Pallas kernels, call(): pl.pallas_call(kernel, out_shape=shapes, scratch_shapes=scratch, in_specs...  6.61 us
    all_to_all x1, starting transfers between devices, per_device(): columns = lax.all_to_all(columns, 'lev', 0, 0, tiled=True)  6.4 us
    all_to_all x1, waiting for transfers between devices, per_device(): columns = lax.all_to_all(columns, 'lev', 0, 0, tiled=True)  5.72 us
    all_to_all x2, waiting for transfers between devices, exchange(): return lax.all_to_all(x, 'lev', 0, 0, tiled=True, axis_index_groups=among)  4.96 us
  transfers between devices with their start and end apart: 10, of which 5 were waited for; matrix products, arithmetic and copies ran while one was open for 0% of the time, Pallas kernels for 5%

profile of v6, /device:TPU:134, one launch (start us, length us, event | category | flops | bytes accessed | tf_op | source)
XLA Modules:
  0.0 77.0 jit_solution(12723139348696587071)
XLA Ops:
  0.6 0.0 copy-start.2
  0.6 0.0 copy-start
  0.6 0.0 copy-start.1
  0.7 1.2 %shard_map.87 = (f32[7,2,4,1152]{3,2,1,0:T(4,128)S(1)}, f32[7,2,4,1152]{3,2,1,0:T(4,128)S(1)}) custom-call(f32[6,3,4,1152]{3,2,1,0:T(4,128)} %q_ref.5, f32[2,3,4,1152]{3,2,1,0:T(4,128)} %courant_ref.11, s32[2,3,4,1152]{3,2,1,0:T(4,128)} %offsets_ref.11), custom_call_target="tpu_custom_call" | custom-call | tf_op jit(solution)/shard_map/pallas_call | solution.py:274
  1.8 7.2 %collective-permute-start = (f32[7,2,4,1152]{3,2,1,0:T(4,128)S(1)}, f32[7,2,4,1152]{3,2,1,0:T(4,128)S(1)}, u32[]{:S(2)}, u32[]{:S(2)}) collective-permute-start(f32[7,2,4,1152]{3,2,1,0:T(4,128)S(1)} %get-tuple-element.14), channel_id=1, source_target_pairs={{32,64},{64,32},{96,128},{128,96},{160,192},{192,160},{224,256},{2... | collective-permute-start | bytes 774152 | tf_op jit(solution)/shard_map/ppermute | solution.py:282
  9.0 1.9 %collective-permute-start.1 = (f32[7,2,4,1152]{3,2,1,0:T(4,128)S(1)}, f32[7,2,4,1152]{3,2,1,0:T(4,128)S(1)}, u32[]{:S(2)}, u32[]{:S(2)}) collective-permute-start(f32[7,2,4,1152]{3,2,1,0:T(4,128)S(1)} %get-tuple-element.15), channel_id=1, source_target_pairs={{0,32},{32,0},{64,96},{96,64},{128,160},{160,128},{192,224},{224,1... | collective-permute-start | bytes 774152 | tf_op jit(solution)/shard_map/ppermute | solution.py:283
  11.0 0.0 copy-done.2
  11.0 0.0 copy-done
  11.0 0.0 copy-done.1
  11.0 0.8 %shard_map.86.base_ref = f32[6,3,4,1152]{3,2,1,0:T(4,128)S(1)} custom-call(f32[6,3,4,1152]{3,2,1,0:T(4,128)S(1)} %copy-done.2, f32[2,3,4,1152]{3,2,1,0:T(4,128)S(1)} %copy-done, s32[2,3,4,1152]{3,2,1,0:T(4,128)S(1)} %copy-done.1), custom_call_target="tpu_custom_call" | custom-call | flops 1658880 | bytes 884736 | tf_op jit(solution)/shard_map/pallas_call | solution.py:254
  11.9 9.6 %collective-permute-done.slow_ref = f32[7,2,4,1152]{3,2,1,0:T(4,128)S(1)} collective-permute-done((f32[7,2,4,1152]{3,2,1,0:T(4,128)S(1)}, f32[7,2,4,1152]{3,2,1,0:T(4,128)S(1)}, u32[]{:S(2)}, u32[]{:S(2)}) %collective-permute-start) | collective-permute-done | bytes 258080 | tf_op jit(solution)/shard_map/ppermute | solution.py:282
  21.4 0.0 collective-permute-done.1.fast_ref
  21.4 0.2 shard_map.88
  21.6 1.9 %collective-permute-start.4 = (f32[6,2,4,1152]{3,2,1,0:T(4,128)S(1)}, f32[6,2,4,1152]{3,2,1,0:T(4,128)S(1)}, u32[]{:S(2)}, u32[]{:S(2)}) collective-permute-start(f32[6,2,4,1152]{3,2,1,0:T(4,128)S(1)} %get-tuple-element.19), channel_id=1, source_target_pairs={{0,32},{32,0},{64,96},{96,64},{128,160},{160,128},{192,224},{224,1... | collective-permute-start | bytes 663560 | tf_op jit(solution)/shard_map/ppermute | solution.py:308
  23.6 7.3 %collective-permute-start.2 = (f32[3,2,4,1152]{3,2,1,0:T(4,128)S(1)}, f32[3,2,4,1152]{3,2,1,0:T(4,128)S(1)}, u32[]{:S(2)}, u32[]{:S(2)}) collective-permute-start(f32[3,2,4,1152]{3,2,1,0:T(4,128)S(1)} %get-tuple-element.17), channel_id=1, source_target_pairs={{32,64},{64,32},{96,128},{128,96},{160,192},{192,160},{224,256},{2... | collective-permute-start | bytes 331784 | tf_op jit(solution)/shard_map/ppermute | solution.py:307
  30.8 0.0 copy-start.5
  30.8 0.0 copy-start.6
  30.9 0.8 %shard_map.89.base_ref = f32[6,3,4,1152]{3,2,1,0:T(4,128)S(1)} custom-call(f32[6,3,4,1152]{3,2,1,0:T(4,128)S(1)} %get-tuple-element.16.q_ref, f32[2,3,4,1152]{3,2,1,0:T(4,128)S(1)} %copy-done, s32[2,3,4,1152]{3,2,1,0:T(4,128)S(1)} %copy-done.1), custom_call_target="tpu_custom_call" | custom-call | flops 1658880 | bytes 884736 | tf_op jit(solution)/shard_map/pallas_call | solution.py:254
  31.7 3.1 %collective-permute-done.2.slow_ref.early_ref = f32[3,2,4,1152]{3,2,1,0:T(4,128)S(1)} collective-permute-done((f32[3,2,4,1152]{3,2,1,0:T(4,128)S(1)}, f32[3,2,4,1152]{3,2,1,0:T(4,128)S(1)}, u32[]{:S(2)}, u32[]{:S(2)}) %collective-permute-start.2) | collective-permute-done | bytes 110624 | tf_op jit(solution)/shard_map/ppermute | solution.py:307
  34.8 0.0 collective-permute-done.4.fast_ref
  34.8 0.0 copy-done.5
  34.8 0.0 copy-done.6
  34.8 0.7 shard_map.90
  35.5 0.0 copy-start.3
  35.5 0.0 copy-start.4
  35.5 7.2 %all-to-all-start.1 = ((f32[8,1,3456]{2,1,0:T(1,128)}), f32[8,1,3456]{2,1,0:T(1,128)S(1)}, u32[]{:S(2)}, u32[]{:S(2)}) async-start(f32[8,1,3456]{2,1,0:T(1,128)} %get-tuple-element.25), calls=%async_computation.1 | async-start | bytes 221184 | tf_op jit(solution)/shard_map/all_to_all | solution.py:289
  42.8 6.9 %collective-permute-start.3 = (f32[3,2,4,1152]{3,2,1,0:T(4,128)S(1)}, f32[3,2,4,1152]{3,2,1,0:T(4,128)S(1)}, u32[]{:S(2)}, u32[]{:S(2)}) collective-permute-start(f32[3,2,4,1152]{3,2,1,0:T(4,128)S(1)} %get-tuple-element.18), channel_id=1, source_target_pairs={{32,64},{64,32},{96,128},{128,96},{160,192},{192,160},{224,256},{2... | collective-permute-start | bytes 331784 | tf_op jit(solution)/shard_map/ppermute | solution.py:309
  49.6 0.0 copy-done.3
  49.7 0.0 copy-done.4
  49.7 0.8 shard_map.92
  50.4 1.2 %all-to-all-done.1.sums_ref = f32[8,1,3456]{2,1,0:T(1,128)S(1)} async-done(((f32[8,1,3456]{2,1,0:T(1,128)}), f32[8,1,3456]{2,1,0:T(1,128)S(1)}, u32[]{:S(2)}, u32[]{:S(2)}) %all-to-all-start.1) | async-done | bytes 110624 | tf_op jit(solution)/shard_map/all_to_all | solution.py:289
  51.6 6.4 %all-to-all-start = ((f32[32,4,256]{2,1,0:T(4,128)}), f32[32,4,256]{2,1,0:T(4,128)S(1)}, u32[]{:S(2)}, u32[]{:S(2)}) async-start(f32[32,4,256]{2,1,0:T(4,128)} %shard_map.92), calls=%async_computation | async-start | bytes 262144 | tf_op jit(solution)/shard_map/all_to_all | solution.py:299
  58.0 0.0 collective-permute-done.3.slow_ref
  58.1 0.2 shard_map.91.q_ref
  58.2 2.2 %collective-permute-start.5 = (f32[6,3,4,1152]{3,2,1,0:T(4,128)S(1)}, f32[6,3,4,1152]{3,2,1,0:T(4,128)S(1)}, u32[]{:S(2)}, u32[]{:S(2)}) collective-permute-start(f32[6,3,4,1152]{3,2,1,0:T(4,128)S(1)} %shard_map.91.q_ref), channel_id=1, source_target_pairs={{0,1},{1,0},{2,3},{3,2},{4,5},{5,4},{6,7},{7,6},{8,9},{9,8},{10,11... | collective-permute-start | bytes 995336 | tf_op jit(solution)/shard_map/ppermute | solution.py:322
  60.4 0.7 collective-permute-start.6
  61.1 0.7 shard_map.95
  61.8 5.7 %all-to-all-done.in_ref = f32[32,4,256]{2,1,0:T(4,128)S(1)} async-done(((f32[32,4,256]{2,1,0:T(4,128)}), f32[32,4,256]{2,1,0:T(4,128)S(1)}, u32[]{:S(2)}, u32[]{:S(2)}) %all-to-all-start) | async-done | bytes 131104 | tf_op jit(solution)/shard_map/all_to_all | solution.py:299
  67.5 3.3 %all-to-all-start.2 = ((f32[4,1,3456]{2,1,0:T(1,128)}), f32[4,1,3456]{2,1,0:T(1,128)S(1)}, u32[]{:S(2)}, u32[]{:S(2)}) async-start(f32[4,1,3456]{2,1,0:T(1,128)} %shard_map.95), calls=%async_computation.2 | async-start | bytes 110592 | tf_op jit(solution)/shard_map/all_to_all | solution.py:289
  70.8 0.3 shard_map.93
  71.0 3.8 %all-to-all-done.2.sums_ref = f32[4,1,3456]{2,1,0:T(1,128)S(1)} async-done(((f32[4,1,3456]{2,1,0:T(1,128)}), f32[4,1,3456]{2,1,0:T(1,128)S(1)}, u32[]{:S(2)}, u32[]{:S(2)}) %all-to-all-start.2) | async-done | bytes 55328 | tf_op jit(solution)/shard_map/all_to_all | solution.py:289
  74.8 0.6 shard_map.96
  75.4 0.0 collective-permute-done.5.chip_ref
  75.4 0.0 collective-permute-done.6.other_ref
  75.4 1.5 %shard_map.94 = f32[6,3,4,1152]{3,2,1,0:T(4,128)} custom-call(f32[6,3,4,1152]{3,2,1,0:T(4,128)S(1)} %shard_map.91.q_ref, f32[6,3,4,1152]{3,2,1,0:T(4,128)S(1)} %collective-permute-done.5.chip_ref, f32[6,3,4,1152]{3,2,1,0:T(4,128)S(1)} %collective-permute-done.6.other_ref, f32[3,4,1152]{2,1,0:T(4,128)S(1)} %get-tuple-element.22.delta_ref, ...), custom_call_target="tpu_custom_call" | custom-call | flops 3317760 | bytes 1437696 | tf_op jit(solution)/shard_map/pallas_call | solution.py:254
Async XLA Ops:
  0.6 10.3 %copy-start.2 = (f32[6,3,4,1152]{3,2,1,0:T(4,128)S(1)}, f32[6,3,4,1152]{3,2,1,0:T(4,128)}, u32[]{:S(2)}) copy-start(f32[6,3,4,1152]{3,2,1,0:T(4,128)} %q_ref.5) | copy-start | bytes 995332
  0.6 10.3 %copy-start = (f32[2,3,4,1152]{3,2,1,0:T(4,128)S(1)}, f32[2,3,4,1152]{3,2,1,0:T(4,128)}, u32[]{:S(2)}) copy-start(f32[2,3,4,1152]{3,2,1,0:T(4,128)} %courant_ref.11) | copy-start | bytes 331780
  0.6 10.3 %copy-start.1 = (s32[2,3,4,1152]{3,2,1,0:T(4,128)S(1)}, s32[2,3,4,1152]{3,2,1,0:T(4,128)}, u32[]{:S(2)}) copy-start(s32[2,3,4,1152]{3,2,1,0:T(4,128)} %offsets_ref.11) | copy-start | bytes 331780
  1.8 19.6 %collective-permute-start = (f32[7,2,4,1152]{3,2,1,0:T(4,128)S(1)}, f32[7,2,4,1152]{3,2,1,0:T(4,128)S(1)}, u32[]{:S(2)}, u32[]{:S(2)}) collective-permute-start(f32[7,2,4,1152]{3,2,1,0:T(4,128)S(1)} %get-tuple-element.14), channel_id=1, source_target_pairs={{32,64},{64,32},{96,128},{128,96},{160,192},{192,160},{224,256},{2... | collective-permute-start | bytes 774152 | tf_op jit(solution)/shard_map/ppermute | solution.py:282
  9.0 12.4 %collective-permute-start.1 = (f32[7,2,4,1152]{3,2,1,0:T(4,128)S(1)}, f32[7,2,4,1152]{3,2,1,0:T(4,128)S(1)}, u32[]{:S(2)}, u32[]{:S(2)}) collective-permute-start(f32[7,2,4,1152]{3,2,1,0:T(4,128)S(1)} %get-tuple-element.15), channel_id=1, source_target_pairs={{0,32},{32,0},{64,96},{96,64},{128,160},{160,128},{192,224},{224,1... | collective-permute-start | bytes 774152 | tf_op jit(solution)/shard_map/ppermute | solution.py:283
  21.6 13.2 %collective-permute-start.4 = (f32[6,2,4,1152]{3,2,1,0:T(4,128)S(1)}, f32[6,2,4,1152]{3,2,1,0:T(4,128)S(1)}, u32[]{:S(2)}, u32[]{:S(2)}) collective-permute-start(f32[6,2,4,1152]{3,2,1,0:T(4,128)S(1)} %get-tuple-element.19), channel_id=1, source_target_pairs={{0,32},{32,0},{64,96},{96,64},{128,160},{160,128},{192,224},{224,1... | collective-permute-start | bytes 663560 | tf_op jit(solution)/shard_map/ppermute | solution.py:308
  23.6 11.2 %collective-permute-start.2 = (f32[3,2,4,1152]{3,2,1,0:T(4,128)S(1)}, f32[3,2,4,1152]{3,2,1,0:T(4,128)S(1)}, u32[]{:S(2)}, u32[]{:S(2)}) collective-permute-start(f32[3,2,4,1152]{3,2,1,0:T(4,128)S(1)} %get-tuple-element.17), channel_id=1, source_target_pairs={{32,64},{64,32},{96,128},{128,96},{160,192},{192,160},{224,256},{2... | collective-permute-start | bytes 331784 | tf_op jit(solution)/shard_map/ppermute | solution.py:307
  30.8 4.0 %copy-start.5 = (f32[3,4,1152]{2,1,0:T(4,128)S(1)}, f32[3,4,1152]{2,1,0:T(4,128)}, u32[]{:S(2)}) copy-start(f32[3,4,1152]{2,1,0:T(4,128)} %thickness_ref.1) | copy-start | bytes 165892
  30.8 4.0 %copy-start.6 = (f32[3,1152]{1,0:T(4,128)S(1)}, f32[3,1152]{1,0:T(4,128)}, u32[]{:S(2)}) copy-start(f32[3,1152]{1,0:T(4,128)} %surface_ref.1) | copy-start | bytes 41476
  35.5 14.1 %copy-start.3 = (s32[3,128,36]{1,2,0:T(8,128)S(1)}, s32[3,128,36]{1,2,0:T(8,128)}, u32[]{:S(2)}) copy-start(s32[3,128,36]{1,2,0:T(8,128)} %param.12) | copy-start | bytes 165892
  35.5 14.1 %copy-start.4 = (f32[3,128,36]{1,2,0:T(8,128)S(1)}, f32[3,128,36]{1,2,0:T(8,128)}, u32[]{:S(2)}) copy-start(f32[3,128,36]{1,2,0:T(8,128)} %param.13) | copy-start | bytes 165892
  35.5 16.1 %all-to-all-start.1 = ((f32[8,1,3456]{2,1,0:T(1,128)}), f32[8,1,3456]{2,1,0:T(1,128)S(1)}, u32[]{:S(2)}, u32[]{:S(2)}) async-start(f32[8,1,3456]{2,1,0:T(1,128)} %get-tuple-element.25), calls=%async_computation.1 | async-start | bytes 221184 | tf_op jit(solution)/shard_map/all_to_all | solution.py:289
  42.8 15.3 %collective-permute-start.3 = (f32[3,2,4,1152]{3,2,1,0:T(4,128)S(1)}, f32[3,2,4,1152]{3,2,1,0:T(4,128)S(1)}, u32[]{:S(2)}, u32[]{:S(2)}) collective-permute-start(f32[3,2,4,1152]{3,2,1,0:T(4,128)S(1)} %get-tuple-element.18), channel_id=1, source_target_pairs={{32,64},{64,32},{96,128},{128,96},{160,192},{192,160},{224,256},{2... | collective-permute-start | bytes 331784 | tf_op jit(solution)/shard_map/ppermute | solution.py:309
  51.6 15.8 %all-to-all-start = ((f32[32,4,256]{2,1,0:T(4,128)}), f32[32,4,256]{2,1,0:T(4,128)S(1)}, u32[]{:S(2)}, u32[]{:S(2)}) async-start(f32[32,4,256]{2,1,0:T(4,128)} %shard_map.92), calls=%async_computation | async-start | bytes 262144 | tf_op jit(solution)/shard_map/all_to_all | solution.py:299
  58.2 17.2 %collective-permute-start.5 = (f32[6,3,4,1152]{3,2,1,0:T(4,128)S(1)}, f32[6,3,4,1152]{3,2,1,0:T(4,128)S(1)}, u32[]{:S(2)}, u32[]{:S(2)}) collective-permute-start(f32[6,3,4,1152]{3,2,1,0:T(4,128)S(1)} %shard_map.91.q_ref), channel_id=1, source_target_pairs={{0,1},{1,0},{2,3},{3,2},{4,5},{5,4},{6,7},{7,6},{8,9},{9,8},{10,11... | collective-permute-start | bytes 995336 | tf_op jit(solution)/shard_map/ppermute | solution.py:322
  60.4 15.0 %collective-permute-start.6 = (f32[6,3,4,1152]{3,2,1,0:T(4,128)S(1)}, f32[6,3,4,1152]{3,2,1,0:T(4,128)S(1)}, u32[]{:S(2)}, u32[]{:S(2)}) collective-permute-start(f32[6,3,4,1152]{3,2,1,0:T(4,128)S(1)} %shard_map.91.q_ref), channel_id=1, source_target_pairs={{1,2},{2,1},{3,4},{4,3},{5,6},{6,5},{7,8},{8,7},{9,10},{10,9},{11,... | collective-permute-start | bytes 995336 | tf_op jit(solution)/shard_map/ppermute | solution.py:323
  67.5 7.3 %all-to-all-start.2 = ((f32[4,1,3456]{2,1,0:T(1,128)}), f32[4,1,3456]{2,1,0:T(1,128)S(1)}, u32[]{:S(2)}, u32[]{:S(2)}) async-start(f32[4,1,3456]{2,1,0:T(1,128)} %shard_map.95), calls=%async_computation.2 | async-start | bytes 110592 | tf_op jit(solution)/shard_map/all_to_all | solution.py:289
